TPU v7x, 256 devices: a whole 4x4x8 slice. The times are simulated.
256 devices in a mesh: slab: 4 (over z_lo, core), modes: 64 (over z_hi, y, x).
Axes of the slice: x: 4, y: 4, z: 8 (z_hi: 4, z_lo: 2; z = z_hi * 2 + z_lo), core: 2. Of those that a mesh axis runs over, the one named last changes fastest.
Arguments:
- occupation_prior: float32 [512, 32768], P('slab', 'modes'), may hold values from -6 to 6
- coupling: bfloat16 [256, 64, 128, 128], P('modes'), may hold values from -0.1875 to 0.1875
- pattern: int32 [256, 64], P('modes'), may hold values from 0 to 3
- pseudo_weights: float32 [32768], P('modes'), may hold values from -0.03125 to 0.03125
- equilibrium_slope: float32 [32768], replicated, may hold values from 0.3 to 3
- direction: int32 [256], P('modes'), may hold values from 0 to 1
- stream_rate: float32 [32768], P('modes'), may hold values from 0.15 to 0.95
- inscatter: float32 [256, 128, 128], P('modes'), may hold values from -0.125 to 0.125
- inflow_low: float32 [4, 32768], P(None, 'modes'), may hold values from -6 to 6
- inflow_high: float32 [4, 32768], P(None, 'modes'), may hold values from -6 to 6
- front_of_row: int32 [16], replicated, may hold values from 0 to 3
Outputs:
- swept: float32 [512, 32768], P('slab', 'modes')
Inputs may be any that keep to these rules, and one draw needn't show every extreme that they name: `pattern`: each entry names one of the 4 blocks of a group.
All inputs are finite; a program needn't handle non-finite values.
Results may differ from a plain program's by a relative error of at most 0.002.
Values sent between devices are 32-bit elements; how exact they have to be, the bound alone decides.
No kernel may reach another device: no remote copies, remote signals or barrier semaphores. Data moves between devices by JAX's collectives and lax.ppermute only.
A program may use at most 128 MiB of HBM per device.

v0:
```python
import functools

import jax
import jax.numpy as jnp
from jax import lax
from jax.experimental import pallas as pl
from jax.experimental.pallas import tpu as pltpu
from jax.sharding import PartitionSpec as P


BLK = 128
SHELL = 4
SIDE = 4
LAYERS = 8
LATERAL = 16
WIDTH = SHELL * BLK
CELL = LAYERS * LATERAL
HALF = CELL // 2


def route(axis, step):
    pairs = []
    for z in range(SIDE):
        for y in range(SIDE):
            for x in range(SIDE):
                there = [z, y, x]
                there[axis] = (there[axis] + step) % SIDE
                pairs.append(
                    ((z * SIDE + y) * SIDE + x, (there[0] * SIDE + there[1]) * SIDE + there[2])
                )
    return pairs


def send(block, axis, step):
    return lax.ppermute(block, "modes", route(axis, step))


def target(segment, place, i):
    _, _, z_step, upper, pair, step = segment
    along = pair + i
    y, x = (along, step) if upper else (step, along)
    z = ((place >> 4) + z_step) & 3
    return z * 16 + (((place >> 2) + y) & 3) * 4 + ((place + x) & 3)


def partial_kernel(jobs, addends, place_ref, pattern_ref, x_ref, weight_ref, *refs):
    segments = sum(len(job) for job in jobs)
    slopes, couplings = refs[:segments], refs[segments : 2 * segments]
    refs = refs[2 * segments :]
    added, outs = refs[:addends], refs[addends : addends + len(jobs)]
    rounded, warmth = refs[addends + len(jobs) :]
    step = pl.program_id(0)

    @pl.when(step == 0)
    def _():
        prior = x_ref[...]
        rounded[...] = prior.astype(jnp.bfloat16)
        total = jnp.sum(prior * weight_ref[...], axis=1, keepdims=True)
        warmth[...] = jnp.broadcast_to(total, warmth.shape)

    n = 0
    for index, job in enumerate(jobs):
        out_ref = outs[index]
        base = 0
        for segment in job:
            from_row, count = segment[:2]
            cells = pl.ds(from_row, count)
            rows = pl.ds(base, count)
            group = target(segment, place_ref[0], step)
            heat = warmth[cells, :]
            for t in range(SHELL):
                lanes = pl.ds(t * BLK, BLK)
                start = heat * slopes[n][0, :, lanes]
                if addends:
                    start += added[index][0, rows, lanes]
                out_ref[0, rows, lanes] = start
            for b in range(SHELL):
                product = jnp.dot(
                    rounded[cells, pl.ds(b * BLK, BLK)],
                    couplings[n][b, 0],
                    preferred_element_type=jnp.float32,
                )
                where = pattern_ref[b, group]
                lanes = pl.ds(pl.multiple_of(where * BLK, BLK), BLK)
                out_ref[0, rows, lanes] += product
            base += count
            n += 1


def partial_sums(jobs, units, addends, place, pattern, prior, weights, slope, coupling):
    segments = [segment for job in jobs for segment in job]
    slope_specs = [
        pl.BlockSpec(
            (1, 1, WIDTH), functools.partial(lambda n, i, m, p: (target(n, m[0], i), 0, 0), n)
        )
        for n in segments
    ]
    coupling_specs = [
        pl.BlockSpec(
            (SHELL, 1, BLK, BLK),
            functools.partial(lambda n, i, m, p: (0, target(n, m[0], i), 0, 0), n),
        )
        for n in segments
    ]
    heights = [sum(segment[1] for segment in job) for job in jobs]
    blocks = [pl.BlockSpec((1, rows, WIDTH), lambda i, g, p: (i, 0, 0)) for rows in heights]
    return pl.pallas_call(
        functools.partial(partial_kernel, jobs, len(addends)),
        grid_spec=pltpu.PrefetchScalarGridSpec(
            num_scalar_prefetch=2,
            grid=(units,),
            in_specs=[
                pl.BlockSpec((CELL, WIDTH), lambda i, g, p: (0, 0)),
                pl.BlockSpec((1, WIDTH), lambda i, g, p: (0, 0)),
            ]
            + slope_specs
            + coupling_specs
            + blocks[: len(addends)],
            out_specs=blocks,
            scratch_shapes=[
                pltpu.VMEM((CELL, WIDTH), jnp.bfloat16),
                pltpu.VMEM((CELL, BLK), jnp.float32),
            ],
        ),
        out_shape=[jax.ShapeDtypeStruct((units, rows, WIDTH), jnp.float32) for rows in heights],
        cost_estimate=pl.CostEstimate(
            flops=2 * sum(heights) * units * WIDTH * BLK,
            bytes_accessed=sum(heights) * units * WIDTH * 6,
            transcendentals=0,
        ),
        name="partial_sums",
    )(
        place,
        pattern,
        prior,
        weights,
        *([slope] * len(segments)),
        *([coupling] * len(segments)),
        *addends,
    )


def powers_kernel(rate_ref, inscatter_ref, high_ref, low_ref):
    row = lax.broadcasted_iota(jnp.int32, (BLK, BLK), 0)
    column = lax.broadcasted_iota(jnp.int32, (BLK, BLK), 1)
    unit = jnp.where(row == column, 1.0, 0.0).astype(jnp.float32)
    now = [unit + inscatter_ref[b] for b in range(SHELL)]
    for k in range(LAYERS):
        for b in range(SHELL):
            high = now[b].astype(jnp.bfloat16)
            high_ref[b, k] = high
            low_ref[b, k] = (now[b] - high.astype(jnp.float32)).astype(jnp.bfloat16)
            if k + 1 < LAYERS:
                now[b] = product(
                    now[b] * rate_ref[:, pl.ds(b * BLK, BLK)], high_ref[b, 0], low_ref[b, 0]
                )


def product(face, high, low):
    top = face.astype(jnp.bfloat16)
    rest = (face - top.astype(jnp.float32)).astype(jnp.bfloat16)
    rows = face.shape[0]
    both = jnp.dot(
        jnp.concatenate([top, rest], axis=0), high, preferred_element_type=jnp.float32
    )
    return both[:rows] + both[rows:] + jnp.dot(top, low, preferred_element_type=jnp.float32)


def last_kernel(direction_ref, *refs):
    halves, wholes, quarters = refs[:8], refs[8:10], refs[10:12]
    high_ref, low_ref, source_ref, out_ref = refs[12:]
    for side in range(2):
        rows = pl.ds(side * HALF, HALF)
        total = quarters[side][...]
        for part in halves[4 * side : 4 * side + 4]:
            total += part[...]
        for part in wholes:
            total += part[rows, :]
        source_ref[rows, :] = total
    for b in range(SHELL):
        lanes = pl.ds(b * BLK, BLK)
        up = direction_ref[b] == 1
        total = jnp.zeros((LATERAL, BLK), jnp.float32)
        for t in range(LAYERS):
            k = jnp.where(up, LAYERS - 1 - t, t)
            total += product(
                source_ref[pl.ds(t * LATERAL, LATERAL), lanes], high_ref[b, k], low_ref[b, k]
            )
        out_ref[:, lanes] = total


def particular_kernel(direction_ref, source_ref, rate_ref, high_ref, low_ref, out_ref):
    now = [jnp.zeros((LATERAL, BLK), jnp.float32) for _ in range(SHELL)]
    for t in range(LAYERS):
        for b in range(SHELL):
            lanes = pl.ds(b * BLK, BLK)
            at = jnp.where(direction_ref[b] == 1, t, LAYERS - 1 - t)
            rows = pl.ds(pl.multiple_of(at * LATERAL, LATERAL), LATERAL)
            now[b] = product(
                source_ref[rows, lanes] + rate_ref[:, lanes] * now[b], high_ref[b, 0], low_ref[b, 0]
            )
            out_ref[rows, lanes] = now[b]


def finish_kernel(
    direction_ref,
    slab_ref,
    wall_ref,
    one_ref,
    two_ref,
    three_ref,
    rate_ref,
    particular_ref,
    high_ref,
    low_ref,
    out_ref,
    faces,
):
    for k, face in enumerate((one_ref, two_ref, three_ref)):
        faces[k] = face[...]
    slab = slab_ref[0]
    now = [wall_ref[:, pl.ds(b * BLK, BLK)] for b in range(SHELL)]
    for n in range(3):
        for b in range(SHELL):
            lanes = pl.ds(b * BLK, BLK)
            up = direction_ref[b] == 1
            k = jnp.where(up, 2 - n, n)
            active = jnp.where(
                up, (k + 1 <= slab).astype(jnp.int32), (k + 1 > slab).astype(jnp.int32)
            )
            moved = faces[k, :, lanes] + product(
                now[b] * rate_ref[:, lanes], high_ref[b, LAYERS - 1], low_ref[b, LAYERS - 1]
            )
            now[b] = jnp.where(active == 1, moved, now[b])
    for b in range(SHELL):
        lanes = pl.ds(b * BLK, BLK)
        up = direction_ref[b] == 1
        scaled = now[b] * rate_ref[:, lanes]
        for t in range(LAYERS):
            k = jnp.where(up, t, LAYERS - 1 - t)
            rows = pl.ds(t * LATERAL, LATERAL)
            out_ref[rows, lanes] = particular_ref[rows, lanes] + product(
                scaled, high_ref[b, k], low_ref[b, k]
            )


SMEM = pl.BlockSpec(memory_space=pltpu.SMEM)
VMEM = pl.BlockSpec(memory_space=pltpu.VMEM)


def small_call(kernel, outs, specs, scratch=(), flops=0):
    return pl.pallas_call(
        kernel,
        in_specs=specs,
        out_specs=[VMEM] * len(outs),
        out_shape=[jax.ShapeDtypeStruct(*out) for out in outs],
        scratch_shapes=list(scratch),
        cost_estimate=pl.CostEstimate(flops=flops, bytes_accessed=3 << 20, transcendentals=0),
    )


def per_device(
    occupation_prior,
    coupling,
    pattern,
    pseudo_weights,
    equilibrium_slope,
    direction,
    stream_rate,
    inscatter,
    inflow_low,
    inflow_high,
    front_of_row,
):
    modes = lax.axis_index("modes").astype(jnp.int32)
    slab = lax.axis_index("slab").astype(jnp.int32)
    weights = pseudo_weights.reshape(1, WIDTH)
    rate = stream_rate.reshape(1, WIDTH)
    slope = equilibrium_slope.reshape(SIDE**3, 1, WIDTH)
    make = functools.partial(
        partial_sums,
        place=modes.reshape(1),
        pattern=pattern,
        weights=weights,
        slope=slope,
        coupling=coupling,
    )

    def ring_sums(low_step, high_step, prior, addends=()):
        jobs = [
            (
                (0, CELL, 1 if upper else 3, upper, pair, step),
                (0 if upper else HALF, HALF, 2, upper, pair, step),
            )
            for upper in (True, False)
            for pair, step in ((0, low_step), (2, high_step))
        ]
        return make(tuple(jobs), 2, addends, prior=prior)

    def ring(blocks, step):
        axes = (2, 2, 1, 1)
        signs = (step, -step, step, -step)
        moved = []
        for index, block in enumerate(blocks):
            moved.append(send(block, axes[index], signs[index]))
        return moved

    def spread(blocks, axis):
        return [send(block, axis, step) for block, step in zip(blocks, (1, 2, -1))]

    prior = occupation_prior
    split = [((SHELL, LAYERS, BLK, BLK), jnp.bfloat16)] * 2
    high, low = small_call(powers_kernel, split, [VMEM, VMEM], flops=200_000_000)(rate, inscatter)
    picks = front_of_row[:, None] == jnp.arange(inflow_low.shape[0], dtype=jnp.int32)[None, :]
    ahead = (jnp.repeat(direction, BLK) == 1)[None, :]
    inflow = jnp.where(ahead, inflow_low, inflow_high)
    wall = jnp.sum(jnp.where(picks[:, :, None], inflow[None, :, :], 0.0), axis=1)

    far_got = ring(ring_sums(2, 2, prior), 1)
    direct = ring_sums(3, 1, prior)
    early = ring(direct, -1)
    after, _ = lax.optimization_barrier((prior, direct))
    near = make(
        tuple(
            ((0 if upper else HALF, HALF, 0, upper, 0, step),)
            for upper in (True, False)
            for step in range(SIDE)
        ),
        SIDE,
        (),
        prior=after,
    )
    far_got, near = lax.optimization_barrier((far_got, near))
    late = ring(ring_sums(1, 3, prior, far_got), 1)
    early, high, low, wall = lax.optimization_barrier((early, high, low, wall))
    kept = ring_sums(0, 0, prior, early)
    a1, a3, a2 = kept[0][1] + late[0][1], kept[1][1] + late[1][1], kept[1][0] + late[1][0]
    b1, b3, b2 = kept[2][1] + late[2][1], kept[3][1] + late[3][1], kept[3][0] + late[3][0]
    near, _ = lax.optimization_barrier((near, (a1, a2, a3, b1, b2, b3)))
    a_got = spread((a1, a2, a3), 1)
    b_got = spread((b1, b2, b3), 2)
    near_a = spread(near[1:4], 2)
    near_b = spread(near[5:8], 1)
    a_own, b_own, a_got, b_got = lax.optimization_barrier(
        ((kept[0], late[0]), (kept[2], late[2]), a_got, b_got)
    )
    a_sum = a_own[0][0] + a_own[1][0] + a_got[0] + a_got[1] + a_got[2]
    b_sum = b_own[0][0] + b_own[1][0] + b_got[0] + b_got[1] + b_got[2]
    from_below = send(a_sum[:CELL], 0, 1)
    far_a = send(a_sum[CELL:], 0, 2)
    from_above = send(b_sum[:CELL], 0, -1)
    far_b = send(b_sum[CELL:], 0, 2)

    def ends(own, got, axis):
        parts = [own[i] + got[0][i] + got[1][i] + got[2][i] for i in range(SIDE)]
        return [parts[0]] + spread(parts[1:], axis)

    halves = ends(near[0], near_a, 1) + ends(near[4], near_b, 2)

    whole = ((CELL, WIDTH), jnp.float32)
    source, last = small_call(
        last_kernel,
        [whole, ((LATERAL, WIDTH), jnp.float32)],
        [SMEM] + [VMEM] * 14,
        flops=40_000_000,
    )(direction, *halves, from_below, from_above, far_a, far_b, high, low)
    faces = [
        lax.ppermute(last, "slab", [(i, (i + k) % 4) for i in range(4)]) for k in (1, 2, 3)
    ]
    (particular,) = small_call(
        particular_kernel, [whole], [SMEM] + [VMEM] * 4, flops=40_000_000
    )(direction, source, rate, high, low)
    (swept,) = small_call(
        finish_kernel,
        [whole],
        [SMEM, SMEM] + [VMEM] * 8,
        scratch=[pltpu.VMEM((3, LATERAL, WIDTH), jnp.float32)],
        flops=60_000_000,
    )(direction, slab.reshape(1), wall, *faces, rate, particular, high, low)
    return swept


def solution(mesh):
    placed = (
        P("slab", "modes"),
        P("modes", None, None, None),
        P("modes", None),
        P("modes"),
        P(),
        P("modes"),
        P("modes"),
        P("modes", None, None),
        P(None, "modes"),
        P(None, "modes"),
        P(),
    )

    return jax.shard_map(
        per_device, mesh=mesh, in_specs=placed, out_specs=P("slab", "modes"), check_vma=False
    )
```

profile of v0, /device:TPU:1, one launch (start us, length us, event | category | flops | bytes accessed | tf_op | source)
XLA Modules:
  0.0 177.8 jit_solution(11884067954378179838)
XLA Ops:
  0.0 5.1 %partial_sums.6 = (f32[2,192,512]{2,1,0:T(8,128)}, f32[2,192,512]{2,1,0:T(8,128)}, f32[2,192,512]{2,1,0:T(8,128)}, f32[2,192,512]{2,1,0:T(8,128)}) custom-call(s32[1]{0:T(128)} %bitcast.1.place_ref, s32[4,64]{1,0:T(4,128)} %pattern_ref.9, f32[128,512]{1,0:T(8,128)} %x_ref.8, f32[1,512]{1,0:T(1,128)} %bitcast.87, f32[64,1,512]{2,1,0:T(1,128)} %bitcast.47, ...), custom_call_target="tpu_custom_call" | custom-call | flops 201326592 | bytes 4718592 | tf_op jit(solution)/shard_map/partial_sums/pallas_call | solution.py:107
  5.1 2.1 %collective-permute-start.4 = (f32[2,192,512]{2,1,0:T(8,128)}, f32[2,192,512]{2,1,0:T(8,128)S(1)}, u32[]{:S(2)}, u32[]{:S(2)}) collective-permute-start(f32[2,192,512]{2,1,0:T(8,128)} %get-tuple-element.78), channel_id=1, source_target_pairs={{0,1},{1,2},{2,3},{3,0},{4,5},{5,6},{6,7},{7,4},{8,9},{9,10},{10,1... | collective-permute-start | bytes 2359304 | tf_op jit(solution)/shard_map/ppermute | solution.py:35
  7.2 1.4 collective-permute-start.5
  8.6 1.4 collective-permute-start.6
  10.0 1.4 collective-permute-start.7
  11.4 5.1 %partial_sums.5 = (f32[2,192,512]{2,1,0:T(8,128)}, f32[2,192,512]{2,1,0:T(8,128)}, f32[2,192,512]{2,1,0:T(8,128)}, f32[2,192,512]{2,1,0:T(8,128)}) custom-call(s32[1]{0:T(128)} %bitcast.1.place_ref, s32[4,64]{1,0:T(4,128)} %pattern_ref.9, f32[128,512]{1,0:T(8,128)} %x_ref.8, f32[1,512]{1,0:T(1,128)} %bitcast.88, f32[64,1,512]{2,1,0:T(1,128)} %bitcast.55, ...), custom_call_target="tpu_custom_call" | custom-call | flops 201326592 | bytes 4718592 | tf_op jit(solution)/shard_map/partial_sums/pallas_call | solution.py:107
  16.5 1.4 collective-permute-start
  17.8 6.0 %collective-permute-done.4.refs_16_ = f32[2,192,512]{2,1,0:T(8,128)S(1)} collective-permute-done((f32[2,192,512]{2,1,0:T(8,128)}, f32[2,192,512]{2,1,0:T(8,128)S(1)}, u32[]{:S(2)}, u32[]{:S(2)}) %collective-permute-start.4) | collective-permute-done | bytes 786464 | tf_op jit(solution)/shard_map/ppermute | solution.py:35
  23.9 1.9 %collective-permute-start.1 = (f32[2,192,512]{2,1,0:T(8,128)}, f32[2,192,512]{2,1,0:T(8,128)S(1)}, u32[]{:S(2)}, u32[]{:S(2)}) collective-permute-start(f32[2,192,512]{2,1,0:T(8,128)} %get-tuple-element.72), channel_id=1, source_target_pairs={{0,1},{1,2},{2,3},{3,0},{4,5},{5,6},{6,7},{7,4},{8,9},{9,10},{10,1... | collective-permute-start | bytes 2359304 | tf_op jit(solution)/shard_map/ppermute | solution.py:35
  25.7 3.6 %shard_map.109 = (bf16[4,8,128,128]{3,2,1,0:T(8,128)(2,1)}, bf16[4,8,128,128]{3,2,1,0:T(8,128)(2,1)}) custom-call(f32[1,512]{1,0:T(1,128)} %bitcast.92, f32[4,128,128]{2,1,0:T(8,128)} %inscatter_ref.1), custom_call_target="tpu_custom_call" | custom-call | flops 200000000 | bytes 3145728 | tf_op jit(solution)/shard_map/pallas_call | solution.py:313
  29.4 7.1 %partial_sums.7 = (f32[4,64,512]{2,1,0:T(8,128)}, f32[4,64,512]{2,1,0:T(8,128)}, f32[4,64,512]{2,1,0:T(8,128)}, f32[4,64,512]{2,1,0:T(8,128)}, f32[4,64,512]{2,1...) custom-call(s32[1]{0:T(128)} %bitcast.1.place_ref, s32[4,64]{1,0:T(4,128)} %pattern_ref.9, ...), custom_call_target="tpu_custom_call" | custom-call | flops 268435456 | bytes 6291456 | tf_op jit(solution)/shard_map/partial_sums/pallas_call | solution.py:107
  36.5 3.2 %collective-permute-start.2 = (f32[2,192,512]{2,1,0:T(8,128)}, f32[2,192,512]{2,1,0:T(8,128)S(1)}, u32[]{:S(2)}, u32[]{:S(2)}) collective-permute-start(f32[2,192,512]{2,1,0:T(8,128)} %get-tuple-element.73), channel_id=1, source_target_pairs={{0,12},{1,13},{2,14},{3,15},{4,0},{5,1},{6,2},{7,3},{8,4},{9,5},{1... | collective-permute-start | bytes 2359304 | tf_op jit(solution)/shard_map/ppermute | solution.py:35
  39.8 5.8 %partial_sums.9 = (f32[2,192,512]{2,1,0:T(8,128)}, f32[2,192,512]{2,1,0:T(8,128)}, f32[2,192,512]{2,1,0:T(8,128)}, f32[2,192,512]{2,1,0:T(8,128)}) custom-call(s32[1]{0:T(128)} %bitcast.1.place_ref, s32[4,64]{1,0:T(4,128)} %pattern_ref.9, f32[128,512]{1,0:T(8,128)} %x_ref.8, f32[1,512]{1,0:T(1,128)} %bitcast.90, f32[64,1,512]{2,1,0:T(1,128)} %bitcast.71, ...), custom_call_target="tpu_custom_call" | custom-call | flops 201326592 | bytes 4718592 | tf_op jit(solution)/shard_map/partial_sums/pallas_call | solution.py:107
  46.7 1.9 %collective-permute-start.9 = (f32[2,192,512]{2,1,0:T(8,128)}, f32[2,192,512]{2,1,0:T(8,128)}, u32[]{:S(2)}, u32[]{:S(2)}) collective-permute-start(f32[2,192,512]{2,1,0:T(8,128)} %get-tuple-element.110), channel_id=1, source_target_pairs={{0,3},{1,0},{2,1},{3,2},{4,7},{5,4},{6,5},{7,6},{8,11},{9,8},{10,9... | collective-permute-start | bytes 2359304 | tf_op jit(solution)/shard_map/ppermute | solution.py:35
  49.6 5.9 %collective-permute-done.2.refs_18_ = f32[2,192,512]{2,1,0:T(8,128)S(1)} collective-permute-done((f32[2,192,512]{2,1,0:T(8,128)}, f32[2,192,512]{2,1,0:T(8,128)S(1)}, u32[]{:S(2)}, u32[]{:S(2)}) %collective-permute-start.2) | collective-permute-done | bytes 786464 | tf_op jit(solution)/shard_map/ppermute | solution.py:35
  55.5 3.1 %collective-permute-done.3.refs_19_ = f32[2,192,512]{2,1,0:T(8,128)S(1)} collective-permute-done((f32[2,192,512]{2,1,0:T(8,128)}, f32[2,192,512]{2,1,0:T(8,128)S(1)}, u32[]{:S(2)}, u32[]{:S(2)}) %collective-permute-start.3) | collective-permute-done | bytes 786464 | tf_op jit(solution)/shard_map/ppermute | solution.py:35
  59.5 5.8 %partial_sums.8 = (f32[2,192,512]{2,1,0:T(8,128)}, f32[2,192,512]{2,1,0:T(8,128)}, f32[2,192,512]{2,1,0:T(8,128)}, f32[2,192,512]{2,1,0:T(8,128)}) custom-call(s32[1]{0:T(128)} %bitcast.1.place_ref, s32[4,64]{1,0:T(4,128)} %pattern_ref.9, f32[128,512]{1,0:T(8,128)} %x_ref.8, f32[1,512]{1,0:T(1,128)} %bitcast.91, f32[64,1,512]{2,1,0:T(1,128)} %bitcast.79, ...), custom_call_target="tpu_custom_call" | custom-call | flops 201326592 | bytes 4718592 | tf_op jit(solution)/shard_map/partial_sums/pallas_call | solution.py:107
  65.3 1.3 fusion.5
  67.4 1.5 fusion.3
  68.9 2.1 %collective-permute-start.26 = (f32[192,512]{1,0:T(8,128)S(1)}, f32[192,512]{1,0:T(8,128)S(1)}, u32[]{:S(2)}, u32[]{:S(2)}) collective-permute-start(f32[192,512]{1,0:T(8,128)S(1)} %get-tuple-element.147), channel_id=1, source_target_pairs={{0,12},{1,13},{2,14},{3,15},{4,0},{5,1},{6,2},{7,3},{8,4},{9,5},{1... | collective-permute-start | bytes 1179656 | tf_op jit(solution)/shard_map/ppermute | solution.py:35
  71.1 4.3 %collective-permute-done.10 = f32[2,192,512]{2,1,0:T(8,128)} collective-permute-done((f32[2,192,512]{2,1,0:T(8,128)}, f32[2,192,512]{2,1,0:T(8,128)}, u32[]{:S(2)}, u32[]{:S(2)}) %collective-permute-start.10) | collective-permute-done | bytes 786464 | tf_op jit(solution)/shard_map/ppermute | solution.py:35
  75.5 1.2 fusion.2
  77.5 1.5 fusion
  79.0 2.0 %collective-permute-start.29 = (f32[192,512]{1,0:T(8,128)S(1)}, f32[192,512]{1,0:T(8,128)S(1)}, u32[]{:S(2)}, u32[]{:S(2)}) collective-permute-start(f32[192,512]{1,0:T(8,128)S(1)} %get-tuple-element.145), channel_id=1, source_target_pairs={{0,3},{1,0},{2,1},{3,2},{4,7},{5,4},{6,5},{7,6},{8,11},{9,8},{10,9... | collective-permute-start | bytes 1179656 | tf_op jit(solution)/shard_map/ppermute | solution.py:35
  81.0 4.0 %collective-permute-done.24 = f32[192,512]{1,0:T(8,128)S(1)} collective-permute-done((f32[192,512]{1,0:T(8,128)S(1)}, f32[192,512]{1,0:T(8,128)S(1)}, u32[]{:S(2)}, u32[]{:S(2)}) %collective-permute-start.24) | collective-permute-done | bytes 393248 | tf_op jit(solution)/shard_map/ppermute | solution.py:35
  84.9 1.9 %collective-permute-start.28 = (f32[192,512]{1,0:T(8,128)S(1)}, f32[192,512]{1,0:T(8,128)S(1)}, u32[]{:S(2)}, u32[]{:S(2)}) collective-permute-start(f32[192,512]{1,0:T(8,128)S(1)} %get-tuple-element.146), channel_id=1, source_target_pairs={{0,2},{1,3},{2,0},{3,1},{4,6},{5,7},{6,4},{7,5},{8,10},{9,11},{10,... | collective-permute-start | bytes 1179656 | tf_op jit(solution)/shard_map/ppermute | solution.py:35
  87.8 3.3 %collective-permute-done.25 = f32[192,512]{1,0:T(8,128)S(1)} collective-permute-done((f32[192,512]{1,0:T(8,128)S(1)}, f32[192,512]{1,0:T(8,128)S(1)}, u32[]{:S(2)}, u32[]{:S(2)}) %collective-permute-start.25) | collective-permute-done | bytes 393248 | tf_op jit(solution)/shard_map/ppermute | solution.py:35
  91.1 2.1 %collective-permute-start.13 = (f32[4,64,512]{2,1,0:T(8,128)}, f32[4,64,512]{2,1,0:T(8,128)S(1)}, u32[]{:S(2)}, u32[]{:S(2)}) collective-permute-start(f32[4,64,512]{2,1,0:T(8,128)} %get-tuple-element.117), channel_id=1, source_target_pairs={{0,2},{1,3},{2,0},{3,1},{4,6},{5,7},{6,4},{7,5},{8,10},{9,11},{10,... | collective-permute-start | bytes 1572872 | tf_op jit(solution)/shard_map/ppermute | solution.py:35
  93.2 1.2 collective-permute-start.14
  96.1 1.3 fusion.9
  97.4 3.0 %collective-permute-done.12 = f32[4,64,512]{2,1,0:T(8,128)S(1)} collective-permute-done((f32[4,64,512]{2,1,0:T(8,128)}, f32[4,64,512]{2,1,0:T(8,128)S(1)}, u32[]{:S(2)}, u32[]{:S(2)}) %collective-permute-start.12) | collective-permute-done | bytes 524320 | tf_op jit(solution)/shard_map/ppermute | solution.py:35
  100.5 1.2 fusion.7
  101.7 12.1 %collective-permute-done.13 = f32[4,64,512]{2,1,0:T(8,128)S(1)} collective-permute-done((f32[4,64,512]{2,1,0:T(8,128)}, f32[4,64,512]{2,1,0:T(8,128)S(1)}, u32[]{:S(2)}, u32[]{:S(2)}) %collective-permute-start.13) | collective-permute-done | bytes 524320 | tf_op jit(solution)/shard_map/ppermute | solution.py:35
  113.8 3.0 %collective-permute-start.30 = (f32[128,512]{1,0:T(8,128)S(1)}, f32[128,512]{1,0:T(8,128)S(1)}, u32[]{:S(2)}, u32[]{:S(2)}) collective-permute-start(f32[128,512]{1,0:T(8,128)S(1)} %slice.238), channel_id=1, source_target_pairs={{0,16},{1,17},{2,18},{3,19},{4,20},{5,21},{6,22},{7,23},{8,24},{9,... | collective-permute-start | bytes 786440 | tf_op jit(solution)/shard_map/ppermute | solution.py:35
  116.9 5.7 %collective-permute-done.14 = f32[4,64,512]{2,1,0:T(8,128)S(1)} collective-permute-done((f32[4,64,512]{2,1,0:T(8,128)}, f32[4,64,512]{2,1,0:T(8,128)S(1)}, u32[]{:S(2)}, u32[]{:S(2)}) %collective-permute-start.14) | collective-permute-done | bytes 524320 | tf_op jit(solution)/shard_map/ppermute | solution.py:35
  122.6 6.0 %collective-permute-start.31 = (f32[128,512]{1,0:T(8,128)S(1)}, f32[128,512]{1,0:T(8,128)S(1)}, u32[]{:S(2)}, u32[]{:S(2)}) collective-permute-start(f32[128,512]{1,0:T(8,128)S(1)} %slice.239), channel_id=1, source_target_pairs={{0,48},{1,49},{2,50},{3,51},{4,52},{5,53},{6,54},{7,55},{8,56},{9,... | collective-permute-start | bytes 786440 | tf_op jit(solution)/shard_map/ppermute | solution.py:35
  130.3 4.5 %collective-permute-start.33 = (f32[64,512]{1,0:T(8,128)S(1)}, f32[64,512]{1,0:T(8,128)S(1)}, u32[]{:S(2)}, u32[]{:S(2)}) collective-permute-start(f32[64,512]{1,0:T(8,128)S(1)} %slice.241), channel_id=1, source_target_pairs={{0,32},{1,33},{2,34},{3,35},{4,36},{5,37},{6,38},{7,39},{8,40},{9,... | collective-permute-start | bytes 393224 | tf_op jit(solution)/shard_map/ppermute | solution.py:35
  135.7 5.4 %collective-permute-done.32.refs_10_ = f32[64,512]{1,0:T(8,128)S(1)} collective-permute-done((f32[64,512]{1,0:T(8,128)S(1)}, f32[64,512]{1,0:T(8,128)S(1)}, u32[]{:S(2)}, u32[]{:S(2)}) %collective-permute-start.32) | collective-permute-done | bytes 131104 | tf_op jit(solution)/shard_map/ppermute | solution.py:35
  141.1 3.8 %collective-permute-done.33.refs_11_ = f32[64,512]{1,0:T(8,128)S(1)} collective-permute-done((f32[64,512]{1,0:T(8,128)S(1)}, f32[64,512]{1,0:T(8,128)S(1)}, u32[]{:S(2)}, u32[]{:S(2)}) %collective-permute-start.33) | collective-permute-done | bytes 131104 | tf_op jit(solution)/shard_map/ppermute | solution.py:35
  144.9 3.1 %collective-permute-start.23 = (f32[64,512]{1,0:T(8,128)S(1)}, f32[64,512]{1,0:T(8,128)S(1)}, u32[]{:S(2)}, u32[]{:S(2)}) collective-permute-start(f32[64,512]{1,0:T(8,128)S(1)} %get-tuple-element.137), channel_id=1, source_target_pairs={{0,3},{1,0},{2,1},{3,2},{4,7},{5,4},{6,5},{7,6},{8,11},{9,8},{10,9... | collective-permute-start | bytes 393224 | tf_op jit(solution)/shard_map/ppermute | solution.py:35
  148.7 3.1 %collective-permute-done.15.refs_1_ = f32[64,512]{1,0:T(8,128)S(1)} collective-permute-done((f32[64,512]{1,0:T(8,128)S(1)}, f32[64,512]{1,0:T(8,128)S(1)}, u32[]{:S(2)}, u32[]{:S(2)}) %collective-permute-start.15) | collective-permute-done | bytes 131104 | tf_op jit(solution)/shard_map/ppermute | solution.py:35
  151.8 1.6 collective-permute-done.22.refs_6_
  153.4 1.1 collective-permute-done.21.refs_5_
  155.1 3.5 %shard_map.110 = (f32[128,512]{1,0:T(8,128)}, f32[16,512]{1,0:T(8,128)}) custom-call(s32[4]{0:T(128)} %direction_ref.5, f32[64,512]{1,0:T(8,128)} %get-tuple-element.144.refs_0_, f32[64,512]{1,0:T(8,128)} %copy-done.14, f32[64,512]{1,0:T(8,128)} %copy-done.13, f32[64,512]{1,0:T(8,128)} %copy-done.12, f32[64,512]{1,0:T(8,128)} %get-tuple-element.140.refs_4_, ...), custom_call_target="tpu_custom_call" | custom-call | flops 40000000 | bytes 3145728 | tf_op jit(solution)/shard_map/pallas_call | solution.py:361
  158.6 5.3 %collective-permute-start.36 = (f32[16,512]{1,0:T(8,128)}, f32[16,512]{1,0:T(8,128)S(1)}, u32[]{:S(2)}, u32[]{:S(2)}) collective-permute-start(f32[16,512]{1,0:T(8,128)} %get-tuple-element.135), channel_id=1, source_target_pairs={{0,192},{64,0},{128,64},{192,128},{1,193},{65,1},{129,65},{193,129... | collective-permute-start | bytes 98312 | tf_op jit(solution)/shard_map/ppermute | solution.py:368
  164.0 6.3 %collective-permute-start.35 = (f32[16,512]{1,0:T(8,128)}, f32[16,512]{1,0:T(8,128)S(1)}, u32[]{:S(2)}, u32[]{:S(2)}) collective-permute-start(f32[16,512]{1,0:T(8,128)} %get-tuple-element.135), channel_id=1, source_target_pairs={{0,128},{64,192},{128,0},{192,64},{1,129},{65,193},{129,1},{193,65... | collective-permute-start | bytes 98312 | tf_op jit(solution)/shard_map/ppermute | solution.py:368
  170.4 3.4 %shard_map.111.particular_ref = f32[128,512]{1,0:T(8,128)} custom-call(s32[4]{0:T(128)} %direction_ref.5, f32[128,512]{1,0:T(8,128)} %get-tuple-element.136.source_ref, f32[1,512]{1,0:T(1,128)} %bitcast.93, bf16[4,8,128,128]{3,2,1,0:T(8,128)(2,1)} %get-tuple-element.133.refs_12_.high_ref, bf16[4,8,128,128]{3,2,1,0:T(8,128)(2,1)} %get-tuple-element.134.refs_13_.low_ref), custom_call_target="tpu_custom_call" | custom-call | flops 40000000 | bytes 3145728 | tf_op jit(solution)/shard_map/pallas_call | solution.py:370
  174.4 3.5 %shard_map.112 = f32[128,512]{1,0:T(8,128)} custom-call(s32[4]{0:T(128)} %direction_ref.5, s32[1]{0:T(128)} %bitcast.slab_ref, f32[16,512]{1,0:T(8,128)} %select_reduce_fusion.wall_ref, f32[16,512]{1,0:T(8,128)} %copy-done.20, f32[16,512]{1,0:T(8,128)} %copy-done.19, f32[16,512]{1,0:T(8,128)} %copy-done.18, f32[1,512]{1,0:T(1,128)} %bitcast.94, ...), custom_call_target="tpu_custom_call" | custom-call | flops 60000000 | bytes 3145728 | tf_op jit(solution)/shard_map/pallas_call | solution.py:373
  (104 shorter events, 12.1 us)
Async XLA Ops:
  5.1 18.8 %collective-permute-start.4 = (f32[2,192,512]{2,1,0:T(8,128)}, f32[2,192,512]{2,1,0:T(8,128)S(1)}, u32[]{:S(2)}, u32[]{:S(2)}) collective-permute-start(f32[2,192,512]{2,1,0:T(8,128)} %get-tuple-element.78), channel_id=1, source_target_pairs={{0,1},{1,2},{2,3},{3,0},{4,5},{5,6},{6,7},{7,4},{8,9},{9,10},{10,1... | collective-permute-start | bytes 2359304 | tf_op jit(solution)/shard_map/ppermute | solution.py:35
  7.2 29.3 %collective-permute-start.5 = (f32[2,192,512]{2,1,0:T(8,128)}, f32[2,192,512]{2,1,0:T(8,128)}, u32[]{:S(2)}, u32[]{:S(2)}) collective-permute-start(f32[2,192,512]{2,1,0:T(8,128)} %get-tuple-element.79), channel_id=1, source_target_pairs={{0,3},{1,0},{2,1},{3,2},{4,7},{5,4},{6,5},{7,6},{8,11},{9,8},{10,9... | collective-permute-start | bytes 2359304 | tf_op jit(solution)/shard_map/ppermute | solution.py:35
  8.6 31.2 %collective-permute-start.6 = (f32[2,192,512]{2,1,0:T(8,128)}, f32[2,192,512]{2,1,0:T(8,128)}, u32[]{:S(2)}, u32[]{:S(2)}) collective-permute-start(f32[2,192,512]{2,1,0:T(8,128)} %get-tuple-element.80), channel_id=1, source_target_pairs={{0,4},{1,5},{2,6},{3,7},{4,8},{5,9},{6,10},{7,11},{8,12},{9,13},{1... | collective-permute-start | bytes 2359304 | tf_op jit(solution)/shard_map/ppermute | solution.py:35
  10.0 29.8 %collective-permute-start.7 = (f32[2,192,512]{2,1,0:T(8,128)}, f32[2,192,512]{2,1,0:T(8,128)}, u32[]{:S(2)}, u32[]{:S(2)}) collective-permute-start(f32[2,192,512]{2,1,0:T(8,128)} %get-tuple-element.81), channel_id=1, source_target_pairs={{0,12},{1,13},{2,14},{3,15},{4,0},{5,1},{6,2},{7,3},{8,4},{9,5},{1... | collective-permute-start | bytes 2359304 | tf_op jit(solution)/shard_map/ppermute | solution.py:35
  16.5 30.2 %collective-permute-start = (f32[2,192,512]{2,1,0:T(8,128)}, f32[2,192,512]{2,1,0:T(8,128)S(1)}, u32[]{:S(2)}, u32[]{:S(2)}) collective-permute-start(f32[2,192,512]{2,1,0:T(8,128)} %get-tuple-element.71), channel_id=1, source_target_pairs={{0,3},{1,0},{2,1},{3,2},{4,7},{5,4},{6,5},{7,6},{8,11},{9,8},{10,9... | collective-permute-start | bytes 2359304 | tf_op jit(solution)/shard_map/ppermute | solution.py:35
  23.9 12.6 %copy-start.3 = (f32[2,192,512]{2,1,0:T(8,128)}, f32[2,192,512]{2,1,0:T(8,128)S(1)}, u32[]{:S(2)}) copy-start(f32[2,192,512]{2,1,0:T(8,128)S(1)} %collective-permute-done.4.refs_16_) | copy-start | bytes 2359300
  23.9 24.8 %collective-permute-start.1 = (f32[2,192,512]{2,1,0:T(8,128)}, f32[2,192,512]{2,1,0:T(8,128)S(1)}, u32[]{:S(2)}, u32[]{:S(2)}) collective-permute-start(f32[2,192,512]{2,1,0:T(8,128)} %get-tuple-element.72), channel_id=1, source_target_pairs={{0,1},{1,2},{2,3},{3,0},{4,5},{5,6},{6,7},{7,4},{8,9},{9,10},{10,1... | collective-permute-start | bytes 2359304 | tf_op jit(solution)/shard_map/ppermute | solution.py:35
  36.5 19.0 %collective-permute-start.2 = (f32[2,192,512]{2,1,0:T(8,128)}, f32[2,192,512]{2,1,0:T(8,128)S(1)}, u32[]{:S(2)}, u32[]{:S(2)}) collective-permute-start(f32[2,192,512]{2,1,0:T(8,128)} %get-tuple-element.73), channel_id=1, source_target_pairs={{0,12},{1,13},{2,14},{3,15},{4,0},{5,1},{6,2},{7,3},{8,4},{9,5},{1... | collective-permute-start | bytes 2359304 | tf_op jit(solution)/shard_map/ppermute | solution.py:35
  39.8 18.9 %collective-permute-start.3 = (f32[2,192,512]{2,1,0:T(8,128)}, f32[2,192,512]{2,1,0:T(8,128)S(1)}, u32[]{:S(2)}, u32[]{:S(2)}) collective-permute-start(f32[2,192,512]{2,1,0:T(8,128)} %get-tuple-element.74), channel_id=1, source_target_pairs={{0,4},{1,5},{2,6},{3,7},{4,8},{5,9},{6,10},{7,11},{8,12},{9,13},{1... | collective-permute-start | bytes 2359304 | tf_op jit(solution)/shard_map/ppermute | solution.py:35
  39.8 9.0 %copy-start.25 = (s32[16]{0:T(128)S(1)}, s32[16]{0:T(128)}, u32[]{:S(2)}) copy-start(s32[16]{0:T(128)} %param.21) | copy-start | bytes 196
  45.6 19.7 %collective-permute-start.8 = (f32[2,192,512]{2,1,0:T(8,128)}, f32[2,192,512]{2,1,0:T(8,128)}, u32[]{:S(2)}, u32[]{:S(2)}) collective-permute-start(f32[2,192,512]{2,1,0:T(8,128)} %get-tuple-element.108), channel_id=1, source_target_pairs={{0,1},{1,2},{2,3},{3,0},{4,5},{5,6},{6,7},{7,4},{8,9},{9,10},{10,1... | collective-permute-start | bytes 2359304 | tf_op jit(solution)/shard_map/ppermute | solution.py:35
  46.7 12.3 %copy-start = (f32[2,192,512]{2,1,0:T(8,128)}, f32[2,192,512]{2,1,0:T(8,128)S(1)}, u32[]{:S(2)}) copy-start(f32[2,192,512]{2,1,0:T(8,128)S(1)} %collective-permute-done.refs_16_) | copy-start | bytes 2359300
  46.7 20.6 %collective-permute-start.9 = (f32[2,192,512]{2,1,0:T(8,128)}, f32[2,192,512]{2,1,0:T(8,128)}, u32[]{:S(2)}, u32[]{:S(2)}) collective-permute-start(f32[2,192,512]{2,1,0:T(8,128)} %get-tuple-element.110), channel_id=1, source_target_pairs={{0,3},{1,0},{2,1},{3,2},{4,7},{5,4},{6,5},{7,6},{8,11},{9,8},{10,9... | collective-permute-start | bytes 2359304 | tf_op jit(solution)/shard_map/ppermute | solution.py:35
  48.7 10.3 %copy-start.1 = (f32[2,192,512]{2,1,0:T(8,128)}, f32[2,192,512]{2,1,0:T(8,128)S(1)}, u32[]{:S(2)}) copy-start(f32[2,192,512]{2,1,0:T(8,128)S(1)} %collective-permute-done.1.refs_17_) | copy-start | bytes 2359300
  48.7 26.8 %collective-permute-start.10 = (f32[2,192,512]{2,1,0:T(8,128)}, f32[2,192,512]{2,1,0:T(8,128)}, u32[]{:S(2)}, u32[]{:S(2)}) collective-permute-start(f32[2,192,512]{2,1,0:T(8,128)} %get-tuple-element.112), channel_id=1, source_target_pairs={{0,4},{1,5},{2,6},{3,7},{4,8},{5,9},{6,10},{7,11},{8,12},{9,13},{1... | collective-permute-start | bytes 2359304 | tf_op jit(solution)/shard_map/ppermute | solution.py:35
  58.6 18.9 %collective-permute-start.11 = (f32[2,192,512]{2,1,0:T(8,128)}, f32[2,192,512]{2,1,0:T(8,128)}, u32[]{:S(2)}, u32[]{:S(2)}) collective-permute-start(f32[2,192,512]{2,1,0:T(8,128)} %get-tuple-element.114), channel_id=1, source_target_pairs={{0,12},{1,13},{2,14},{3,15},{4,0},{5,1},{6,2},{7,3},{8,4},{9,5},{1... | collective-permute-start | bytes 2359304 | tf_op jit(solution)/shard_map/ppermute | solution.py:35
  65.3 35.2 %copy-start.24 = (f32[4,64,512]{2,1,0:T(8,128)S(1)}, f32[4,64,512]{2,1,0:T(8,128)}, u32[]{:S(2)}) copy-start(f32[4,64,512]{2,1,0:T(8,128)} %get-tuple-element.122) | copy-start | bytes 1572868
  65.3 35.2 %copy-start.5 = (f32[2,192,512]{2,1,0:T(8,128)S(1)}, f32[2,192,512]{2,1,0:T(8,128)}, u32[]{:S(2)}) copy-start(f32[2,192,512]{2,1,0:T(8,128)} %get-tuple-element.128) | copy-start | bytes 2359300
  65.3 63.2 %copy-start.7 = (f32[4,64,512]{2,1,0:T(8,128)S(1)}, f32[4,64,512]{2,1,0:T(8,128)}, u32[]{:S(2)}) copy-start(f32[4,64,512]{2,1,0:T(8,128)} %get-tuple-element.115) | copy-start | bytes 1572868
  65.3 69.5 %copy-start.6 = (f32[4,64,512]{2,1,0:T(8,128)S(1)}, f32[4,64,512]{2,1,0:T(8,128)}, u32[]{:S(2)}) copy-start(f32[4,64,512]{2,1,0:T(8,128)} %get-tuple-element.119) | copy-start | bytes 1572868
  66.7 18.3 %collective-permute-start.24 = (f32[192,512]{1,0:T(8,128)S(1)}, f32[192,512]{1,0:T(8,128)S(1)}, u32[]{:S(2)}, u32[]{:S(2)}) collective-permute-start(f32[192,512]{1,0:T(8,128)S(1)} %fusion.5), channel_id=1, source_target_pairs={{0,4},{1,5},{2,6},{3,7},{4,8},{5,9},{6,10},{7,11},{8,12},{9,13},{1... | collective-permute-start | bytes 1179656 | tf_op jit(solution)/shard_map/ppermute | solution.py:35
  68.9 18.0 %collective-permute-start.26 = (f32[192,512]{1,0:T(8,128)S(1)}, f32[192,512]{1,0:T(8,128)S(1)}, u32[]{:S(2)}, u32[]{:S(2)}) collective-permute-start(f32[192,512]{1,0:T(8,128)S(1)} %get-tuple-element.147), channel_id=1, source_target_pairs={{0,12},{1,13},{2,14},{3,15},{4,0},{5,1},{6,2},{7,3},{8,4},{9,5},{1... | collective-permute-start | bytes 1179656 | tf_op jit(solution)/shard_map/ppermute | solution.py:35
  71.0 20.1 %collective-permute-start.25 = (f32[192,512]{1,0:T(8,128)S(1)}, f32[192,512]{1,0:T(8,128)S(1)}, u32[]{:S(2)}, u32[]{:S(2)}) collective-permute-start(f32[192,512]{1,0:T(8,128)S(1)} %get-tuple-element.148), channel_id=1, source_target_pairs={{0,8},{1,9},{2,10},{3,11},{4,12},{5,13},{6,14},{7,15},{8,0},{9,1},... | collective-permute-start | bytes 1179656 | tf_op jit(solution)/shard_map/ppermute | solution.py:35
  76.7 16.6 %collective-permute-start.27 = (f32[192,512]{1,0:T(8,128)S(1)}, f32[192,512]{1,0:T(8,128)S(1)}, u32[]{:S(2)}, u32[]{:S(2)}) collective-permute-start(f32[192,512]{1,0:T(8,128)S(1)} %fusion.2), channel_id=1, source_target_pairs={{0,1},{1,2},{2,3},{3,0},{4,5},{5,6},{6,7},{7,4},{8,9},{9,10},{10,1... | collective-permute-start | bytes 1179656 | tf_op jit(solution)/shard_map/ppermute | solution.py:35
  79.0 15.4 %collective-permute-start.29 = (f32[192,512]{1,0:T(8,128)S(1)}, f32[192,512]{1,0:T(8,128)S(1)}, u32[]{:S(2)}, u32[]{:S(2)}) collective-permute-start(f32[192,512]{1,0:T(8,128)S(1)} %get-tuple-element.145), channel_id=1, source_target_pairs={{0,3},{1,0},{2,1},{3,2},{4,7},{5,4},{6,5},{7,6},{8,11},{9,8},{10,9... | collective-permute-start | bytes 1179656 | tf_op jit(solution)/shard_map/ppermute | solution.py:35
  84.9 10.4 %collective-permute-start.28 = (f32[192,512]{1,0:T(8,128)S(1)}, f32[192,512]{1,0:T(8,128)S(1)}, u32[]{:S(2)}, u32[]{:S(2)}) collective-permute-start(f32[192,512]{1,0:T(8,128)S(1)} %get-tuple-element.146), channel_id=1, source_target_pairs={{0,2},{1,3},{2,0},{3,1},{4,6},{5,7},{6,4},{7,5},{8,10},{9,11},{10,... | collective-permute-start | bytes 1179656 | tf_op jit(solution)/shard_map/ppermute | solution.py:35
  86.9 13.6 %collective-permute-start.12 = (f32[4,64,512]{2,1,0:T(8,128)}, f32[4,64,512]{2,1,0:T(8,128)S(1)}, u32[]{:S(2)}, u32[]{:S(2)}) collective-permute-start(f32[4,64,512]{2,1,0:T(8,128)} %get-tuple-element.116), channel_id=1, source_target_pairs={{0,1},{1,2},{2,3},{3,0},{4,5},{5,6},{6,7},{7,4},{8,9},{9,10},{10,1... | collective-permute-start | bytes 1572872 | tf_op jit(solution)/shard_map/ppermute | solution.py:35
  91.1 22.7 %collective-permute-start.13 = (f32[4,64,512]{2,1,0:T(8,128)}, f32[4,64,512]{2,1,0:T(8,128)S(1)}, u32[]{:S(2)}, u32[]{:S(2)}) collective-permute-start(f32[4,64,512]{2,1,0:T(8,128)} %get-tuple-element.117), channel_id=1, source_target_pairs={{0,2},{1,3},{2,0},{3,1},{4,6},{5,7},{6,4},{7,5},{8,10},{9,11},{10,... | collective-permute-start | bytes 1572872 | tf_op jit(solution)/shard_map/ppermute | solution.py:35
  93.2 29.4 %collective-permute-start.14 = (f32[4,64,512]{2,1,0:T(8,128)}, f32[4,64,512]{2,1,0:T(8,128)S(1)}, u32[]{:S(2)}, u32[]{:S(2)}) collective-permute-start(f32[4,64,512]{2,1,0:T(8,128)} %get-tuple-element.118), channel_id=1, source_target_pairs={{0,3},{1,0},{2,1},{3,2},{4,7},{5,4},{6,5},{7,6},{8,11},{9,8},{10,9... | collective-permute-start | bytes 1572872 | tf_op jit(solution)/shard_map/ppermute | solution.py:35
  94.4 35.0 %collective-permute-start.18 = (f32[4,64,512]{2,1,0:T(8,128)}, f32[4,64,512]{2,1,0:T(8,128)S(1)}, u32[]{:S(2)}, u32[]{:S(2)}) collective-permute-start(f32[4,64,512]{2,1,0:T(8,128)} %get-tuple-element.120), channel_id=1, source_target_pairs={{0,4},{1,5},{2,6},{3,7},{4,8},{5,9},{6,10},{7,11},{8,12},{9,13},{1... | collective-permute-start | bytes 1572872 | tf_op jit(solution)/shard_map/ppermute | solution.py:35
  95.3 35.0 %collective-permute-start.19 = (f32[4,64,512]{2,1,0:T(8,128)}, f32[4,64,512]{2,1,0:T(8,128)S(1)}, u32[]{:S(2)}, u32[]{:S(2)}) collective-permute-start(f32[4,64,512]{2,1,0:T(8,128)} %get-tuple-element.121), channel_id=1, source_target_pairs={{0,8},{1,9},{2,10},{3,11},{4,12},{5,13},{6,14},{7,15},{8,0},{9,1},... | collective-permute-start | bytes 1572872 | tf_op jit(solution)/shard_map/ppermute | solution.py:35
  100.5 34.4 %collective-permute-start.20 = (f32[4,64,512]{2,1,0:T(8,128)S(1)}, f32[4,64,512]{2,1,0:T(8,128)S(1)}, u32[]{:S(2)}, u32[]{:S(2)}) collective-permute-start(f32[4,64,512]{2,1,0:T(8,128)S(1)} %copy-done.24), channel_id=1, source_target_pairs={{0,12},{1,13},{2,14},{3,15},{4,0},{5,1},{6,2},{7,3},{8,4},{9,5},{1... | collective-permute-start | bytes 1572872 | tf_op jit(solution)/shard_map/ppermute | solution.py:35
  113.8 31.0 %collective-permute-start.30 = (f32[128,512]{1,0:T(8,128)S(1)}, f32[128,512]{1,0:T(8,128)S(1)}, u32[]{:S(2)}, u32[]{:S(2)}) collective-permute-start(f32[128,512]{1,0:T(8,128)S(1)} %slice.238), channel_id=1, source_target_pairs={{0,16},{1,17},{2,18},{3,19},{4,20},{5,21},{6,22},{7,23},{8,24},{9,... | collective-permute-start | bytes 786440 | tf_op jit(solution)/shard_map/ppermute | solution.py:35
  122.6 25.4 %collective-permute-start.31 = (f32[128,512]{1,0:T(8,128)S(1)}, f32[128,512]{1,0:T(8,128)S(1)}, u32[]{:S(2)}, u32[]{:S(2)}) collective-permute-start(f32[128,512]{1,0:T(8,128)S(1)} %slice.239), channel_id=1, source_target_pairs={{0,48},{1,49},{2,50},{3,51},{4,52},{5,53},{6,54},{7,55},{8,56},{9,... | collective-permute-start | bytes 786440 | tf_op jit(solution)/shard_map/ppermute | solution.py:35
  129.4 11.7 %collective-permute-start.32 = (f32[64,512]{1,0:T(8,128)S(1)}, f32[64,512]{1,0:T(8,128)S(1)}, u32[]{:S(2)}, u32[]{:S(2)}) collective-permute-start(f32[64,512]{1,0:T(8,128)S(1)} %slice.240), channel_id=1, source_target_pairs={{0,32},{1,33},{2,34},{3,35},{4,36},{5,37},{6,38},{7,39},{8,40},{9,... | collective-permute-start | bytes 393224 | tf_op jit(solution)/shard_map/ppermute | solution.py:35
  130.3 14.5 %collective-permute-start.33 = (f32[64,512]{1,0:T(8,128)S(1)}, f32[64,512]{1,0:T(8,128)S(1)}, u32[]{:S(2)}, u32[]{:S(2)}) collective-permute-start(f32[64,512]{1,0:T(8,128)S(1)} %slice.241), channel_id=1, source_target_pairs={{0,32},{1,33},{2,34},{3,35},{4,36},{5,37},{6,38},{7,39},{8,40},{9,... | collective-permute-start | bytes 393224 | tf_op jit(solution)/shard_map/ppermute | solution.py:35
  134.8 13.2 %collective-permute-start.17 = (f32[64,512]{1,0:T(8,128)S(1)}, f32[64,512]{1,0:T(8,128)S(1)}, u32[]{:S(2)}, u32[]{:S(2)}) collective-permute-start(f32[64,512]{1,0:T(8,128)S(1)} %get-tuple-element.141), channel_id=1, source_target_pairs={{0,12},{1,13},{2,14},{3,15},{4,0},{5,1},{6,2},{7,3},{8,4},{9,5},{1... | collective-permute-start | bytes 393224 | tf_op jit(solution)/shard_map/ppermute | solution.py:35
  141.1 13.4 %copy-start.10 = (f32[64,512]{1,0:T(8,128)}, f32[64,512]{1,0:T(8,128)S(1)}, u32[]{:S(2)}) copy-start(f32[64,512]{1,0:T(8,128)S(1)} %collective-permute-done.32.refs_10_) | copy-start | bytes 393220
  141.1 7.6 %collective-permute-start.16 = (f32[64,512]{1,0:T(8,128)S(1)}, f32[64,512]{1,0:T(8,128)S(1)}, u32[]{:S(2)}, u32[]{:S(2)}) collective-permute-start(f32[64,512]{1,0:T(8,128)S(1)} %get-tuple-element.142), channel_id=1, source_target_pairs={{0,8},{1,9},{2,10},{3,11},{4,12},{5,13},{6,14},{7,15},{8,0},{9,1},... | collective-permute-start | bytes 393224 | tf_op jit(solution)/shard_map/ppermute | solution.py:35
  144.8 9.7 %copy-start.11 = (f32[64,512]{1,0:T(8,128)}, f32[64,512]{1,0:T(8,128)S(1)}, u32[]{:S(2)}) copy-start(f32[64,512]{1,0:T(8,128)S(1)} %collective-permute-done.33.refs_11_) | copy-start | bytes 393220
  144.8 6.9 %collective-permute-start.15 = (f32[64,512]{1,0:T(8,128)S(1)}, f32[64,512]{1,0:T(8,128)S(1)}, u32[]{:S(2)}, u32[]{:S(2)}) collective-permute-start(f32[64,512]{1,0:T(8,128)S(1)} %get-tuple-element.143), channel_id=1, source_target_pairs={{0,4},{1,5},{2,6},{3,7},{4,8},{5,9},{6,10},{7,11},{8,12},{9,13},{1... | collective-permute-start | bytes 393224 | tf_op jit(solution)/shard_map/ppermute | solution.py:35
  144.8 9.6 %copy-start.8 = (f32[128,512]{1,0:T(8,128)}, f32[128,512]{1,0:T(8,128)S(1)}, u32[]{:S(2)}) copy-start(f32[128,512]{1,0:T(8,128)S(1)} %collective-permute-done.30.refs_8_) | copy-start | bytes 786436
  144.9 6.9 %collective-permute-start.23 = (f32[64,512]{1,0:T(8,128)S(1)}, f32[64,512]{1,0:T(8,128)S(1)}, u32[]{:S(2)}, u32[]{:S(2)}) collective-permute-start(f32[64,512]{1,0:T(8,128)S(1)} %get-tuple-element.137), channel_id=1, source_target_pairs={{0,3},{1,0},{2,1},{3,2},{4,7},{5,4},{6,5},{7,6},{8,11},{9,8},{10,9... | collective-permute-start | bytes 393224 | tf_op jit(solution)/shard_map/ppermute | solution.py:35
  147.9 5.4 %collective-permute-start.22 = (f32[64,512]{1,0:T(8,128)S(1)}, f32[64,512]{1,0:T(8,128)S(1)}, u32[]{:S(2)}, u32[]{:S(2)}) collective-permute-start(f32[64,512]{1,0:T(8,128)S(1)} %get-tuple-element.138), channel_id=1, source_target_pairs={{0,2},{1,3},{2,0},{3,1},{4,6},{5,7},{6,4},{7,5},{8,10},{9,11},{10,... | collective-permute-start | bytes 393224 | tf_op jit(solution)/shard_map/ppermute | solution.py:35
  148.0 6.5 %collective-permute-start.21 = (f32[64,512]{1,0:T(8,128)S(1)}, f32[64,512]{1,0:T(8,128)S(1)}, u32[]{:S(2)}, u32[]{:S(2)}) collective-permute-start(f32[64,512]{1,0:T(8,128)S(1)} %get-tuple-element.139), channel_id=1, source_target_pairs={{0,1},{1,2},{2,3},{3,0},{4,5},{5,6},{6,7},{7,4},{8,9},{9,10},{10,1... | collective-permute-start | bytes 393224 | tf_op jit(solution)/shard_map/ppermute | solution.py:35
  158.6 15.1 %collective-permute-start.36 = (f32[16,512]{1,0:T(8,128)}, f32[16,512]{1,0:T(8,128)S(1)}, u32[]{:S(2)}, u32[]{:S(2)}) collective-permute-start(f32[16,512]{1,0:T(8,128)} %get-tuple-element.135), channel_id=1, source_target_pairs={{0,192},{64,0},{128,64},{192,128},{1,193},{65,1},{129,65},{193,129... | collective-permute-start | bytes 98312 | tf_op jit(solution)/shard_map/ppermute | solution.py:368
  164.0 9.8 %collective-permute-start.35 = (f32[16,512]{1,0:T(8,128)}, f32[16,512]{1,0:T(8,128)S(1)}, u32[]{:S(2)}, u32[]{:S(2)}) collective-permute-start(f32[16,512]{1,0:T(8,128)} %get-tuple-element.135), channel_id=1, source_target_pairs={{0,128},{64,192},{128,0},{192,64},{1,129},{65,193},{129,1},{193,65... | collective-permute-start | bytes 98312 | tf_op jit(solution)/shard_map/ppermute | solution.py:368
  170.3 3.5 %collective-permute-start.34 = (f32[16,512]{1,0:T(8,128)}, f32[16,512]{1,0:T(8,128)S(1)}, u32[]{:S(2)}, u32[]{:S(2)}) collective-permute-start(f32[16,512]{1,0:T(8,128)} %get-tuple-element.135), channel_id=1, source_target_pairs={{0,64},{64,128},{128,192},{192,0},{1,65},{65,129},{129,193},{193,1... | collective-permute-start | bytes 98312 | tf_op jit(solution)/shard_map/ppermute | solution.py:368
  (15 other events, 57.4 us)
where the time goes:
time: 178 us
  waiting for transfers between devices  63.4 us (36%)
  starting transfers between devices  58.8 us (33%)
  Pallas kernels  42.8 us (24%)
  other arithmetic  10.5 us (6%)
  local copies, waits for them, and re-layouts  1.94 us (1%)
    ppermute x34, waiting for transfers between devices, send(): return lax.ppermute(block, 'modes', route(axis, step))  63.4 us
    ppermute x34, starting transfers between devices, send(): return lax.ppermute(block, 'modes', route(axis, step))  47.1 us
    pallas_call x5, Pallas kernels, partial_sums(): pl.pallas_call(functools.partial(partial_kernel, jobs, len(addends)), gri...  28.8 us
    ppermute x3, starting transfers between devices, per_device(): lax.ppermute(last, 'slab', [(i, (i + k) % 4) for i in range(4)])  11.7 us
    pallas_call x1, Pallas kernels, per_device(): small_call(powers_kernel, split, [VMEM, VMEM], flops=200000000)  3.64 us
  transfers between devices with their start and end apart: 37, of which 15 were waited for; matrix products, arithmetic and copies ran while one was open for 6% of the time, Pallas kernels for 17%

commit v1 on v0

--- a/solution.py
+++ b/solution.py
@@ -331,19 +331,22 @@
         prior=after,
     )
     far_got, near = lax.optimization_barrier((far_got, near))
+    beside = ((near[1], 2, 1), (near[3], 2, -1), (near[5], 1, 1), (near[7], 1, -1))
     late = ring(ring_sums(1, 3, prior, far_got), 1)
     early, high, low, wall = lax.optimization_barrier((early, high, low, wall))
     kept = ring_sums(0, 0, prior, early)
     a1, a3, a2 = kept[0][1] + late[0][1], kept[1][1] + late[1][1], kept[1][0] + late[1][0]
     b1, b3, b2 = kept[2][1] + late[2][1], kept[3][1] + late[3][1], kept[3][0] + late[3][0]
-    near, _ = lax.optimization_barrier((near, (a1, a2, a3, b1, b2, b3)))
+    near_got = []
+    for block, axis, step in beside:
+        near_got.append(send(block, axis, step))
+    across, _ = lax.optimization_barrier(((near[2], near[6]), (a1, a2, a3, b1, b2, b3)))
     a_got = spread((a1, a2, a3), 1)
     b_got = spread((b1, b2, b3), 2)
-    near_a = spread(near[1:4], 2)
-    near_b = spread(near[5:8], 1)
-    a_own, b_own, a_got, b_got = lax.optimization_barrier(
-        ((kept[0], late[0]), (kept[2], late[2]), a_got, b_got)
-    )
+    near_a = [near_got[0], near_got[1], send(across[0], 2, 2)]
+    near_b = [near_got[2], near_got[3], send(across[1], 1, 2)]
+    a_own, a_got = lax.optimization_barrier(((kept[0], late[0]), a_got))
+    b_own, b_got = lax.optimization_barrier(((kept[2], late[2]), b_got))
     a_sum = a_own[0][0] + a_own[1][0] + a_got[0] + a_got[1] + a_got[2]
     b_sum = b_own[0][0] + b_own[1][0] + b_got[0] + b_got[1] + b_got[2]
     from_below = send(a_sum[:CELL], 0, 1)

time: 178 us -> 176 us (0.989)
  waiting for transfers between devices: 63.4 us -> 46.5 us
  starting transfers between devices: 58.8 us -> 73.1 us
    ppermute x34, waiting for transfers between devices: 63.4 us -> 46.5 us  [send(): return lax.ppermute(block, 'modes', route(axis, step))]
    ppermute x34, starting transfers between devices: 47.1 us -> 59.7 us  [send(): return lax.ppermute(block, 'modes', route(axis, step))]
  transfers between devices with their start and end apart: 37 -> 37, of which waited for: 15 -> 13; matrix products, arithmetic and copies ran while one was open for 6% -> 6% of each run, Pallas kernels for 17% -> 18%
where the time goes in v1:
time: 176 us; the launch traced here: 175 us
  starting transfers between devices  73.1 us (42%)
  waiting for transfers between devices  46.5 us (26%)
  Pallas kernels  42.8 us (24%)
  other arithmetic  10.5 us (6%)
  local copies, waits for them, and re-layouts  1.94 us (1%)
    ppermute x34, starting transfers between devices, send(): return lax.ppermute(block, 'modes', route(axis, step))  59.7 us
    ppermute x34, waiting for transfers between devices, send(): return lax.ppermute(block, 'modes', route(axis, step))  46.5 us
    pallas_call x5, Pallas kernels, partial_sums(): pl.pallas_call(functools.partial(partial_kernel, jobs, len(addends)), gri...  28.8 us
    ppermute x3, starting transfers between devices, per_device(): lax.ppermute(last, 'slab', [(i, (i + k) % 4) for i in range(4)])  13.3 us
    pallas_call x1, Pallas kernels, per_device(): small_call(powers_kernel, split, [VMEM, VMEM], flops=200000000)  3.63 us
  transfers between devices with their start and end apart: 37, of which 13 were waited for; matrix products, arithmetic and copies ran while one was open for 6% of the time, Pallas kernels for 18%

profile of v1, /device:TPU:1, one launch (start us, length us, event | category | flops | bytes accessed | tf_op | source)
XLA Modules:
  0.0 175.2 jit_solution(8184026826921383379)
XLA Ops:
  0.0 5.1 %partial_sums.6 = (f32[2,192,512]{2,1,0:T(8,128)}, f32[2,192,512]{2,1,0:T(8,128)}, f32[2,192,512]{2,1,0:T(8,128)}, f32[2,192,512]{2,1,0:T(8,128)}) custom-call(s32[1]{0:T(128)} %bitcast.1.place_ref, s32[4,64]{1,0:T(4,128)} %pattern_ref.9, f32[128,512]{1,0:T(8,128)} %x_ref.8, f32[1,512]{1,0:T(1,128)} %bitcast.87, f32[64,1,512]{2,1,0:T(1,128)} %bitcast.47, ...), custom_call_target="tpu_custom_call" | custom-call | flops 201326592 | bytes 4718592 | tf_op jit(solution)/shard_map/partial_sums/pallas_call | solution.py:107
  5.1 2.1 %collective-permute-start.4 = (f32[2,192,512]{2,1,0:T(8,128)}, f32[2,192,512]{2,1,0:T(8,128)S(1)}, u32[]{:S(2)}, u32[]{:S(2)}) collective-permute-start(f32[2,192,512]{2,1,0:T(8,128)} %get-tuple-element.72), channel_id=1, source_target_pairs={{0,1},{1,2},{2,3},{3,0},{4,5},{5,6},{6,7},{7,4},{8,9},{9,10},{10,1... | collective-permute-start | bytes 2359304 | tf_op jit(solution)/shard_map/ppermute | solution.py:35
  7.2 1.4 collective-permute-start.5
  8.6 1.4 collective-permute-start.6
  10.0 1.4 collective-permute-start.7
  11.4 5.1 %partial_sums.5 = (f32[2,192,512]{2,1,0:T(8,128)}, f32[2,192,512]{2,1,0:T(8,128)}, f32[2,192,512]{2,1,0:T(8,128)}, f32[2,192,512]{2,1,0:T(8,128)}) custom-call(s32[1]{0:T(128)} %bitcast.1.place_ref, s32[4,64]{1,0:T(4,128)} %pattern_ref.9, f32[128,512]{1,0:T(8,128)} %x_ref.8, f32[1,512]{1,0:T(1,128)} %bitcast.88, f32[64,1,512]{2,1,0:T(1,128)} %bitcast.55, ...), custom_call_target="tpu_custom_call" | custom-call | flops 201326592 | bytes 4718592 | tf_op jit(solution)/shard_map/partial_sums/pallas_call | solution.py:107
  16.5 1.4 collective-permute-start
  17.8 6.0 %collective-permute-done.4.refs_16_ = f32[2,192,512]{2,1,0:T(8,128)S(1)} collective-permute-done((f32[2,192,512]{2,1,0:T(8,128)}, f32[2,192,512]{2,1,0:T(8,128)S(1)}, u32[]{:S(2)}, u32[]{:S(2)}) %collective-permute-start.4) | collective-permute-done | bytes 786464 | tf_op jit(solution)/shard_map/ppermute | solution.py:35
  23.9 1.9 %collective-permute-start.1 = (f32[2,192,512]{2,1,0:T(8,128)}, f32[2,192,512]{2,1,0:T(8,128)S(1)}, u32[]{:S(2)}, u32[]{:S(2)}) collective-permute-start(f32[2,192,512]{2,1,0:T(8,128)} %get-tuple-element.66), channel_id=1, source_target_pairs={{0,1},{1,2},{2,3},{3,0},{4,5},{5,6},{6,7},{7,4},{8,9},{9,10},{10,1... | collective-permute-start | bytes 2359304 | tf_op jit(solution)/shard_map/ppermute | solution.py:35
  25.7 3.6 %shard_map.109 = (bf16[4,8,128,128]{3,2,1,0:T(8,128)(2,1)}, bf16[4,8,128,128]{3,2,1,0:T(8,128)(2,1)}) custom-call(f32[1,512]{1,0:T(1,128)} %bitcast.92, f32[4,128,128]{2,1,0:T(8,128)} %inscatter_ref.1), custom_call_target="tpu_custom_call" | custom-call | flops 200000000 | bytes 3145728 | tf_op jit(solution)/shard_map/pallas_call | solution.py:313
  29.4 7.1 %partial_sums.7 = (f32[4,64,512]{2,1,0:T(8,128)}, f32[4,64,512]{2,1,0:T(8,128)}, f32[4,64,512]{2,1,0:T(8,128)}, f32[4,64,512]{2,1,0:T(8,128)}, f32[4,64,512]{2,1...) custom-call(s32[1]{0:T(128)} %bitcast.1.place_ref, s32[4,64]{1,0:T(4,128)} %pattern_ref.9, ...), custom_call_target="tpu_custom_call" | custom-call | flops 268435456 | bytes 6291456 | tf_op jit(solution)/shard_map/partial_sums/pallas_call | solution.py:107
  36.5 3.2 %collective-permute-start.2 = (f32[2,192,512]{2,1,0:T(8,128)}, f32[2,192,512]{2,1,0:T(8,128)S(1)}, u32[]{:S(2)}, u32[]{:S(2)}) collective-permute-start(f32[2,192,512]{2,1,0:T(8,128)} %get-tuple-element.67), channel_id=1, source_target_pairs={{0,12},{1,13},{2,14},{3,15},{4,0},{5,1},{6,2},{7,3},{8,4},{9,5},{1... | collective-permute-start | bytes 2359304 | tf_op jit(solution)/shard_map/ppermute | solution.py:35
  39.8 5.8 %partial_sums.9 = (f32[2,192,512]{2,1,0:T(8,128)}, f32[2,192,512]{2,1,0:T(8,128)}, f32[2,192,512]{2,1,0:T(8,128)}, f32[2,192,512]{2,1,0:T(8,128)}) custom-call(s32[1]{0:T(128)} %bitcast.1.place_ref, s32[4,64]{1,0:T(4,128)} %pattern_ref.9, f32[128,512]{1,0:T(8,128)} %x_ref.8, f32[1,512]{1,0:T(1,128)} %bitcast.90, f32[64,1,512]{2,1,0:T(1,128)} %bitcast.71, ...), custom_call_target="tpu_custom_call" | custom-call | flops 201326592 | bytes 4718592 | tf_op jit(solution)/shard_map/partial_sums/pallas_call | solution.py:107
  45.6 1.1 collective-permute-start.10
  46.7 1.9 %collective-permute-start.11 = (f32[2,192,512]{2,1,0:T(8,128)}, f32[2,192,512]{2,1,0:T(8,128)}, u32[]{:S(2)}, u32[]{:S(2)}) collective-permute-start(f32[2,192,512]{2,1,0:T(8,128)} %get-tuple-element.101), channel_id=1, source_target_pairs={{0,3},{1,0},{2,1},{3,2},{4,7},{5,4},{6,5},{7,6},{8,11},{9,8},{10,9... | collective-permute-start | bytes 2359304 | tf_op jit(solution)/shard_map/ppermute | solution.py:35
  49.6 5.9 %collective-permute-done.2.refs_18_ = f32[2,192,512]{2,1,0:T(8,128)S(1)} collective-permute-done((f32[2,192,512]{2,1,0:T(8,128)}, f32[2,192,512]{2,1,0:T(8,128)S(1)}, u32[]{:S(2)}, u32[]{:S(2)}) %collective-permute-start.2) | collective-permute-done | bytes 786464 | tf_op jit(solution)/shard_map/ppermute | solution.py:35
  55.5 3.1 %collective-permute-done.3.refs_19_ = f32[2,192,512]{2,1,0:T(8,128)S(1)} collective-permute-done((f32[2,192,512]{2,1,0:T(8,128)}, f32[2,192,512]{2,1,0:T(8,128)S(1)}, u32[]{:S(2)}, u32[]{:S(2)}) %collective-permute-start.3) | collective-permute-done | bytes 786464 | tf_op jit(solution)/shard_map/ppermute | solution.py:35
  59.5 5.8 %partial_sums.8 = (f32[2,192,512]{2,1,0:T(8,128)}, f32[2,192,512]{2,1,0:T(8,128)}, f32[2,192,512]{2,1,0:T(8,128)}, f32[2,192,512]{2,1,0:T(8,128)}) custom-call(s32[1]{0:T(128)} %bitcast.1.place_ref, s32[4,64]{1,0:T(4,128)} %pattern_ref.9, f32[128,512]{1,0:T(8,128)} %x_ref.8, f32[1,512]{1,0:T(1,128)} %bitcast.91, f32[64,1,512]{2,1,0:T(1,128)} %bitcast.79, ...), custom_call_target="tpu_custom_call" | custom-call | flops 201326592 | bytes 4718592 | tf_op jit(solution)/shard_map/partial_sums/pallas_call | solution.py:107
  65.4 1.3 fusion.5
  67.4 1.5 fusion.3
  68.9 2.1 %collective-permute-start.26 = (f32[192,512]{1,0:T(8,128)S(1)}, f32[192,512]{1,0:T(8,128)S(1)}, u32[]{:S(2)}, u32[]{:S(2)}) collective-permute-start(f32[192,512]{1,0:T(8,128)S(1)} %get-tuple-element.135), channel_id=1, source_target_pairs={{0,12},{1,13},{2,14},{3,15},{4,0},{5,1},{6,2},{7,3},{8,4},{9,5},{1... | collective-permute-start | bytes 1179656 | tf_op jit(solution)/shard_map/ppermute | solution.py:35
  71.2 4.3 %collective-permute-done.12 = f32[2,192,512]{2,1,0:T(8,128)} collective-permute-done((f32[2,192,512]{2,1,0:T(8,128)}, f32[2,192,512]{2,1,0:T(8,128)}, u32[]{:S(2)}, u32[]{:S(2)}) %collective-permute-start.12) | collective-permute-done | bytes 786464 | tf_op jit(solution)/shard_map/ppermute | solution.py:35
  75.5 1.2 fusion.2
  78.4 1.5 fusion
  79.9 5.0 %collective-permute-done.24 = f32[192,512]{1,0:T(8,128)S(1)} collective-permute-done((f32[192,512]{1,0:T(8,128)S(1)}, f32[192,512]{1,0:T(8,128)S(1)}, u32[]{:S(2)}, u32[]{:S(2)}) %collective-permute-start.24) | collective-permute-done | bytes 393248 | tf_op jit(solution)/shard_map/ppermute | solution.py:35
  85.0 2.3 %collective-permute-start.30 = (f32[192,512]{1,0:T(8,128)S(1)}, f32[192,512]{1,0:T(8,128)S(1)}, u32[]{:S(2)}, u32[]{:S(2)}) collective-permute-start(f32[192,512]{1,0:T(8,128)S(1)} %get-tuple-element.133), channel_id=1, source_target_pairs={{0,3},{1,0},{2,1},{3,2},{4,7},{5,4},{6,5},{7,6},{8,11},{9,8},{10,9... | collective-permute-start | bytes 1179656 | tf_op jit(solution)/shard_map/ppermute | solution.py:35
  87.4 3.7 %collective-permute-done.25 = f32[192,512]{1,0:T(8,128)S(1)} collective-permute-done((f32[192,512]{1,0:T(8,128)S(1)}, f32[192,512]{1,0:T(8,128)S(1)}, u32[]{:S(2)}, u32[]{:S(2)}) %collective-permute-start.25) | collective-permute-done | bytes 393248 | tf_op jit(solution)/shard_map/ppermute | solution.py:35
  91.1 2.1 %collective-permute-start.9 = (f32[4,64,512]{2,1,0:T(8,128)}, f32[4,64,512]{2,1,0:T(8,128)S(1)}, u32[]{:S(2)}, u32[]{:S(2)}) collective-permute-start(f32[4,64,512]{2,1,0:T(8,128)} %get-tuple-element.87), channel_id=1, source_target_pairs={{0,3},{1,0},{2,1},{3,2},{4,7},{5,4},{6,5},{7,6},{8,11},{9,8},{10,9... | collective-permute-start | bytes 1572872 | tf_op jit(solution)/shard_map/ppermute | solution.py:35
  93.8 1.3 fusion.9
  95.1 1.1 collective-permute-done.30
  96.2 7.2 %collective-permute-done.29 = f32[192,512]{1,0:T(8,128)S(1)} collective-permute-done((f32[192,512]{1,0:T(8,128)S(1)}, f32[192,512]{1,0:T(8,128)S(1)}, u32[]{:S(2)}, u32[]{:S(2)}) %collective-permute-start.29) | collective-permute-done | bytes 393248 | tf_op jit(solution)/shard_map/ppermute | solution.py:35
  103.5 1.4 collective-permute-start.20
  104.9 1.2 fusion.7
  106.1 11.5 %collective-permute-start.27 = (f32[128,512]{1,0:T(8,128)S(1)}, f32[128,512]{1,0:T(8,128)S(1)}, u32[]{:S(2)}, u32[]{:S(2)}) collective-permute-start(f32[128,512]{1,0:T(8,128)S(1)} %slice.238), channel_id=1, source_target_pairs={{0,16},{1,17},{2,18},{3,19},{4,20},{5,21},{6,22},{7,23},{8,24},{9,... | collective-permute-start | bytes 786440 | tf_op jit(solution)/shard_map/ppermute | solution.py:35
  117.6 3.3 %collective-permute-start.31 = (f32[128,512]{1,0:T(8,128)S(1)}, f32[128,512]{1,0:T(8,128)S(1)}, u32[]{:S(2)}, u32[]{:S(2)}) collective-permute-start(f32[128,512]{1,0:T(8,128)S(1)} %slice.239), channel_id=1, source_target_pairs={{0,48},{1,49},{2,50},{3,51},{4,52},{5,53},{6,54},{7,55},{8,56},{9,... | collective-permute-start | bytes 786440 | tf_op jit(solution)/shard_map/ppermute | solution.py:35
  122.7 4.5 %collective-permute-start.33 = (f32[64,512]{1,0:T(8,128)S(1)}, f32[64,512]{1,0:T(8,128)S(1)}, u32[]{:S(2)}, u32[]{:S(2)}) collective-permute-start(f32[64,512]{1,0:T(8,128)S(1)} %slice.241), channel_id=1, source_target_pairs={{0,32},{1,33},{2,34},{3,35},{4,36},{5,37},{6,38},{7,39},{8,40},{9,... | collective-permute-start | bytes 393224 | tf_op jit(solution)/shard_map/ppermute | solution.py:35
  128.0 1.5 collective-permute-done.32.refs_10_
  129.6 1.6 collective-permute-start.16
  131.2 2.4 %collective-permute-done.33.refs_11_ = f32[64,512]{1,0:T(8,128)S(1)} collective-permute-done((f32[64,512]{1,0:T(8,128)S(1)}, f32[64,512]{1,0:T(8,128)S(1)}, u32[]{:S(2)}, u32[]{:S(2)}) %collective-permute-start.33) | collective-permute-done | bytes 131104 | tf_op jit(solution)/shard_map/ppermute | solution.py:35
  133.6 9.8 %collective-permute-start.23 = (f32[64,512]{1,0:T(8,128)S(1)}, f32[64,512]{1,0:T(8,128)S(1)}, u32[]{:S(2)}, u32[]{:S(2)}) collective-permute-start(f32[64,512]{1,0:T(8,128)S(1)} %get-tuple-element.125), channel_id=1, source_target_pairs={{0,3},{1,0},{2,1},{3,2},{4,7},{5,4},{6,5},{7,6},{8,11},{9,8},{10,9... | collective-permute-start | bytes 393224 | tf_op jit(solution)/shard_map/ppermute | solution.py:35
  144.1 2.6 %collective-permute-done.23.refs_7_ = f32[64,512]{1,0:T(8,128)S(1)} collective-permute-done((f32[64,512]{1,0:T(8,128)S(1)}, f32[64,512]{1,0:T(8,128)S(1)}, u32[]{:S(2)}, u32[]{:S(2)}) %collective-permute-start.23) | collective-permute-done | bytes 131104 | tf_op jit(solution)/shard_map/ppermute | solution.py:35
  146.7 2.3 %collective-permute-done.22.refs_6_ = f32[64,512]{1,0:T(8,128)S(1)} collective-permute-done((f32[64,512]{1,0:T(8,128)S(1)}, f32[64,512]{1,0:T(8,128)S(1)}, u32[]{:S(2)}, u32[]{:S(2)}) %collective-permute-start.22) | collective-permute-done | bytes 131104 | tf_op jit(solution)/shard_map/ppermute | solution.py:35
  149.0 1.2 collective-permute-done.21.refs_5_
  150.9 3.5 %shard_map.110 = (f32[128,512]{1,0:T(8,128)}, f32[16,512]{1,0:T(8,128)}) custom-call(s32[4]{0:T(128)} %direction_ref.5, f32[64,512]{1,0:T(8,128)} %get-tuple-element.132.refs_0_, f32[64,512]{1,0:T(8,128)} %copy-done.14, f32[64,512]{1,0:T(8,128)} %copy-done.13, f32[64,512]{1,0:T(8,128)} %copy-done.12, f32[64,512]{1,0:T(8,128)} %get-tuple-element.128.refs_4_, ...), custom_call_target="tpu_custom_call" | custom-call | flops 40000000 | bytes 3145728 | tf_op jit(solution)/shard_map/pallas_call | solution.py:364
  154.4 11.0 %collective-permute-start.36 = (f32[16,512]{1,0:T(8,128)}, f32[16,512]{1,0:T(8,128)S(1)}, u32[]{:S(2)}, u32[]{:S(2)}) collective-permute-start(f32[16,512]{1,0:T(8,128)} %get-tuple-element.123), channel_id=1, source_target_pairs={{0,192},{64,0},{128,64},{192,128},{1,193},{65,1},{129,65},{193,129... | collective-permute-start | bytes 98312 | tf_op jit(solution)/shard_map/ppermute | solution.py:371
  165.4 2.3 %collective-permute-start.35 = (f32[16,512]{1,0:T(8,128)}, f32[16,512]{1,0:T(8,128)S(1)}, u32[]{:S(2)}, u32[]{:S(2)}) collective-permute-start(f32[16,512]{1,0:T(8,128)} %get-tuple-element.123), channel_id=1, source_target_pairs={{0,128},{64,192},{128,0},{192,64},{1,129},{65,193},{129,1},{193,65... | collective-permute-start | bytes 98312 | tf_op jit(solution)/shard_map/ppermute | solution.py:371
  167.7 3.4 %shard_map.111.particular_ref = f32[128,512]{1,0:T(8,128)} custom-call(s32[4]{0:T(128)} %direction_ref.5, f32[128,512]{1,0:T(8,128)} %get-tuple-element.124.source_ref, f32[1,512]{1,0:T(1,128)} %bitcast.93, bf16[4,8,128,128]{3,2,1,0:T(8,128)(2,1)} %get-tuple-element.121.refs_12_.high_ref, bf16[4,8,128,128]{3,2,1,0:T(8,128)(2,1)} %get-tuple-element.122.refs_13_.low_ref), custom_call_target="tpu_custom_call" | custom-call | flops 40000000 | bytes 3145728 | tf_op jit(solution)/shard_map/pallas_call | solution.py:373
  171.7 3.5 %shard_map.112 = f32[128,512]{1,0:T(8,128)} custom-call(s32[4]{0:T(128)} %direction_ref.5, s32[1]{0:T(128)} %bitcast.slab_ref, f32[16,512]{1,0:T(8,128)} %select_reduce_fusion.wall_ref, f32[16,512]{1,0:T(8,128)} %copy-done.20, f32[16,512]{1,0:T(8,128)} %copy-done.19, f32[16,512]{1,0:T(8,128)} %copy-done.18, f32[1,512]{1,0:T(1,128)} %bitcast.94, ...), custom_call_target="tpu_custom_call" | custom-call | flops 60000000 | bytes 3145728 | tf_op jit(solution)/shard_map/pallas_call | solution.py:376
  (108 shorter events, 10.0 us)
Async XLA Ops:
  5.1 18.8 %collective-permute-start.4 = (f32[2,192,512]{2,1,0:T(8,128)}, f32[2,192,512]{2,1,0:T(8,128)S(1)}, u32[]{:S(2)}, u32[]{:S(2)}) collective-permute-start(f32[2,192,512]{2,1,0:T(8,128)} %get-tuple-element.72), channel_id=1, source_target_pairs={{0,1},{1,2},{2,3},{3,0},{4,5},{5,6},{6,7},{7,4},{8,9},{9,10},{10,1... | collective-permute-start | bytes 2359304 | tf_op jit(solution)/shard_map/ppermute | solution.py:35
  7.2 29.3 %collective-permute-start.5 = (f32[2,192,512]{2,1,0:T(8,128)}, f32[2,192,512]{2,1,0:T(8,128)}, u32[]{:S(2)}, u32[]{:S(2)}) collective-permute-start(f32[2,192,512]{2,1,0:T(8,128)} %get-tuple-element.73), channel_id=1, source_target_pairs={{0,3},{1,0},{2,1},{3,2},{4,7},{5,4},{6,5},{7,6},{8,11},{9,8},{10,9... | collective-permute-start | bytes 2359304 | tf_op jit(solution)/shard_map/ppermute | solution.py:35
  8.6 31.2 %collective-permute-start.6 = (f32[2,192,512]{2,1,0:T(8,128)}, f32[2,192,512]{2,1,0:T(8,128)}, u32[]{:S(2)}, u32[]{:S(2)}) collective-permute-start(f32[2,192,512]{2,1,0:T(8,128)} %get-tuple-element.74), channel_id=1, source_target_pairs={{0,4},{1,5},{2,6},{3,7},{4,8},{5,9},{6,10},{7,11},{8,12},{9,13},{1... | collective-permute-start | bytes 2359304 | tf_op jit(solution)/shard_map/ppermute | solution.py:35
  10.0 29.8 %collective-permute-start.7 = (f32[2,192,512]{2,1,0:T(8,128)}, f32[2,192,512]{2,1,0:T(8,128)}, u32[]{:S(2)}, u32[]{:S(2)}) collective-permute-start(f32[2,192,512]{2,1,0:T(8,128)} %get-tuple-element.75), channel_id=1, source_target_pairs={{0,12},{1,13},{2,14},{3,15},{4,0},{5,1},{6,2},{7,3},{8,4},{9,5},{1... | collective-permute-start | bytes 2359304 | tf_op jit(solution)/shard_map/ppermute | solution.py:35
  16.5 30.3 %collective-permute-start = (f32[2,192,512]{2,1,0:T(8,128)}, f32[2,192,512]{2,1,0:T(8,128)S(1)}, u32[]{:S(2)}, u32[]{:S(2)}) collective-permute-start(f32[2,192,512]{2,1,0:T(8,128)} %get-tuple-element.65), channel_id=1, source_target_pairs={{0,3},{1,0},{2,1},{3,2},{4,7},{5,4},{6,5},{7,6},{8,11},{9,8},{10,9... | collective-permute-start | bytes 2359304 | tf_op jit(solution)/shard_map/ppermute | solution.py:35
  23.9 12.6 %copy-start.3 = (f32[2,192,512]{2,1,0:T(8,128)}, f32[2,192,512]{2,1,0:T(8,128)S(1)}, u32[]{:S(2)}) copy-start(f32[2,192,512]{2,1,0:T(8,128)S(1)} %collective-permute-done.4.refs_16_) | copy-start | bytes 2359300
  23.9 24.8 %collective-permute-start.1 = (f32[2,192,512]{2,1,0:T(8,128)}, f32[2,192,512]{2,1,0:T(8,128)S(1)}, u32[]{:S(2)}, u32[]{:S(2)}) collective-permute-start(f32[2,192,512]{2,1,0:T(8,128)} %get-tuple-element.66), channel_id=1, source_target_pairs={{0,1},{1,2},{2,3},{3,0},{4,5},{5,6},{6,7},{7,4},{8,9},{9,10},{10,1... | collective-permute-start | bytes 2359304 | tf_op jit(solution)/shard_map/ppermute | solution.py:35
  36.5 19.0 %collective-permute-start.2 = (f32[2,192,512]{2,1,0:T(8,128)}, f32[2,192,512]{2,1,0:T(8,128)S(1)}, u32[]{:S(2)}, u32[]{:S(2)}) collective-permute-start(f32[2,192,512]{2,1,0:T(8,128)} %get-tuple-element.67), channel_id=1, source_target_pairs={{0,12},{1,13},{2,14},{3,15},{4,0},{5,1},{6,2},{7,3},{8,4},{9,5},{1... | collective-permute-start | bytes 2359304 | tf_op jit(solution)/shard_map/ppermute | solution.py:35
  39.8 18.9 %collective-permute-start.3 = (f32[2,192,512]{2,1,0:T(8,128)}, f32[2,192,512]{2,1,0:T(8,128)S(1)}, u32[]{:S(2)}, u32[]{:S(2)}) collective-permute-start(f32[2,192,512]{2,1,0:T(8,128)} %get-tuple-element.68), channel_id=1, source_target_pairs={{0,4},{1,5},{2,6},{3,7},{4,8},{5,9},{6,10},{7,11},{8,12},{9,13},{1... | collective-permute-start | bytes 2359304 | tf_op jit(solution)/shard_map/ppermute | solution.py:35
  45.6 19.8 %collective-permute-start.10 = (f32[2,192,512]{2,1,0:T(8,128)}, f32[2,192,512]{2,1,0:T(8,128)}, u32[]{:S(2)}, u32[]{:S(2)}) collective-permute-start(f32[2,192,512]{2,1,0:T(8,128)} %get-tuple-element.99), channel_id=1, source_target_pairs={{0,1},{1,2},{2,3},{3,0},{4,5},{5,6},{6,7},{7,4},{8,9},{9,10},{10,1... | collective-permute-start | bytes 2359304 | tf_op jit(solution)/shard_map/ppermute | solution.py:35
  46.7 12.3 %copy-start = (f32[2,192,512]{2,1,0:T(8,128)}, f32[2,192,512]{2,1,0:T(8,128)S(1)}, u32[]{:S(2)}) copy-start(f32[2,192,512]{2,1,0:T(8,128)S(1)} %collective-permute-done.refs_16_) | copy-start | bytes 2359300
  46.7 20.7 %collective-permute-start.11 = (f32[2,192,512]{2,1,0:T(8,128)}, f32[2,192,512]{2,1,0:T(8,128)}, u32[]{:S(2)}, u32[]{:S(2)}) collective-permute-start(f32[2,192,512]{2,1,0:T(8,128)} %get-tuple-element.101), channel_id=1, source_target_pairs={{0,3},{1,0},{2,1},{3,2},{4,7},{5,4},{6,5},{7,6},{8,11},{9,8},{10,9... | collective-permute-start | bytes 2359304 | tf_op jit(solution)/shard_map/ppermute | solution.py:35
  48.7 26.8 %collective-permute-start.12 = (f32[2,192,512]{2,1,0:T(8,128)}, f32[2,192,512]{2,1,0:T(8,128)}, u32[]{:S(2)}, u32[]{:S(2)}) collective-permute-start(f32[2,192,512]{2,1,0:T(8,128)} %get-tuple-element.103), channel_id=1, source_target_pairs={{0,4},{1,5},{2,6},{3,7},{4,8},{5,9},{6,10},{7,11},{8,12},{9,13},{1... | collective-permute-start | bytes 2359304 | tf_op jit(solution)/shard_map/ppermute | solution.py:35
  58.6 18.9 %collective-permute-start.13 = (f32[2,192,512]{2,1,0:T(8,128)}, f32[2,192,512]{2,1,0:T(8,128)}, u32[]{:S(2)}, u32[]{:S(2)}) collective-permute-start(f32[2,192,512]{2,1,0:T(8,128)} %get-tuple-element.105), channel_id=1, source_target_pairs={{0,12},{1,13},{2,14},{3,15},{4,0},{5,1},{6,2},{7,3},{8,4},{9,5},{1... | collective-permute-start | bytes 2359304 | tf_op jit(solution)/shard_map/ppermute | solution.py:35
  65.3 30.9 %copy-start.26 = (f32[4,64,512]{2,1,0:T(8,128)S(1)}, f32[4,64,512]{2,1,0:T(8,128)}, u32[]{:S(2)}) copy-start(f32[4,64,512]{2,1,0:T(8,128)} %get-tuple-element.108) | copy-start | bytes 1572868
  65.3 38.1 %copy-start.25 = (f32[4,64,512]{2,1,0:T(8,128)S(1)}, f32[4,64,512]{2,1,0:T(8,128)}, u32[]{:S(2)}) copy-start(f32[4,64,512]{2,1,0:T(8,128)} %get-tuple-element.109) | copy-start | bytes 1572868
  65.3 38.1 %copy-start.24 = (f32[4,64,512]{2,1,0:T(8,128)S(1)}, f32[4,64,512]{2,1,0:T(8,128)}, u32[]{:S(2)}) copy-start(f32[4,64,512]{2,1,0:T(8,128)} %get-tuple-element.110) | copy-start | bytes 1572868
  65.3 39.5 %copy-start.5 = (f32[2,192,512]{2,1,0:T(8,128)S(1)}, f32[2,192,512]{2,1,0:T(8,128)}, u32[]{:S(2)}) copy-start(f32[2,192,512]{2,1,0:T(8,128)} %get-tuple-element.116) | copy-start | bytes 2359300
  65.3 55.6 %copy-start.7 = (f32[4,64,512]{2,1,0:T(8,128)S(1)}, f32[4,64,512]{2,1,0:T(8,128)}, u32[]{:S(2)}) copy-start(f32[4,64,512]{2,1,0:T(8,128)} %get-tuple-element.85) | copy-start | bytes 1572868
  65.4 61.8 %copy-start.6 = (f32[4,64,512]{2,1,0:T(8,128)S(1)}, f32[4,64,512]{2,1,0:T(8,128)}, u32[]{:S(2)}) copy-start(f32[4,64,512]{2,1,0:T(8,128)} %get-tuple-element.107) | copy-start | bytes 1572868
  66.7 18.3 %collective-permute-start.24 = (f32[192,512]{1,0:T(8,128)S(1)}, f32[192,512]{1,0:T(8,128)S(1)}, u32[]{:S(2)}, u32[]{:S(2)}) collective-permute-start(f32[192,512]{1,0:T(8,128)S(1)} %fusion.5), channel_id=1, source_target_pairs={{0,4},{1,5},{2,6},{3,7},{4,8},{5,9},{6,10},{7,11},{8,12},{9,13},{1... | collective-permute-start | bytes 1179656 | tf_op jit(solution)/shard_map/ppermute | solution.py:35
  68.9 18.4 %collective-permute-start.26 = (f32[192,512]{1,0:T(8,128)S(1)}, f32[192,512]{1,0:T(8,128)S(1)}, u32[]{:S(2)}, u32[]{:S(2)}) collective-permute-start(f32[192,512]{1,0:T(8,128)S(1)} %get-tuple-element.135), channel_id=1, source_target_pairs={{0,12},{1,13},{2,14},{3,15},{4,0},{5,1},{6,2},{7,3},{8,4},{9,5},{1... | collective-permute-start | bytes 1179656 | tf_op jit(solution)/shard_map/ppermute | solution.py:35
  71.0 20.1 %collective-permute-start.25 = (f32[192,512]{1,0:T(8,128)S(1)}, f32[192,512]{1,0:T(8,128)S(1)}, u32[]{:S(2)}, u32[]{:S(2)}) collective-permute-start(f32[192,512]{1,0:T(8,128)S(1)} %get-tuple-element.136), channel_id=1, source_target_pairs={{0,8},{1,9},{2,10},{3,11},{4,12},{5,13},{6,14},{7,15},{8,0},{9,1},... | collective-permute-start | bytes 1179656 | tf_op jit(solution)/shard_map/ppermute | solution.py:35
  76.7 16.6 %collective-permute-start.28 = (f32[192,512]{1,0:T(8,128)S(1)}, f32[192,512]{1,0:T(8,128)S(1)}, u32[]{:S(2)}, u32[]{:S(2)}) collective-permute-start(f32[192,512]{1,0:T(8,128)S(1)} %fusion.2), channel_id=1, source_target_pairs={{0,1},{1,2},{2,3},{3,0},{4,5},{5,6},{6,7},{7,4},{8,9},{9,10},{10,1... | collective-permute-start | bytes 1179656 | tf_op jit(solution)/shard_map/ppermute | solution.py:35
  77.5 25.9 %collective-permute-start.8 = (f32[4,64,512]{2,1,0:T(8,128)}, f32[4,64,512]{2,1,0:T(8,128)S(1)}, u32[]{:S(2)}, u32[]{:S(2)}) collective-permute-start(f32[4,64,512]{2,1,0:T(8,128)} %get-tuple-element.86), channel_id=1, source_target_pairs={{0,1},{1,2},{2,3},{3,0},{4,5},{5,6},{6,7},{7,4},{8,9},{9,10},{10,1... | collective-permute-start | bytes 1572872 | tf_op jit(solution)/shard_map/ppermute | solution.py:35
  85.0 11.2 %collective-permute-start.30 = (f32[192,512]{1,0:T(8,128)S(1)}, f32[192,512]{1,0:T(8,128)S(1)}, u32[]{:S(2)}, u32[]{:S(2)}) collective-permute-start(f32[192,512]{1,0:T(8,128)S(1)} %get-tuple-element.133), channel_id=1, source_target_pairs={{0,3},{1,0},{2,1},{3,2},{4,7},{5,4},{6,5},{7,6},{8,11},{9,8},{10,9... | collective-permute-start | bytes 1179656 | tf_op jit(solution)/shard_map/ppermute | solution.py:35
  87.3 16.2 %collective-permute-start.29 = (f32[192,512]{1,0:T(8,128)S(1)}, f32[192,512]{1,0:T(8,128)S(1)}, u32[]{:S(2)}, u32[]{:S(2)}) collective-permute-start(f32[192,512]{1,0:T(8,128)S(1)} %get-tuple-element.134), channel_id=1, source_target_pairs={{0,2},{1,3},{2,0},{3,1},{4,6},{5,7},{6,4},{7,5},{8,10},{9,11},{10,... | collective-permute-start | bytes 1179656 | tf_op jit(solution)/shard_map/ppermute | solution.py:35
  91.1 15.0 %collective-permute-start.9 = (f32[4,64,512]{2,1,0:T(8,128)}, f32[4,64,512]{2,1,0:T(8,128)S(1)}, u32[]{:S(2)}, u32[]{:S(2)}) collective-permute-start(f32[4,64,512]{2,1,0:T(8,128)} %get-tuple-element.87), channel_id=1, source_target_pairs={{0,3},{1,0},{2,1},{3,2},{4,7},{5,4},{6,5},{7,6},{8,11},{9,8},{10,9... | collective-permute-start | bytes 1572872 | tf_op jit(solution)/shard_map/ppermute | solution.py:35
  93.2 24.3 %collective-permute-start.14 = (f32[4,64,512]{2,1,0:T(8,128)}, f32[4,64,512]{2,1,0:T(8,128)S(1)}, u32[]{:S(2)}, u32[]{:S(2)}) collective-permute-start(f32[4,64,512]{2,1,0:T(8,128)} %get-tuple-element.106), channel_id=1, source_target_pairs={{0,2},{1,3},{2,0},{3,1},{4,6},{5,7},{6,4},{7,5},{8,10},{9,11},{10,... | collective-permute-start | bytes 1572872 | tf_op jit(solution)/shard_map/ppermute | solution.py:35
  96.2 25.6 %collective-permute-start.18 = (f32[4,64,512]{2,1,0:T(8,128)S(1)}, f32[4,64,512]{2,1,0:T(8,128)S(1)}, u32[]{:S(2)}, u32[]{:S(2)}) collective-permute-start(f32[4,64,512]{2,1,0:T(8,128)S(1)} %copy-done.26), channel_id=1, source_target_pairs={{0,4},{1,5},{2,6},{3,7},{4,8},{5,9},{6,10},{7,11},{8,12},{9,13},{1... | collective-permute-start | bytes 1572872 | tf_op jit(solution)/shard_map/ppermute | solution.py:35
  103.4 19.3 %collective-permute-start.19 = (f32[4,64,512]{2,1,0:T(8,128)S(1)}, f32[4,64,512]{2,1,0:T(8,128)S(1)}, u32[]{:S(2)}, u32[]{:S(2)}) collective-permute-start(f32[4,64,512]{2,1,0:T(8,128)S(1)} %copy-done.25), channel_id=1, source_target_pairs={{0,12},{1,13},{2,14},{3,15},{4,0},{5,1},{6,2},{7,3},{8,4},{9,5},{1... | collective-permute-start | bytes 1572872 | tf_op jit(solution)/shard_map/ppermute | solution.py:35
  103.5 23.7 %collective-permute-start.20 = (f32[4,64,512]{2,1,0:T(8,128)S(1)}, f32[4,64,512]{2,1,0:T(8,128)S(1)}, u32[]{:S(2)}, u32[]{:S(2)}) collective-permute-start(f32[4,64,512]{2,1,0:T(8,128)S(1)} %copy-done.24), channel_id=1, source_target_pairs={{0,8},{1,9},{2,10},{3,11},{4,12},{5,13},{6,14},{7,15},{8,0},{9,1},... | collective-permute-start | bytes 1572872 | tf_op jit(solution)/shard_map/ppermute | solution.py:35
  106.1 27.5 %collective-permute-start.27 = (f32[128,512]{1,0:T(8,128)S(1)}, f32[128,512]{1,0:T(8,128)S(1)}, u32[]{:S(2)}, u32[]{:S(2)}) collective-permute-start(f32[128,512]{1,0:T(8,128)S(1)} %slice.238), channel_id=1, source_target_pairs={{0,16},{1,17},{2,18},{3,19},{4,20},{5,21},{6,22},{7,23},{8,24},{9,... | collective-permute-start | bytes 786440 | tf_op jit(solution)/shard_map/ppermute | solution.py:35
  117.6 25.8 %collective-permute-start.31 = (f32[128,512]{1,0:T(8,128)S(1)}, f32[128,512]{1,0:T(8,128)S(1)}, u32[]{:S(2)}, u32[]{:S(2)}) collective-permute-start(f32[128,512]{1,0:T(8,128)S(1)} %slice.239), channel_id=1, source_target_pairs={{0,48},{1,49},{2,50},{3,51},{4,52},{5,53},{6,54},{7,55},{8,56},{9,... | collective-permute-start | bytes 786440 | tf_op jit(solution)/shard_map/ppermute | solution.py:35
  121.8 7.8 %collective-permute-start.32 = (f32[64,512]{1,0:T(8,128)S(1)}, f32[64,512]{1,0:T(8,128)S(1)}, u32[]{:S(2)}, u32[]{:S(2)}) collective-permute-start(f32[64,512]{1,0:T(8,128)S(1)} %slice.240), channel_id=1, source_target_pairs={{0,32},{1,33},{2,34},{3,35},{4,36},{5,37},{6,38},{7,39},{8,40},{9,... | collective-permute-start | bytes 393224 | tf_op jit(solution)/shard_map/ppermute | solution.py:35
  122.7 10.9 %collective-permute-start.33 = (f32[64,512]{1,0:T(8,128)S(1)}, f32[64,512]{1,0:T(8,128)S(1)}, u32[]{:S(2)}, u32[]{:S(2)}) collective-permute-start(f32[64,512]{1,0:T(8,128)S(1)} %slice.241), channel_id=1, source_target_pairs={{0,32},{1,33},{2,34},{3,35},{4,36},{5,37},{6,38},{7,39},{8,40},{9,... | collective-permute-start | bytes 393224 | tf_op jit(solution)/shard_map/ppermute | solution.py:35
  127.2 16.2 %collective-permute-start.17 = (f32[64,512]{1,0:T(8,128)S(1)}, f32[64,512]{1,0:T(8,128)S(1)}, u32[]{:S(2)}, u32[]{:S(2)}) collective-permute-start(f32[64,512]{1,0:T(8,128)S(1)} %get-tuple-element.129), channel_id=1, source_target_pairs={{0,12},{1,13},{2,14},{3,15},{4,0},{5,1},{6,2},{7,3},{8,4},{9,5},{1... | collective-permute-start | bytes 393224 | tf_op jit(solution)/shard_map/ppermute | solution.py:35
  129.6 20.7 %copy-start.10 = (f32[64,512]{1,0:T(8,128)}, f32[64,512]{1,0:T(8,128)S(1)}, u32[]{:S(2)}) copy-start(f32[64,512]{1,0:T(8,128)S(1)} %collective-permute-done.32.refs_10_) | copy-start | bytes 393220
  129.6 14.5 %collective-permute-start.16 = (f32[64,512]{1,0:T(8,128)S(1)}, f32[64,512]{1,0:T(8,128)S(1)}, u32[]{:S(2)}, u32[]{:S(2)}) collective-permute-start(f32[64,512]{1,0:T(8,128)S(1)} %get-tuple-element.130), channel_id=1, source_target_pairs={{0,8},{1,9},{2,10},{3,11},{4,12},{5,13},{6,14},{7,15},{8,0},{9,1},... | collective-permute-start | bytes 393224 | tf_op jit(solution)/shard_map/ppermute | solution.py:35
  133.6 16.6 %copy-start.11 = (f32[64,512]{1,0:T(8,128)}, f32[64,512]{1,0:T(8,128)S(1)}, u32[]{:S(2)}) copy-start(f32[64,512]{1,0:T(8,128)S(1)} %collective-permute-done.33.refs_11_) | copy-start | bytes 393220
  133.6 10.5 %collective-permute-start.15 = (f32[64,512]{1,0:T(8,128)S(1)}, f32[64,512]{1,0:T(8,128)S(1)}, u32[]{:S(2)}, u32[]{:S(2)}) collective-permute-start(f32[64,512]{1,0:T(8,128)S(1)} %get-tuple-element.131), channel_id=1, source_target_pairs={{0,4},{1,5},{2,6},{3,7},{4,8},{5,9},{6,10},{7,11},{8,12},{9,13},{1... | collective-permute-start | bytes 393224 | tf_op jit(solution)/shard_map/ppermute | solution.py:35
  133.6 16.6 %copy-start.8 = (f32[128,512]{1,0:T(8,128)}, f32[128,512]{1,0:T(8,128)S(1)}, u32[]{:S(2)}) copy-start(f32[128,512]{1,0:T(8,128)S(1)} %collective-permute-done.27.refs_8_) | copy-start | bytes 786436
  133.6 13.1 %collective-permute-start.23 = (f32[64,512]{1,0:T(8,128)S(1)}, f32[64,512]{1,0:T(8,128)S(1)}, u32[]{:S(2)}, u32[]{:S(2)}) collective-permute-start(f32[64,512]{1,0:T(8,128)S(1)} %get-tuple-element.125), channel_id=1, source_target_pairs={{0,3},{1,0},{2,1},{3,2},{4,7},{5,4},{6,5},{7,6},{8,11},{9,8},{10,9... | collective-permute-start | bytes 393224 | tf_op jit(solution)/shard_map/ppermute | solution.py:35
  143.4 5.7 %collective-permute-start.22 = (f32[64,512]{1,0:T(8,128)S(1)}, f32[64,512]{1,0:T(8,128)S(1)}, u32[]{:S(2)}, u32[]{:S(2)}) collective-permute-start(f32[64,512]{1,0:T(8,128)S(1)} %get-tuple-element.126), channel_id=1, source_target_pairs={{0,2},{1,3},{2,0},{3,1},{4,6},{5,7},{6,4},{7,5},{8,10},{9,11},{10,... | collective-permute-start | bytes 393224 | tf_op jit(solution)/shard_map/ppermute | solution.py:35
  143.4 6.8 %collective-permute-start.21 = (f32[64,512]{1,0:T(8,128)S(1)}, f32[64,512]{1,0:T(8,128)S(1)}, u32[]{:S(2)}, u32[]{:S(2)}) collective-permute-start(f32[64,512]{1,0:T(8,128)S(1)} %get-tuple-element.127), channel_id=1, source_target_pairs={{0,1},{1,2},{2,3},{3,0},{4,5},{5,6},{6,7},{7,4},{8,9},{9,10},{10,1... | collective-permute-start | bytes 393224 | tf_op jit(solution)/shard_map/ppermute | solution.py:35
  154.4 16.7 %collective-permute-start.36 = (f32[16,512]{1,0:T(8,128)}, f32[16,512]{1,0:T(8,128)S(1)}, u32[]{:S(2)}, u32[]{:S(2)}) collective-permute-start(f32[16,512]{1,0:T(8,128)} %get-tuple-element.123), channel_id=1, source_target_pairs={{0,192},{64,0},{128,64},{192,128},{1,193},{65,1},{129,65},{193,129... | collective-permute-start | bytes 98312 | tf_op jit(solution)/shard_map/ppermute | solution.py:371
  165.4 5.7 %collective-permute-start.35 = (f32[16,512]{1,0:T(8,128)}, f32[16,512]{1,0:T(8,128)S(1)}, u32[]{:S(2)}, u32[]{:S(2)}) collective-permute-start(f32[16,512]{1,0:T(8,128)} %get-tuple-element.123), channel_id=1, source_target_pairs={{0,128},{64,192},{128,0},{192,64},{1,129},{65,193},{129,1},{193,65... | collective-permute-start | bytes 98312 | tf_op jit(solution)/shard_map/ppermute | solution.py:371
  167.6 3.5 %collective-permute-start.34 = (f32[16,512]{1,0:T(8,128)}, f32[16,512]{1,0:T(8,128)S(1)}, u32[]{:S(2)}, u32[]{:S(2)}) collective-permute-start(f32[16,512]{1,0:T(8,128)} %get-tuple-element.123), channel_id=1, source_target_pairs={{0,64},{64,128},{128,192},{192,0},{1,65},{65,129},{129,193},{193,1... | collective-permute-start | bytes 98312 | tf_op jit(solution)/shard_map/ppermute | solution.py:371
  (17 other events, 81.9 us)

commit v2 on v1

--- a/solution.py
+++ b/solution.py
@@ -340,19 +340,21 @@
     near_got = []
     for block, axis, step in beside:
         near_got.append(send(block, axis, step))
-    across, _ = lax.optimization_barrier(((near[2], near[6]), (a1, a2, a3, b1, b2, b3)))
     a_got = spread((a1, a2, a3), 1)
     b_got = spread((b1, b2, b3), 2)
-    near_a = [near_got[0], near_got[1], send(across[0], 2, 2)]
-    near_b = [near_got[2], near_got[3], send(across[1], 1, 2)]
     a_own, a_got = lax.optimization_barrier(((kept[0], late[0]), a_got))
     b_own, b_got = lax.optimization_barrier(((kept[2], late[2]), b_got))
     a_sum = a_own[0][0] + a_own[1][0] + a_got[0] + a_got[1] + a_got[2]
     b_sum = b_own[0][0] + b_own[1][0] + b_got[0] + b_got[1] + b_got[2]
-    from_below = send(a_sum[:CELL], 0, 1)
-    far_a = send(a_sum[CELL:], 0, 2)
-    from_above = send(b_sum[:CELL], 0, -1)
-    far_b = send(b_sum[CELL:], 0, 2)
+    depth = []
+    for block, step in ((a_sum[:CELL], 1), (a_sum[CELL:], 2), (b_sum[:CELL], -1), (b_sum[CELL:], 2)):
+        depth.append(send(block, 0, step))
+    from_below, far_a, from_above, far_b = depth
+    across, _ = lax.optimization_barrier(((near[2], near[6]), (a_sum, b_sum)))
+    far_x = send(across[0], 2, 2)
+    far_y = send(across[1], 1, 2)
+    near_a = [near_got[0], near_got[1], far_x]
+    near_b = [near_got[2], near_got[3], far_y]
 
     def ends(own, got, axis):
         parts = [own[i] + got[0][i] + got[1][i] + got[2][i] for i in range(SIDE)]

time: 176 us -> 173 us (0.983)
  waiting for transfers between devices: 46.5 us -> 42 us
  starting transfers between devices: 73.1 us -> 75.3 us
    ppermute x34, waiting for transfers between devices: 46.5 us -> 42 us  [send(): return lax.ppermute(block, 'modes', route(axis, step))]
where the time goes in v2:
time: 173 us; the launch traced here: 172 us
  starting transfers between devices  75.3 us (44%)
  Pallas kernels  42.9 us (25%)
  waiting for transfers between devices  42 us (24%)
  other arithmetic  9.83 us (6%)
  local copies, waits for them, and re-layouts  1.95 us (1%)
    ppermute x34, starting transfers between devices, send(): return lax.ppermute(block, 'modes', route(axis, step))  61.4 us
    ppermute x34, waiting for transfers between devices, send(): return lax.ppermute(block, 'modes', route(axis, step))  42 us
    pallas_call x5, Pallas kernels, partial_sums(): pl.pallas_call(functools.partial(partial_kernel, jobs, len(addends)), gri...  28.9 us
    ppermute x3, starting transfers between devices, per_device(): lax.ppermute(last, 'slab', [(i, (i + k) % 4) for i in range(4)])  13.9 us
    pallas_call x1, Pallas kernels, per_device(): small_call(powers_kernel, split, [VMEM, VMEM], flops=200000000)  3.63 us
    pallas_call x1, Pallas kernels, per_device(): small_call(last_kernel, [whole, ((LATERAL, WIDTH), jnp.float32)], [SMEM]...  3.51 us
    pallas_call x1, Pallas kernels, per_device(): small_call(finish_kernel, [whole], [SMEM, SMEM] + [VMEM] * 8, scratch=[pl...  3.46 us
  transfers between devices with their start and end apart: 37, of which 13 were waited for; matrix products, arithmetic and copies ran while one was open for 6% of the time, Pallas kernels for 18%

profile of v2, /device:TPU:1, one launch (start us, length us, event | category | flops | bytes accessed | tf_op | source)
XLA Modules:
  0.0 172.3 jit_solution(12770904610605081426)
XLA Ops:
  0.0 5.1 %partial_sums.6 = (f32[2,192,512]{2,1,0:T(8,128)}, f32[2,192,512]{2,1,0:T(8,128)}, f32[2,192,512]{2,1,0:T(8,128)}, f32[2,192,512]{2,1,0:T(8,128)}) custom-call(s32[1]{0:T(128)} %bitcast.1.place_ref, s32[4,64]{1,0:T(4,128)} %pattern_ref.9, f32[128,512]{1,0:T(8,128)} %x_ref.8, f32[1,512]{1,0:T(1,128)} %bitcast.87, f32[64,1,512]{2,1,0:T(1,128)} %bitcast.47, ...), custom_call_target="tpu_custom_call" | custom-call | flops 201326592 | bytes 4718592 | tf_op jit(solution)/shard_map/partial_sums/pallas_call | solution.py:107
  5.1 2.1 %collective-permute-start.4 = (f32[2,192,512]{2,1,0:T(8,128)}, f32[2,192,512]{2,1,0:T(8,128)S(1)}, u32[]{:S(2)}, u32[]{:S(2)}) collective-permute-start(f32[2,192,512]{2,1,0:T(8,128)} %get-tuple-element.72), channel_id=1, source_target_pairs={{0,1},{1,2},{2,3},{3,0},{4,5},{5,6},{6,7},{7,4},{8,9},{9,10},{10,1... | collective-permute-start | bytes 2359304 | tf_op jit(solution)/shard_map/ppermute | solution.py:35
  7.2 1.4 collective-permute-start.5
  8.6 1.4 collective-permute-start.6
  10.0 1.4 collective-permute-start.7
  11.4 5.1 %partial_sums.5 = (f32[2,192,512]{2,1,0:T(8,128)}, f32[2,192,512]{2,1,0:T(8,128)}, f32[2,192,512]{2,1,0:T(8,128)}, f32[2,192,512]{2,1,0:T(8,128)}) custom-call(s32[1]{0:T(128)} %bitcast.1.place_ref, s32[4,64]{1,0:T(4,128)} %pattern_ref.9, f32[128,512]{1,0:T(8,128)} %x_ref.8, f32[1,512]{1,0:T(1,128)} %bitcast.88, f32[64,1,512]{2,1,0:T(1,128)} %bitcast.55, ...), custom_call_target="tpu_custom_call" | custom-call | flops 201326592 | bytes 4718592 | tf_op jit(solution)/shard_map/partial_sums/pallas_call | solution.py:107
  16.5 1.4 collective-permute-start
  17.9 6.0 %collective-permute-done.4.refs_16_ = f32[2,192,512]{2,1,0:T(8,128)S(1)} collective-permute-done((f32[2,192,512]{2,1,0:T(8,128)}, f32[2,192,512]{2,1,0:T(8,128)S(1)}, u32[]{:S(2)}, u32[]{:S(2)}) %collective-permute-start.4) | collective-permute-done | bytes 786464 | tf_op jit(solution)/shard_map/ppermute | solution.py:35
  23.9 1.9 %collective-permute-start.1 = (f32[2,192,512]{2,1,0:T(8,128)}, f32[2,192,512]{2,1,0:T(8,128)S(1)}, u32[]{:S(2)}, u32[]{:S(2)}) collective-permute-start(f32[2,192,512]{2,1,0:T(8,128)} %get-tuple-element.66), channel_id=1, source_target_pairs={{0,1},{1,2},{2,3},{3,0},{4,5},{5,6},{6,7},{7,4},{8,9},{9,10},{10,1... | collective-permute-start | bytes 2359304 | tf_op jit(solution)/shard_map/ppermute | solution.py:35
  25.8 3.6 %shard_map.109 = (bf16[4,8,128,128]{3,2,1,0:T(8,128)(2,1)}, bf16[4,8,128,128]{3,2,1,0:T(8,128)(2,1)}) custom-call(f32[1,512]{1,0:T(1,128)} %bitcast.92, f32[4,128,128]{2,1,0:T(8,128)} %inscatter_ref.1), custom_call_target="tpu_custom_call" | custom-call | flops 200000000 | bytes 3145728 | tf_op jit(solution)/shard_map/pallas_call | solution.py:313
  29.4 7.1 %partial_sums.7 = (f32[4,64,512]{2,1,0:T(8,128)}, f32[4,64,512]{2,1,0:T(8,128)}, f32[4,64,512]{2,1,0:T(8,128)}, f32[4,64,512]{2,1,0:T(8,128)}, f32[4,64,512]{2,1...) custom-call(s32[1]{0:T(128)} %bitcast.1.place_ref, s32[4,64]{1,0:T(4,128)} %pattern_ref.9, ...), custom_call_target="tpu_custom_call" | custom-call | flops 268435456 | bytes 6291456 | tf_op jit(solution)/shard_map/partial_sums/pallas_call | solution.py:107
  36.5 3.3 %collective-permute-start.2 = (f32[2,192,512]{2,1,0:T(8,128)}, f32[2,192,512]{2,1,0:T(8,128)S(1)}, u32[]{:S(2)}, u32[]{:S(2)}) collective-permute-start(f32[2,192,512]{2,1,0:T(8,128)} %get-tuple-element.67), channel_id=1, source_target_pairs={{0,12},{1,13},{2,14},{3,15},{4,0},{5,1},{6,2},{7,3},{8,4},{9,5},{1... | collective-permute-start | bytes 2359304 | tf_op jit(solution)/shard_map/ppermute | solution.py:35
  39.8 5.8 %partial_sums.9 = (f32[2,192,512]{2,1,0:T(8,128)}, f32[2,192,512]{2,1,0:T(8,128)}, f32[2,192,512]{2,1,0:T(8,128)}, f32[2,192,512]{2,1,0:T(8,128)}) custom-call(s32[1]{0:T(128)} %bitcast.1.place_ref, s32[4,64]{1,0:T(4,128)} %pattern_ref.9, f32[128,512]{1,0:T(8,128)} %x_ref.8, f32[1,512]{1,0:T(1,128)} %bitcast.90, f32[64,1,512]{2,1,0:T(1,128)} %bitcast.71, ...), custom_call_target="tpu_custom_call" | custom-call | flops 201326592 | bytes 4718592 | tf_op jit(solution)/shard_map/partial_sums/pallas_call | solution.py:107
  46.8 1.9 %collective-permute-start.12 = (f32[2,192,512]{2,1,0:T(8,128)}, f32[2,192,512]{2,1,0:T(8,128)}, u32[]{:S(2)}, u32[]{:S(2)}) collective-permute-start(f32[2,192,512]{2,1,0:T(8,128)} %get-tuple-element.101), channel_id=1, source_target_pairs={{0,3},{1,0},{2,1},{3,2},{4,7},{5,4},{6,5},{7,6},{8,11},{9,8},{10,9... | collective-permute-start | bytes 2359304 | tf_op jit(solution)/shard_map/ppermute | solution.py:35
  49.6 5.9 %collective-permute-done.2.refs_18_ = f32[2,192,512]{2,1,0:T(8,128)S(1)} collective-permute-done((f32[2,192,512]{2,1,0:T(8,128)}, f32[2,192,512]{2,1,0:T(8,128)S(1)}, u32[]{:S(2)}, u32[]{:S(2)}) %collective-permute-start.2) | collective-permute-done | bytes 786464 | tf_op jit(solution)/shard_map/ppermute | solution.py:35
  55.5 3.1 %collective-permute-done.3.refs_19_ = f32[2,192,512]{2,1,0:T(8,128)S(1)} collective-permute-done((f32[2,192,512]{2,1,0:T(8,128)}, f32[2,192,512]{2,1,0:T(8,128)S(1)}, u32[]{:S(2)}, u32[]{:S(2)}) %collective-permute-start.3) | collective-permute-done | bytes 786464 | tf_op jit(solution)/shard_map/ppermute | solution.py:35
  59.6 5.8 %partial_sums.8 = (f32[2,192,512]{2,1,0:T(8,128)}, f32[2,192,512]{2,1,0:T(8,128)}, f32[2,192,512]{2,1,0:T(8,128)}, f32[2,192,512]{2,1,0:T(8,128)}) custom-call(s32[1]{0:T(128)} %bitcast.1.place_ref, s32[4,64]{1,0:T(4,128)} %pattern_ref.9, f32[128,512]{1,0:T(8,128)} %x_ref.8, f32[1,512]{1,0:T(1,128)} %bitcast.91, f32[64,1,512]{2,1,0:T(1,128)} %bitcast.79, ...), custom_call_target="tpu_custom_call" | custom-call | flops 201326592 | bytes 4718592 | tf_op jit(solution)/shard_map/partial_sums/pallas_call | solution.py:107
  65.4 1.3 fusion.5
  67.5 1.5 fusion.3
  68.9 2.1 %collective-permute-start.14 = (f32[192,512]{1,0:T(8,128)S(1)}, f32[192,512]{1,0:T(8,128)S(1)}, u32[]{:S(2)}, u32[]{:S(2)}) collective-permute-start(f32[192,512]{1,0:T(8,128)S(1)} %get-tuple-element.135), channel_id=1, source_target_pairs={{0,12},{1,13},{2,14},{3,15},{4,0},{5,1},{6,2},{7,3},{8,4},{9,5},{1... | collective-permute-start | bytes 1179656 | tf_op jit(solution)/shard_map/ppermute | solution.py:35
  71.2 4.3 %collective-permute-done.15 = f32[2,192,512]{2,1,0:T(8,128)} collective-permute-done((f32[2,192,512]{2,1,0:T(8,128)}, f32[2,192,512]{2,1,0:T(8,128)}, u32[]{:S(2)}, u32[]{:S(2)}) %collective-permute-start.15) | collective-permute-done | bytes 786464 | tf_op jit(solution)/shard_map/ppermute | solution.py:35
  75.5 1.2 fusion.2
  77.5 1.5 fusion
  79.0 2.0 %collective-permute-start.19 = (f32[192,512]{1,0:T(8,128)S(1)}, f32[192,512]{1,0:T(8,128)S(1)}, u32[]{:S(2)}, u32[]{:S(2)}) collective-permute-start(f32[192,512]{1,0:T(8,128)S(1)} %get-tuple-element.133), channel_id=1, source_target_pairs={{0,3},{1,0},{2,1},{3,2},{4,7},{5,4},{6,5},{7,6},{8,11},{9,8},{10,9... | collective-permute-start | bytes 1179656 | tf_op jit(solution)/shard_map/ppermute | solution.py:35
  81.0 4.0 %collective-permute-done.11 = f32[192,512]{1,0:T(8,128)S(1)} collective-permute-done((f32[192,512]{1,0:T(8,128)S(1)}, f32[192,512]{1,0:T(8,128)S(1)}, u32[]{:S(2)}, u32[]{:S(2)}) %collective-permute-start.11) | collective-permute-done | bytes 393248 | tf_op jit(solution)/shard_map/ppermute | solution.py:35
  85.0 1.8 %collective-permute-start.18 = (f32[192,512]{1,0:T(8,128)S(1)}, f32[192,512]{1,0:T(8,128)S(1)}, u32[]{:S(2)}, u32[]{:S(2)}) collective-permute-start(f32[192,512]{1,0:T(8,128)S(1)} %get-tuple-element.134), channel_id=1, source_target_pairs={{0,2},{1,3},{2,0},{3,1},{4,6},{5,7},{6,4},{7,5},{8,10},{9,11},{10,... | collective-permute-start | bytes 1179656 | tf_op jit(solution)/shard_map/ppermute | solution.py:35
  87.8 3.4 %collective-permute-done.13 = f32[192,512]{1,0:T(8,128)S(1)} collective-permute-done((f32[192,512]{1,0:T(8,128)S(1)}, f32[192,512]{1,0:T(8,128)S(1)}, u32[]{:S(2)}, u32[]{:S(2)}) %collective-permute-start.13) | collective-permute-done | bytes 393248 | tf_op jit(solution)/shard_map/ppermute | solution.py:35
  91.1 2.1 %collective-permute-start.9 = (f32[4,64,512]{2,1,0:T(8,128)}, f32[4,64,512]{2,1,0:T(8,128)S(1)}, u32[]{:S(2)}, u32[]{:S(2)}) collective-permute-start(f32[4,64,512]{2,1,0:T(8,128)} %get-tuple-element.87), channel_id=1, source_target_pairs={{0,3},{1,0},{2,1},{3,2},{4,7},{5,4},{6,5},{7,6},{8,11},{9,8},{10,9... | collective-permute-start | bytes 1572872 | tf_op jit(solution)/shard_map/ppermute | solution.py:35
  93.3 2.1 %collective-permute-done.18 = f32[192,512]{1,0:T(8,128)S(1)} collective-permute-done((f32[192,512]{1,0:T(8,128)S(1)}, f32[192,512]{1,0:T(8,128)S(1)}, u32[]{:S(2)}, u32[]{:S(2)}) %collective-permute-start.18) | collective-permute-done | bytes 393248 | tf_op jit(solution)/shard_map/ppermute | solution.py:35
  95.4 1.8 %fusion.7 = (f32[192,512]{1,0:T(8,128)S(1)}, f32[192,512]{1,0:T(8,128)S(1)}) fusion(f32[192,512]{1,0:T(8,128)S(1)} %collective-permute-done.19, f32[192,512]{1,0:T(8,128)S(1)} %collective-permute-done.18, f32[192,512]{1,0:T(8,128)S(1)} %collective-permute-done.16, f32[2,192,512]{2,1,0:T(8,128)} %collective-permute-done.15, ...), kind=kLoop, calls=%fused_computation.14 | loop fusion | flops 786432 | bytes 4718592 | tf_op jit(solution)/shard_map/add | solution.py:348
  97.9 2.7 %collective-permute-start.25 = (f32[4,64,512]{2,1,0:T(8,128)S(1)}, f32[4,64,512]{2,1,0:T(8,128)S(1)}, u32[]{:S(2)}, u32[]{:S(2)}) collective-permute-start(f32[4,64,512]{2,1,0:T(8,128)S(1)} %copy-done.24), channel_id=1, source_target_pairs={{0,12},{1,13},{2,14},{3,15},{4,0},{5,1},{6,2},{7,3},{8,4},{9,5},{1... | collective-permute-start | bytes 1572872 | tf_op jit(solution)/shard_map/ppermute | solution.py:35
  100.5 7.8 %collective-permute-start.26 = (f32[4,64,512]{2,1,0:T(8,128)S(1)}, f32[4,64,512]{2,1,0:T(8,128)S(1)}, u32[]{:S(2)}, u32[]{:S(2)}) collective-permute-start(f32[4,64,512]{2,1,0:T(8,128)S(1)} %copy-done.23), channel_id=1, source_target_pairs={{0,8},{1,9},{2,10},{3,11},{4,12},{5,13},{6,14},{7,15},{8,0},{9,1},... | collective-permute-start | bytes 1572872 | tf_op jit(solution)/shard_map/ppermute | solution.py:35
  108.4 5.1 %collective-permute-done.9 = f32[4,64,512]{2,1,0:T(8,128)S(1)} collective-permute-done((f32[4,64,512]{2,1,0:T(8,128)}, f32[4,64,512]{2,1,0:T(8,128)S(1)}, u32[]{:S(2)}, u32[]{:S(2)}) %collective-permute-start.9) | collective-permute-done | bytes 524320 | tf_op jit(solution)/shard_map/ppermute | solution.py:35
  113.6 3.1 %collective-permute-start.30 = (f32[128,512]{1,0:T(8,128)S(1)}, f32[128,512]{1,0:T(8,128)S(1)}, u32[]{:S(2)}, u32[]{:S(2)}) collective-permute-start(f32[128,512]{1,0:T(8,128)S(1)} %slice.238), channel_id=1, source_target_pairs={{0,16},{1,17},{2,18},{3,19},{4,20},{5,21},{6,22},{7,23},{8,24},{9,... | collective-permute-start | bytes 786440 | tf_op jit(solution)/shard_map/ppermute | solution.py:35
  116.7 3.2 %collective-permute-start.31 = (f32[128,512]{1,0:T(8,128)S(1)}, f32[128,512]{1,0:T(8,128)S(1)}, u32[]{:S(2)}, u32[]{:S(2)}) collective-permute-start(f32[128,512]{1,0:T(8,128)S(1)} %slice.239), channel_id=1, source_target_pairs={{0,48},{1,49},{2,50},{3,51},{4,52},{5,53},{6,54},{7,55},{8,56},{9,... | collective-permute-start | bytes 786440 | tf_op jit(solution)/shard_map/ppermute | solution.py:35
  120.8 4.2 %collective-permute-start.32 = (f32[64,512]{1,0:T(8,128)S(1)}, f32[64,512]{1,0:T(8,128)S(1)}, u32[]{:S(2)}, u32[]{:S(2)}) collective-permute-start(f32[64,512]{1,0:T(8,128)S(1)} %slice.240), channel_id=1, source_target_pairs={{0,32},{1,33},{2,34},{3,35},{4,36},{5,37},{6,38},{7,39},{8,40},{9,... | collective-permute-start | bytes 393224 | tf_op jit(solution)/shard_map/ppermute | solution.py:35
  125.0 1.2 collective-permute-start.33
  127.1 2.8 %collective-permute-done.32.refs_10_ = f32[64,512]{1,0:T(8,128)S(1)} collective-permute-done((f32[64,512]{1,0:T(8,128)S(1)}, f32[64,512]{1,0:T(8,128)S(1)}, u32[]{:S(2)}, u32[]{:S(2)}) %collective-permute-start.32) | collective-permute-done | bytes 131104 | tf_op jit(solution)/shard_map/ppermute | solution.py:35
  129.8 5.9 %collective-permute-start.22 = (f32[64,512]{1,0:T(8,128)S(1)}, f32[64,512]{1,0:T(8,128)S(1)}, u32[]{:S(2)}, u32[]{:S(2)}) collective-permute-start(f32[64,512]{1,0:T(8,128)S(1)} %get-tuple-element.130), channel_id=1, source_target_pairs={{0,8},{1,9},{2,10},{3,11},{4,12},{5,13},{6,14},{7,15},{8,0},{9,1},... | collective-permute-start | bytes 393224 | tf_op jit(solution)/shard_map/ppermute | solution.py:35
  135.7 4.2 %collective-permute-start.21 = (f32[64,512]{1,0:T(8,128)S(1)}, f32[64,512]{1,0:T(8,128)S(1)}, u32[]{:S(2)}, u32[]{:S(2)}) collective-permute-start(f32[64,512]{1,0:T(8,128)S(1)} %get-tuple-element.131), channel_id=1, source_target_pairs={{0,4},{1,5},{2,6},{3,7},{4,8},{5,9},{6,10},{7,11},{8,12},{9,13},{1... | collective-permute-start | bytes 393224 | tf_op jit(solution)/shard_map/ppermute | solution.py:35
  141.9 2.2 %collective-permute-done.29.refs_7_ = f32[64,512]{1,0:T(8,128)S(1)} collective-permute-done((f32[64,512]{1,0:T(8,128)S(1)}, f32[64,512]{1,0:T(8,128)S(1)}, u32[]{:S(2)}, u32[]{:S(2)}) %collective-permute-start.29) | collective-permute-done | bytes 131104 | tf_op jit(solution)/shard_map/ppermute | solution.py:35
  144.1 1.6 collective-permute-done.28.refs_6_
  145.7 1.1 collective-permute-done.27.refs_5_
  147.4 3.5 %shard_map.110 = (f32[128,512]{1,0:T(8,128)}, f32[16,512]{1,0:T(8,128)}) custom-call(s32[4]{0:T(128)} %direction_ref.5, f32[64,512]{1,0:T(8,128)} %get-tuple-element.132.refs_0_, f32[64,512]{1,0:T(8,128)} %copy-done.13, f32[64,512]{1,0:T(8,128)} %copy-done.12, f32[64,512]{1,0:T(8,128)} %copy-done.11, f32[64,512]{1,0:T(8,128)} %get-tuple-element.128.refs_4_, ...), custom_call_target="tpu_custom_call" | custom-call | flops 40000000 | bytes 3145728 | tf_op jit(solution)/shard_map/pallas_call | solution.py:366
  150.9 11.3 %collective-permute-start.36 = (f32[16,512]{1,0:T(8,128)}, f32[16,512]{1,0:T(8,128)S(1)}, u32[]{:S(2)}, u32[]{:S(2)}) collective-permute-start(f32[16,512]{1,0:T(8,128)} %get-tuple-element.123), channel_id=1, source_target_pairs={{0,192},{64,0},{128,64},{192,128},{1,193},{65,1},{129,65},{193,129... | collective-permute-start | bytes 98312 | tf_op jit(solution)/shard_map/ppermute | solution.py:373
  162.2 2.5 %collective-permute-start.35 = (f32[16,512]{1,0:T(8,128)}, f32[16,512]{1,0:T(8,128)S(1)}, u32[]{:S(2)}, u32[]{:S(2)}) collective-permute-start(f32[16,512]{1,0:T(8,128)} %get-tuple-element.123), channel_id=1, source_target_pairs={{0,128},{64,192},{128,0},{192,64},{1,129},{65,193},{129,1},{193,65... | collective-permute-start | bytes 98312 | tf_op jit(solution)/shard_map/ppermute | solution.py:373
  164.8 3.4 %shard_map.111.particular_ref = f32[128,512]{1,0:T(8,128)} custom-call(s32[4]{0:T(128)} %direction_ref.5, f32[128,512]{1,0:T(8,128)} %get-tuple-element.124.source_ref, f32[1,512]{1,0:T(1,128)} %bitcast.93, bf16[4,8,128,128]{3,2,1,0:T(8,128)(2,1)} %get-tuple-element.121.refs_12_.high_ref, bf16[4,8,128,128]{3,2,1,0:T(8,128)(2,1)} %get-tuple-element.122.refs_13_.low_ref), custom_call_target="tpu_custom_call" | custom-call | flops 40000000 | bytes 3145728 | tf_op jit(solution)/shard_map/pallas_call | solution.py:375
  168.9 3.5 %shard_map.112 = f32[128,512]{1,0:T(8,128)} custom-call(s32[4]{0:T(128)} %direction_ref.5, s32[1]{0:T(128)} %bitcast.slab_ref, f32[16,512]{1,0:T(8,128)} %select_reduce_fusion.wall_ref, f32[16,512]{1,0:T(8,128)} %copy-done.19, f32[16,512]{1,0:T(8,128)} %copy-done.18, f32[16,512]{1,0:T(8,128)} %copy-done.17, f32[1,512]{1,0:T(1,128)} %bitcast.94, ...), custom_call_target="tpu_custom_call" | custom-call | flops 60000000 | bytes 3145728 | tf_op jit(solution)/shard_map/pallas_call | solution.py:378
  (107 shorter events, 11.4 us)
Async XLA Ops:
  5.1 18.8 %collective-permute-start.4 = (f32[2,192,512]{2,1,0:T(8,128)}, f32[2,192,512]{2,1,0:T(8,128)S(1)}, u32[]{:S(2)}, u32[]{:S(2)}) collective-permute-start(f32[2,192,512]{2,1,0:T(8,128)} %get-tuple-element.72), channel_id=1, source_target_pairs={{0,1},{1,2},{2,3},{3,0},{4,5},{5,6},{6,7},{7,4},{8,9},{9,10},{10,1... | collective-permute-start | bytes 2359304 | tf_op jit(solution)/shard_map/ppermute | solution.py:35
  7.2 29.3 %collective-permute-start.5 = (f32[2,192,512]{2,1,0:T(8,128)}, f32[2,192,512]{2,1,0:T(8,128)}, u32[]{:S(2)}, u32[]{:S(2)}) collective-permute-start(f32[2,192,512]{2,1,0:T(8,128)} %get-tuple-element.73), channel_id=1, source_target_pairs={{0,3},{1,0},{2,1},{3,2},{4,7},{5,4},{6,5},{7,6},{8,11},{9,8},{10,9... | collective-permute-start | bytes 2359304 | tf_op jit(solution)/shard_map/ppermute | solution.py:35
  8.6 31.2 %collective-permute-start.6 = (f32[2,192,512]{2,1,0:T(8,128)}, f32[2,192,512]{2,1,0:T(8,128)}, u32[]{:S(2)}, u32[]{:S(2)}) collective-permute-start(f32[2,192,512]{2,1,0:T(8,128)} %get-tuple-element.74), channel_id=1, source_target_pairs={{0,4},{1,5},{2,6},{3,7},{4,8},{5,9},{6,10},{7,11},{8,12},{9,13},{1... | collective-permute-start | bytes 2359304 | tf_op jit(solution)/shard_map/ppermute | solution.py:35
  10.0 29.8 %collective-permute-start.7 = (f32[2,192,512]{2,1,0:T(8,128)}, f32[2,192,512]{2,1,0:T(8,128)}, u32[]{:S(2)}, u32[]{:S(2)}) collective-permute-start(f32[2,192,512]{2,1,0:T(8,128)} %get-tuple-element.75), channel_id=1, source_target_pairs={{0,12},{1,13},{2,14},{3,15},{4,0},{5,1},{6,2},{7,3},{8,4},{9,5},{1... | collective-permute-start | bytes 2359304 | tf_op jit(solution)/shard_map/ppermute | solution.py:35
  16.5 30.3 %collective-permute-start = (f32[2,192,512]{2,1,0:T(8,128)}, f32[2,192,512]{2,1,0:T(8,128)S(1)}, u32[]{:S(2)}, u32[]{:S(2)}) collective-permute-start(f32[2,192,512]{2,1,0:T(8,128)} %get-tuple-element.65), channel_id=1, source_target_pairs={{0,3},{1,0},{2,1},{3,2},{4,7},{5,4},{6,5},{7,6},{8,11},{9,8},{10,9... | collective-permute-start | bytes 2359304 | tf_op jit(solution)/shard_map/ppermute | solution.py:35
  23.9 12.6 %copy-start.3 = (f32[2,192,512]{2,1,0:T(8,128)}, f32[2,192,512]{2,1,0:T(8,128)S(1)}, u32[]{:S(2)}) copy-start(f32[2,192,512]{2,1,0:T(8,128)S(1)} %collective-permute-done.4.refs_16_) | copy-start | bytes 2359300
  23.9 24.8 %collective-permute-start.1 = (f32[2,192,512]{2,1,0:T(8,128)}, f32[2,192,512]{2,1,0:T(8,128)S(1)}, u32[]{:S(2)}, u32[]{:S(2)}) collective-permute-start(f32[2,192,512]{2,1,0:T(8,128)} %get-tuple-element.66), channel_id=1, source_target_pairs={{0,1},{1,2},{2,3},{3,0},{4,5},{5,6},{6,7},{7,4},{8,9},{9,10},{10,1... | collective-permute-start | bytes 2359304 | tf_op jit(solution)/shard_map/ppermute | solution.py:35
  36.5 19.0 %collective-permute-start.2 = (f32[2,192,512]{2,1,0:T(8,128)}, f32[2,192,512]{2,1,0:T(8,128)S(1)}, u32[]{:S(2)}, u32[]{:S(2)}) collective-permute-start(f32[2,192,512]{2,1,0:T(8,128)} %get-tuple-element.67), channel_id=1, source_target_pairs={{0,12},{1,13},{2,14},{3,15},{4,0},{5,1},{6,2},{7,3},{8,4},{9,5},{1... | collective-permute-start | bytes 2359304 | tf_op jit(solution)/shard_map/ppermute | solution.py:35
  39.8 18.9 %collective-permute-start.3 = (f32[2,192,512]{2,1,0:T(8,128)}, f32[2,192,512]{2,1,0:T(8,128)S(1)}, u32[]{:S(2)}, u32[]{:S(2)}) collective-permute-start(f32[2,192,512]{2,1,0:T(8,128)} %get-tuple-element.68), channel_id=1, source_target_pairs={{0,4},{1,5},{2,6},{3,7},{4,8},{5,9},{6,10},{7,11},{8,12},{9,13},{1... | collective-permute-start | bytes 2359304 | tf_op jit(solution)/shard_map/ppermute | solution.py:35
  45.7 19.8 %collective-permute-start.10 = (f32[2,192,512]{2,1,0:T(8,128)}, f32[2,192,512]{2,1,0:T(8,128)}, u32[]{:S(2)}, u32[]{:S(2)}) collective-permute-start(f32[2,192,512]{2,1,0:T(8,128)} %get-tuple-element.99), channel_id=1, source_target_pairs={{0,1},{1,2},{2,3},{3,0},{4,5},{5,6},{6,7},{7,4},{8,9},{9,10},{10,1... | collective-permute-start | bytes 2359304 | tf_op jit(solution)/shard_map/ppermute | solution.py:35
  46.8 12.2 %copy-start = (f32[2,192,512]{2,1,0:T(8,128)}, f32[2,192,512]{2,1,0:T(8,128)S(1)}, u32[]{:S(2)}) copy-start(f32[2,192,512]{2,1,0:T(8,128)S(1)} %collective-permute-done.refs_16_) | copy-start | bytes 2359300
  46.8 20.7 %collective-permute-start.12 = (f32[2,192,512]{2,1,0:T(8,128)}, f32[2,192,512]{2,1,0:T(8,128)}, u32[]{:S(2)}, u32[]{:S(2)}) collective-permute-start(f32[2,192,512]{2,1,0:T(8,128)} %get-tuple-element.101), channel_id=1, source_target_pairs={{0,3},{1,0},{2,1},{3,2},{4,7},{5,4},{6,5},{7,6},{8,11},{9,8},{10,9... | collective-permute-start | bytes 2359304 | tf_op jit(solution)/shard_map/ppermute | solution.py:35
  48.7 10.3 %copy-start.1 = (f32[2,192,512]{2,1,0:T(8,128)}, f32[2,192,512]{2,1,0:T(8,128)S(1)}, u32[]{:S(2)}) copy-start(f32[2,192,512]{2,1,0:T(8,128)S(1)} %collective-permute-done.1.refs_17_) | copy-start | bytes 2359300
  48.7 26.8 %collective-permute-start.15 = (f32[2,192,512]{2,1,0:T(8,128)}, f32[2,192,512]{2,1,0:T(8,128)}, u32[]{:S(2)}, u32[]{:S(2)}) collective-permute-start(f32[2,192,512]{2,1,0:T(8,128)} %get-tuple-element.108), channel_id=1, source_target_pairs={{0,4},{1,5},{2,6},{3,7},{4,8},{5,9},{6,10},{7,11},{8,12},{9,13},{1... | collective-permute-start | bytes 2359304 | tf_op jit(solution)/shard_map/ppermute | solution.py:35
  58.7 18.8 %collective-permute-start.17 = (f32[2,192,512]{2,1,0:T(8,128)}, f32[2,192,512]{2,1,0:T(8,128)}, u32[]{:S(2)}, u32[]{:S(2)}) collective-permute-start(f32[2,192,512]{2,1,0:T(8,128)} %get-tuple-element.110), channel_id=1, source_target_pairs={{0,12},{1,13},{2,14},{3,15},{4,0},{5,1},{6,2},{7,3},{8,4},{9,5},{1... | collective-permute-start | bytes 2359304 | tf_op jit(solution)/shard_map/ppermute | solution.py:35
  65.4 31.8 %copy-start.26 = (f32[4,64,512]{2,1,0:T(8,128)S(1)}, f32[4,64,512]{2,1,0:T(8,128)}, u32[]{:S(2)}) copy-start(f32[4,64,512]{2,1,0:T(8,128)} %get-tuple-element.116) | copy-start | bytes 1572868
  65.4 32.5 %copy-start.25 = (f32[4,64,512]{2,1,0:T(8,128)S(1)}, f32[4,64,512]{2,1,0:T(8,128)}, u32[]{:S(2)}) copy-start(f32[4,64,512]{2,1,0:T(8,128)} %get-tuple-element.118) | copy-start | bytes 1572868
  65.4 32.5 %copy-start.24 = (f32[4,64,512]{2,1,0:T(8,128)S(1)}, f32[4,64,512]{2,1,0:T(8,128)}, u32[]{:S(2)}) copy-start(f32[4,64,512]{2,1,0:T(8,128)} %get-tuple-element.119) | copy-start | bytes 1572868
  65.4 35.2 %copy-start.23 = (f32[4,64,512]{2,1,0:T(8,128)S(1)}, f32[4,64,512]{2,1,0:T(8,128)}, u32[]{:S(2)}) copy-start(f32[4,64,512]{2,1,0:T(8,128)} %get-tuple-element.120) | copy-start | bytes 1572868
  65.4 54.5 %copy-start.6 = (f32[4,64,512]{2,1,0:T(8,128)S(1)}, f32[4,64,512]{2,1,0:T(8,128)}, u32[]{:S(2)}) copy-start(f32[4,64,512]{2,1,0:T(8,128)} %get-tuple-element.85) | copy-start | bytes 1572868
  65.4 60.8 %copy-start.5 = (f32[4,64,512]{2,1,0:T(8,128)S(1)}, f32[4,64,512]{2,1,0:T(8,128)}, u32[]{:S(2)}) copy-start(f32[4,64,512]{2,1,0:T(8,128)} %get-tuple-element.117) | copy-start | bytes 1572868
  66.7 18.3 %collective-permute-start.11 = (f32[192,512]{1,0:T(8,128)S(1)}, f32[192,512]{1,0:T(8,128)S(1)}, u32[]{:S(2)}, u32[]{:S(2)}) collective-permute-start(f32[192,512]{1,0:T(8,128)S(1)} %fusion.5), channel_id=1, source_target_pairs={{0,4},{1,5},{2,6},{3,7},{4,8},{5,9},{6,10},{7,11},{8,12},{9,13},{1... | collective-permute-start | bytes 1179656 | tf_op jit(solution)/shard_map/ppermute | solution.py:35
  68.9 17.8 %collective-permute-start.14 = (f32[192,512]{1,0:T(8,128)S(1)}, f32[192,512]{1,0:T(8,128)S(1)}, u32[]{:S(2)}, u32[]{:S(2)}) collective-permute-start(f32[192,512]{1,0:T(8,128)S(1)} %get-tuple-element.135), channel_id=1, source_target_pairs={{0,12},{1,13},{2,14},{3,15},{4,0},{5,1},{6,2},{7,3},{8,4},{9,5},{1... | collective-permute-start | bytes 1179656 | tf_op jit(solution)/shard_map/ppermute | solution.py:35
  71.1 20.1 %collective-permute-start.13 = (f32[192,512]{1,0:T(8,128)S(1)}, f32[192,512]{1,0:T(8,128)S(1)}, u32[]{:S(2)}, u32[]{:S(2)}) collective-permute-start(f32[192,512]{1,0:T(8,128)S(1)} %get-tuple-element.136), channel_id=1, source_target_pairs={{0,8},{1,9},{2,10},{3,11},{4,12},{5,13},{6,14},{7,15},{8,0},{9,1},... | collective-permute-start | bytes 1179656 | tf_op jit(solution)/shard_map/ppermute | solution.py:35
  76.7 16.6 %collective-permute-start.16 = (f32[192,512]{1,0:T(8,128)S(1)}, f32[192,512]{1,0:T(8,128)S(1)}, u32[]{:S(2)}, u32[]{:S(2)}) collective-permute-start(f32[192,512]{1,0:T(8,128)S(1)} %fusion.2), channel_id=1, source_target_pairs={{0,1},{1,2},{2,3},{3,0},{4,5},{5,6},{6,7},{7,4},{8,9},{9,10},{10,1... | collective-permute-start | bytes 1179656 | tf_op jit(solution)/shard_map/ppermute | solution.py:35
  79.0 14.3 %collective-permute-start.19 = (f32[192,512]{1,0:T(8,128)S(1)}, f32[192,512]{1,0:T(8,128)S(1)}, u32[]{:S(2)}, u32[]{:S(2)}) collective-permute-start(f32[192,512]{1,0:T(8,128)S(1)} %get-tuple-element.133), channel_id=1, source_target_pairs={{0,3},{1,0},{2,1},{3,2},{4,7},{5,4},{6,5},{7,6},{8,11},{9,8},{10,9... | collective-permute-start | bytes 1179656 | tf_op jit(solution)/shard_map/ppermute | solution.py:35
  85.0 10.3 %collective-permute-start.18 = (f32[192,512]{1,0:T(8,128)S(1)}, f32[192,512]{1,0:T(8,128)S(1)}, u32[]{:S(2)}, u32[]{:S(2)}) collective-permute-start(f32[192,512]{1,0:T(8,128)S(1)} %get-tuple-element.134), channel_id=1, source_target_pairs={{0,2},{1,3},{2,0},{3,1},{4,6},{5,7},{6,4},{7,5},{8,10},{9,11},{10,... | collective-permute-start | bytes 1179656 | tf_op jit(solution)/shard_map/ppermute | solution.py:35
  86.8 13.7 %collective-permute-start.8 = (f32[4,64,512]{2,1,0:T(8,128)}, f32[4,64,512]{2,1,0:T(8,128)S(1)}, u32[]{:S(2)}, u32[]{:S(2)}) collective-permute-start(f32[4,64,512]{2,1,0:T(8,128)} %get-tuple-element.86), channel_id=1, source_target_pairs={{0,1},{1,2},{2,3},{3,0},{4,5},{5,6},{6,7},{7,4},{8,9},{9,10},{10,1... | collective-permute-start | bytes 1572872 | tf_op jit(solution)/shard_map/ppermute | solution.py:35
  91.1 22.4 %collective-permute-start.9 = (f32[4,64,512]{2,1,0:T(8,128)}, f32[4,64,512]{2,1,0:T(8,128)S(1)}, u32[]{:S(2)}, u32[]{:S(2)}) collective-permute-start(f32[4,64,512]{2,1,0:T(8,128)} %get-tuple-element.87), channel_id=1, source_target_pairs={{0,3},{1,0},{2,1},{3,2},{4,7},{5,4},{6,5},{7,6},{8,11},{9,8},{10,9... | collective-permute-start | bytes 1572872 | tf_op jit(solution)/shard_map/ppermute | solution.py:35
  97.2 19.5 %collective-permute-start.20 = (f32[4,64,512]{2,1,0:T(8,128)S(1)}, f32[4,64,512]{2,1,0:T(8,128)S(1)}, u32[]{:S(2)}, u32[]{:S(2)}) collective-permute-start(f32[4,64,512]{2,1,0:T(8,128)S(1)} %copy-done.26), channel_id=1, source_target_pairs={{0,2},{1,3},{2,0},{3,1},{4,6},{5,7},{6,4},{7,5},{8,10},{9,11},{10,... | collective-permute-start | bytes 1572872 | tf_op jit(solution)/shard_map/ppermute | solution.py:35
  97.9 22.9 %collective-permute-start.24 = (f32[4,64,512]{2,1,0:T(8,128)S(1)}, f32[4,64,512]{2,1,0:T(8,128)S(1)}, u32[]{:S(2)}, u32[]{:S(2)}) collective-permute-start(f32[4,64,512]{2,1,0:T(8,128)S(1)} %copy-done.25), channel_id=1, source_target_pairs={{0,4},{1,5},{2,6},{3,7},{4,8},{5,9},{6,10},{7,11},{8,12},{9,13},{1... | collective-permute-start | bytes 1572872 | tf_op jit(solution)/shard_map/ppermute | solution.py:35
  97.9 27.1 %collective-permute-start.25 = (f32[4,64,512]{2,1,0:T(8,128)S(1)}, f32[4,64,512]{2,1,0:T(8,128)S(1)}, u32[]{:S(2)}, u32[]{:S(2)}) collective-permute-start(f32[4,64,512]{2,1,0:T(8,128)S(1)} %copy-done.24), channel_id=1, source_target_pairs={{0,12},{1,13},{2,14},{3,15},{4,0},{5,1},{6,2},{7,3},{8,4},{9,5},{1... | collective-permute-start | bytes 1572872 | tf_op jit(solution)/shard_map/ppermute | solution.py:35
  100.5 25.6 %collective-permute-start.26 = (f32[4,64,512]{2,1,0:T(8,128)S(1)}, f32[4,64,512]{2,1,0:T(8,128)S(1)}, u32[]{:S(2)}, u32[]{:S(2)}) collective-permute-start(f32[4,64,512]{2,1,0:T(8,128)S(1)} %copy-done.23), channel_id=1, source_target_pairs={{0,8},{1,9},{2,10},{3,11},{4,12},{5,13},{6,14},{7,15},{8,0},{9,1},... | collective-permute-start | bytes 1572872 | tf_op jit(solution)/shard_map/ppermute | solution.py:35
  113.6 26.4 %collective-permute-start.30 = (f32[128,512]{1,0:T(8,128)S(1)}, f32[128,512]{1,0:T(8,128)S(1)}, u32[]{:S(2)}, u32[]{:S(2)}) collective-permute-start(f32[128,512]{1,0:T(8,128)S(1)} %slice.238), channel_id=1, source_target_pairs={{0,16},{1,17},{2,18},{3,19},{4,20},{5,21},{6,22},{7,23},{8,24},{9,... | collective-permute-start | bytes 786440 | tf_op jit(solution)/shard_map/ppermute | solution.py:35
  116.7 23.3 %collective-permute-start.31 = (f32[128,512]{1,0:T(8,128)S(1)}, f32[128,512]{1,0:T(8,128)S(1)}, u32[]{:S(2)}, u32[]{:S(2)}) collective-permute-start(f32[128,512]{1,0:T(8,128)S(1)} %slice.239), channel_id=1, source_target_pairs={{0,48},{1,49},{2,50},{3,51},{4,52},{5,53},{6,54},{7,55},{8,56},{9,... | collective-permute-start | bytes 786440 | tf_op jit(solution)/shard_map/ppermute | solution.py:35
  120.8 9.0 %collective-permute-start.32 = (f32[64,512]{1,0:T(8,128)S(1)}, f32[64,512]{1,0:T(8,128)S(1)}, u32[]{:S(2)}, u32[]{:S(2)}) collective-permute-start(f32[64,512]{1,0:T(8,128)S(1)} %slice.240), channel_id=1, source_target_pairs={{0,32},{1,33},{2,34},{3,35},{4,36},{5,37},{6,38},{7,39},{8,40},{9,... | collective-permute-start | bytes 393224 | tf_op jit(solution)/shard_map/ppermute | solution.py:35
  125.0 10.7 %collective-permute-start.33 = (f32[64,512]{1,0:T(8,128)S(1)}, f32[64,512]{1,0:T(8,128)S(1)}, u32[]{:S(2)}, u32[]{:S(2)}) collective-permute-start(f32[64,512]{1,0:T(8,128)S(1)} %slice.241), channel_id=1, source_target_pairs={{0,32},{1,33},{2,34},{3,35},{4,36},{5,37},{6,38},{7,39},{8,40},{9,... | collective-permute-start | bytes 393224 | tf_op jit(solution)/shard_map/ppermute | solution.py:35
  126.2 14.3 %collective-permute-start.23 = (f32[64,512]{1,0:T(8,128)S(1)}, f32[64,512]{1,0:T(8,128)S(1)}, u32[]{:S(2)}, u32[]{:S(2)}) collective-permute-start(f32[64,512]{1,0:T(8,128)S(1)} %get-tuple-element.129), channel_id=1, source_target_pairs={{0,12},{1,13},{2,14},{3,15},{4,0},{5,1},{6,2},{7,3},{8,4},{9,5},{1... | collective-permute-start | bytes 393224 | tf_op jit(solution)/shard_map/ppermute | solution.py:35
  129.8 17.0 %copy-start.9 = (f32[64,512]{1,0:T(8,128)}, f32[64,512]{1,0:T(8,128)S(1)}, u32[]{:S(2)}) copy-start(f32[64,512]{1,0:T(8,128)S(1)} %collective-permute-done.32.refs_10_) | copy-start | bytes 393220
  129.8 11.7 %collective-permute-start.22 = (f32[64,512]{1,0:T(8,128)S(1)}, f32[64,512]{1,0:T(8,128)S(1)}, u32[]{:S(2)}, u32[]{:S(2)}) collective-permute-start(f32[64,512]{1,0:T(8,128)S(1)} %get-tuple-element.130), channel_id=1, source_target_pairs={{0,8},{1,9},{2,10},{3,11},{4,12},{5,13},{6,14},{7,15},{8,0},{9,1},... | collective-permute-start | bytes 393224 | tf_op jit(solution)/shard_map/ppermute | solution.py:35
  135.7 11.1 %copy-start.10 = (f32[64,512]{1,0:T(8,128)}, f32[64,512]{1,0:T(8,128)S(1)}, u32[]{:S(2)}) copy-start(f32[64,512]{1,0:T(8,128)S(1)} %collective-permute-done.33.refs_11_) | copy-start | bytes 393220
  135.7 6.2 %collective-permute-start.21 = (f32[64,512]{1,0:T(8,128)S(1)}, f32[64,512]{1,0:T(8,128)S(1)}, u32[]{:S(2)}, u32[]{:S(2)}) collective-permute-start(f32[64,512]{1,0:T(8,128)S(1)} %get-tuple-element.131), channel_id=1, source_target_pairs={{0,4},{1,5},{2,6},{3,7},{4,8},{5,9},{6,10},{7,11},{8,12},{9,13},{1... | collective-permute-start | bytes 393224 | tf_op jit(solution)/shard_map/ppermute | solution.py:35
  139.9 4.1 %collective-permute-start.29 = (f32[64,512]{1,0:T(8,128)S(1)}, f32[64,512]{1,0:T(8,128)S(1)}, u32[]{:S(2)}, u32[]{:S(2)}) collective-permute-start(f32[64,512]{1,0:T(8,128)S(1)} %get-tuple-element.125), channel_id=1, source_target_pairs={{0,3},{1,0},{2,1},{3,2},{4,7},{5,4},{6,5},{7,6},{8,11},{9,8},{10,9... | collective-permute-start | bytes 393224 | tf_op jit(solution)/shard_map/ppermute | solution.py:35
  140.0 5.7 %collective-permute-start.28 = (f32[64,512]{1,0:T(8,128)S(1)}, f32[64,512]{1,0:T(8,128)S(1)}, u32[]{:S(2)}, u32[]{:S(2)}) collective-permute-start(f32[64,512]{1,0:T(8,128)S(1)} %get-tuple-element.126), channel_id=1, source_target_pairs={{0,2},{1,3},{2,0},{3,1},{4,6},{5,7},{6,4},{7,5},{8,10},{9,11},{10,... | collective-permute-start | bytes 393224 | tf_op jit(solution)/shard_map/ppermute | solution.py:35
  140.4 6.3 %collective-permute-start.27 = (f32[64,512]{1,0:T(8,128)S(1)}, f32[64,512]{1,0:T(8,128)S(1)}, u32[]{:S(2)}, u32[]{:S(2)}) collective-permute-start(f32[64,512]{1,0:T(8,128)S(1)} %get-tuple-element.127), channel_id=1, source_target_pairs={{0,1},{1,2},{2,3},{3,0},{4,5},{5,6},{6,7},{7,4},{8,9},{9,10},{10,1... | collective-permute-start | bytes 393224 | tf_op jit(solution)/shard_map/ppermute | solution.py:35
  150.9 17.3 %collective-permute-start.36 = (f32[16,512]{1,0:T(8,128)}, f32[16,512]{1,0:T(8,128)S(1)}, u32[]{:S(2)}, u32[]{:S(2)}) collective-permute-start(f32[16,512]{1,0:T(8,128)} %get-tuple-element.123), channel_id=1, source_target_pairs={{0,192},{64,0},{128,64},{192,128},{1,193},{65,1},{129,65},{193,129... | collective-permute-start | bytes 98312 | tf_op jit(solution)/shard_map/ppermute | solution.py:373
  162.2 6.0 %collective-permute-start.35 = (f32[16,512]{1,0:T(8,128)}, f32[16,512]{1,0:T(8,128)S(1)}, u32[]{:S(2)}, u32[]{:S(2)}) collective-permute-start(f32[16,512]{1,0:T(8,128)} %get-tuple-element.123), channel_id=1, source_target_pairs={{0,128},{64,192},{128,0},{192,64},{1,129},{65,193},{129,1},{193,65... | collective-permute-start | bytes 98312 | tf_op jit(solution)/shard_map/ppermute | solution.py:373
  164.8 3.5 %collective-permute-start.34 = (f32[16,512]{1,0:T(8,128)}, f32[16,512]{1,0:T(8,128)S(1)}, u32[]{:S(2)}, u32[]{:S(2)}) collective-permute-start(f32[16,512]{1,0:T(8,128)} %get-tuple-element.123), channel_id=1, source_target_pairs={{0,64},{64,128},{128,192},{192,0},{1,65},{65,129},{129,193},{193,1... | collective-permute-start | bytes 98312 | tf_op jit(solution)/shard_map/ppermute | solution.py:373
  (17 other events, 75.1 us)

commit v3 on v2

--- a/solution.py
+++ b/solution.py
@@ -340,27 +340,30 @@
     near_got = []
     for block, axis, step in beside:
         near_got.append(send(block, axis, step))
-    a_got = spread((a1, a2, a3), 1)
-    b_got = spread((b1, b2, b3), 2)
+    crossed = []
+    for block, axis, step in ((a1, 1, 1), (a2, 1, 2), (a3, 1, -1), (b1, 2, 1), (b2, 2, 2), (b3, 2, -1)):
+        crossed.append(send(block, axis, step))
+    a_got, b_got = crossed[:3], crossed[3:]
+    ready_a = near[0] + near_got[0] + near_got[1]
+    ready_b = near[4] + near_got[2] + near_got[3]
+    ready_a, ready_b = lax.optimization_barrier((ready_a, ready_b))
+    across, _ = lax.optimization_barrier(((near[2], near[6]), (a_got, b_got)))
+    far_x = send(across[0], 2, 2)
+    far_y = send(across[1], 1, 2)
     a_own, a_got = lax.optimization_barrier(((kept[0], late[0]), a_got))
     b_own, b_got = lax.optimization_barrier(((kept[2], late[2]), b_got))
     a_sum = a_own[0][0] + a_own[1][0] + a_got[0] + a_got[1] + a_got[2]
     b_sum = b_own[0][0] + b_own[1][0] + b_got[0] + b_got[1] + b_got[2]
     depth = []
-    for block, step in ((a_sum[:CELL], 1), (a_sum[CELL:], 2), (b_sum[:CELL], -1), (b_sum[CELL:], 2)):
+    for block, step in ((a_sum[:CELL], 1), (b_sum[:CELL], -1), (a_sum[CELL:], 2), (b_sum[CELL:], 2)):
         depth.append(send(block, 0, step))
-    from_below, far_a, from_above, far_b = depth
-    across, _ = lax.optimization_barrier(((near[2], near[6]), (a_sum, b_sum)))
-    far_x = send(across[0], 2, 2)
-    far_y = send(across[1], 1, 2)
-    near_a = [near_got[0], near_got[1], far_x]
-    near_b = [near_got[2], near_got[3], far_y]
-
-    def ends(own, got, axis):
-        parts = [own[i] + got[0][i] + got[1][i] + got[2][i] for i in range(SIDE)]
+    from_below, from_above, far_a, far_b = depth
+
+    def ends(ready, got, axis):
+        parts = [ready[i] + got[i] for i in range(SIDE)]
         return [parts[0]] + spread(parts[1:], axis)
 
-    halves = ends(near[0], near_a, 1) + ends(near[4], near_b, 2)
+    halves = ends(ready_a, far_x, 1) + ends(ready_b, far_y, 2)
 
     whole = ((CELL, WIDTH), jnp.float32)
     source, last = small_call(

time: 173 us -> 171 us (0.988)
  starting transfers between devices: 75.3 us -> 70.9 us
    ppermute x34, starting transfers between devices: 61.4 us -> 53.4 us  [send(): return lax.ppermute(block, 'modes', route(axis, step))]
    ppermute x3, starting transfers between devices: 13.9 us -> 17.6 us  [per_device(): lax.ppermute(last, 'slab', [(i, (i + k) % 4) for i in range(4)])]
    add x2 -> x5, other arithmetic: 1.75 us -> 4.14 us  [the longest x2 1.44 us: ends(): parts = [ready[i] + got[i] for i in range(SIDE)]]
  transfers between devices with their start and end apart: 37 -> 37, of which waited for: 13 -> 12; matrix products, arithmetic and copies ran while one was open for 6% -> 7% of each run, Pallas kernels for 18% -> 18%
where the time goes in v3:
time: 171 us; the launch traced here: 170 us
  starting transfers between devices  70.9 us (41%)
  Pallas kernels  42.9 us (25%)
  waiting for transfers between devices  42.4 us (25%)
  other arithmetic  11.4 us (7%)
  local copies, waits for them, and re-layouts  2.32 us (1%)
    ppermute x34, starting transfers between devices, send(): return lax.ppermute(block, 'modes', route(axis, step))  53.4 us
    ppermute x34, waiting for transfers between devices, send(): return lax.ppermute(block, 'modes', route(axis, step))  42.4 us
    pallas_call x5, Pallas kernels, partial_sums(): pl.pallas_call(functools.partial(partial_kernel, jobs, len(addends)), gri...  28.9 us
    ppermute x3, starting transfers between devices, per_device(): lax.ppermute(last, 'slab', [(i, (i + k) % 4) for i in range(4)])  17.6 us
    pallas_call x1, Pallas kernels, per_device(): small_call(powers_kernel, split, [VMEM, VMEM], flops=200000000)  3.63 us
    pallas_call x1, Pallas kernels, per_device(): small_call(last_kernel, [whole, ((LATERAL, WIDTH), jnp.float32)], [SMEM]...  3.5 us
    pallas_call x1, Pallas kernels, per_device(): small_call(finish_kernel, [whole], [SMEM, SMEM] + [VMEM] * 8, scratch=[pl...  3.46 us
  transfers between devices with their start and end apart: 37, of which 12 were waited for; matrix products, arithmetic and copies ran while one was open for 7% of the time, Pallas kernels for 18%

profile of v3, /device:TPU:1, one launch (start us, length us, event | category | flops | bytes accessed | tf_op | source)
XLA Modules:
  0.0 170.3 jit_solution(845883594408695851)
XLA Ops:
  0.0 5.1 %partial_sums.6 = (f32[2,192,512]{2,1,0:T(8,128)}, f32[2,192,512]{2,1,0:T(8,128)}, f32[2,192,512]{2,1,0:T(8,128)}, f32[2,192,512]{2,1,0:T(8,128)}) custom-call(s32[1]{0:T(128)} %bitcast.1.place_ref, s32[4,64]{1,0:T(4,128)} %pattern_ref.9, f32[128,512]{1,0:T(8,128)} %x_ref.8, f32[1,512]{1,0:T(1,128)} %bitcast.87, f32[64,1,512]{2,1,0:T(1,128)} %bitcast.47, ...), custom_call_target="tpu_custom_call" | custom-call | flops 201326592 | bytes 4718592 | tf_op jit(solution)/shard_map/partial_sums/pallas_call | solution.py:107
  5.1 2.1 %collective-permute-start.4 = (f32[2,192,512]{2,1,0:T(8,128)}, f32[2,192,512]{2,1,0:T(8,128)S(1)}, u32[]{:S(2)}, u32[]{:S(2)}) collective-permute-start(f32[2,192,512]{2,1,0:T(8,128)} %get-tuple-element.74), channel_id=1, source_target_pairs={{0,1},{1,2},{2,3},{3,0},{4,5},{5,6},{6,7},{7,4},{8,9},{9,10},{10,1... | collective-permute-start | bytes 2359304 | tf_op jit(solution)/shard_map/ppermute | solution.py:35
  7.2 1.4 collective-permute-start.5
  8.6 1.4 collective-permute-start.6
  10.0 1.4 collective-permute-start.7
  11.4 5.0 %partial_sums.5 = (f32[2,192,512]{2,1,0:T(8,128)}, f32[2,192,512]{2,1,0:T(8,128)}, f32[2,192,512]{2,1,0:T(8,128)}, f32[2,192,512]{2,1,0:T(8,128)}) custom-call(s32[1]{0:T(128)} %bitcast.1.place_ref, s32[4,64]{1,0:T(4,128)} %pattern_ref.9, f32[128,512]{1,0:T(8,128)} %x_ref.8, f32[1,512]{1,0:T(1,128)} %bitcast.88, f32[64,1,512]{2,1,0:T(1,128)} %bitcast.55, ...), custom_call_target="tpu_custom_call" | custom-call | flops 201326592 | bytes 4718592 | tf_op jit(solution)/shard_map/partial_sums/pallas_call | solution.py:107
  16.4 1.4 collective-permute-start
  17.8 6.0 %collective-permute-done.4.refs_16_ = f32[2,192,512]{2,1,0:T(8,128)S(1)} collective-permute-done((f32[2,192,512]{2,1,0:T(8,128)}, f32[2,192,512]{2,1,0:T(8,128)S(1)}, u32[]{:S(2)}, u32[]{:S(2)}) %collective-permute-start.4) | collective-permute-done | bytes 786464 | tf_op jit(solution)/shard_map/ppermute | solution.py:35
  23.9 1.9 %collective-permute-start.1 = (f32[2,192,512]{2,1,0:T(8,128)}, f32[2,192,512]{2,1,0:T(8,128)S(1)}, u32[]{:S(2)}, u32[]{:S(2)}) collective-permute-start(f32[2,192,512]{2,1,0:T(8,128)} %get-tuple-element.68), channel_id=1, source_target_pairs={{0,1},{1,2},{2,3},{3,0},{4,5},{5,6},{6,7},{7,4},{8,9},{9,10},{10,1... | collective-permute-start | bytes 2359304 | tf_op jit(solution)/shard_map/ppermute | solution.py:35
  26.6 3.0 %collective-permute-start.2 = (f32[2,192,512]{2,1,0:T(8,128)}, f32[2,192,512]{2,1,0:T(8,128)S(1)}, u32[]{:S(2)}, u32[]{:S(2)}) collective-permute-start(f32[2,192,512]{2,1,0:T(8,128)} %get-tuple-element.69), channel_id=1, source_target_pairs={{0,12},{1,13},{2,14},{3,15},{4,0},{5,1},{6,2},{7,3},{8,4},{9,5},{1... | collective-permute-start | bytes 2359304 | tf_op jit(solution)/shard_map/ppermute | solution.py:35
  29.6 3.6 %shard_map.109 = (bf16[4,8,128,128]{3,2,1,0:T(8,128)(2,1)}, bf16[4,8,128,128]{3,2,1,0:T(8,128)(2,1)}) custom-call(f32[1,512]{1,0:T(1,128)} %bitcast.92, f32[4,128,128]{2,1,0:T(8,128)} %inscatter_ref.1), custom_call_target="tpu_custom_call" | custom-call | flops 200000000 | bytes 3145728 | tf_op jit(solution)/shard_map/pallas_call | solution.py:313
  33.3 7.1 %partial_sums.7 = (f32[4,64,512]{2,1,0:T(8,128)}, f32[4,64,512]{2,1,0:T(8,128)}, f32[4,64,512]{2,1,0:T(8,128)}, f32[4,64,512]{2,1,0:T(8,128)}, f32[4,64,512]{2,1...) custom-call(s32[1]{0:T(128)} %bitcast.1.place_ref, s32[4,64]{1,0:T(4,128)} %pattern_ref.9, ...), custom_call_target="tpu_custom_call" | custom-call | flops 268435456 | bytes 6291456 | tf_op jit(solution)/shard_map/partial_sums/pallas_call | solution.py:107
  40.5 5.8 %partial_sums.9 = (f32[2,192,512]{2,1,0:T(8,128)}, f32[2,192,512]{2,1,0:T(8,128)}, f32[2,192,512]{2,1,0:T(8,128)}, f32[2,192,512]{2,1,0:T(8,128)}) custom-call(s32[1]{0:T(128)} %bitcast.1.place_ref, s32[4,64]{1,0:T(4,128)} %pattern_ref.9, f32[128,512]{1,0:T(8,128)} %x_ref.8, f32[1,512]{1,0:T(1,128)} %bitcast.90, f32[64,1,512]{2,1,0:T(1,128)} %bitcast.71, ...), custom_call_target="tpu_custom_call" | custom-call | flops 201326592 | bytes 4718592 | tf_op jit(solution)/shard_map/partial_sums/pallas_call | solution.py:107
  46.4 2.7 %collective-permute-start.14 = (f32[2,192,512]{2,1,0:T(8,128)}, f32[2,192,512]{2,1,0:T(8,128)}, u32[]{:S(2)}, u32[]{:S(2)}) collective-permute-start(f32[2,192,512]{2,1,0:T(8,128)} %get-tuple-element.107), channel_id=1, source_target_pairs={{0,3},{1,0},{2,1},{3,2},{4,7},{5,4},{6,5},{7,6},{8,11},{9,8},{10,9... | collective-permute-start | bytes 2359304 | tf_op jit(solution)/shard_map/ppermute | solution.py:35
  49.5 2.8 %collective-permute-start.19 = (f32[2,192,512]{2,1,0:T(8,128)}, f32[2,192,512]{2,1,0:T(8,128)}, u32[]{:S(2)}, u32[]{:S(2)}) collective-permute-start(f32[2,192,512]{2,1,0:T(8,128)} %get-tuple-element.111), channel_id=1, source_target_pairs={{0,12},{1,13},{2,14},{3,15},{4,0},{5,1},{6,2},{7,3},{8,4},{9,5},{1... | collective-permute-start | bytes 2359304 | tf_op jit(solution)/shard_map/ppermute | solution.py:35
  53.0 4.9 %collective-permute-done.3.refs_19_ = f32[2,192,512]{2,1,0:T(8,128)S(1)} collective-permute-done((f32[2,192,512]{2,1,0:T(8,128)}, f32[2,192,512]{2,1,0:T(8,128)S(1)}, u32[]{:S(2)}, u32[]{:S(2)}) %collective-permute-start.3) | collective-permute-done | bytes 786464 | tf_op jit(solution)/shard_map/ppermute | solution.py:35
  59.1 5.8 %partial_sums.8 = (f32[2,192,512]{2,1,0:T(8,128)}, f32[2,192,512]{2,1,0:T(8,128)}, f32[2,192,512]{2,1,0:T(8,128)}, f32[2,192,512]{2,1,0:T(8,128)}) custom-call(s32[1]{0:T(128)} %bitcast.1.place_ref, s32[4,64]{1,0:T(4,128)} %pattern_ref.9, f32[128,512]{1,0:T(8,128)} %x_ref.8, f32[1,512]{1,0:T(1,128)} %bitcast.91, f32[64,1,512]{2,1,0:T(1,128)} %bitcast.79, ...), custom_call_target="tpu_custom_call" | custom-call | flops 201326592 | bytes 4718592 | tf_op jit(solution)/shard_map/partial_sums/pallas_call | solution.py:107
  64.9 2.5 %collective-permute-start.9 = (f32[4,64,512]{2,1,0:T(8,128)}, f32[4,64,512]{2,1,0:T(8,128)S(1)}, u32[]{:S(2)}, u32[]{:S(2)}) collective-permute-start(f32[4,64,512]{2,1,0:T(8,128)} %get-tuple-element.89), channel_id=1, source_target_pairs={{0,3},{1,0},{2,1},{3,2},{4,7},{5,4},{6,5},{7,6},{8,11},{9,8},{10,9... | collective-permute-start | bytes 1572872 | tf_op jit(solution)/shard_map/ppermute | solution.py:35
  67.4 1.5 fusion.3
  69.0 5.9 %collective-permute-done.17 = f32[2,192,512]{2,1,0:T(8,128)} collective-permute-done((f32[2,192,512]{2,1,0:T(8,128)}, f32[2,192,512]{2,1,0:T(8,128)}, u32[]{:S(2)}, u32[]{:S(2)}) %collective-permute-start.17) | collective-permute-done | bytes 786464 | tf_op jit(solution)/shard_map/ppermute | solution.py:35
  74.9 1.2 fusion.5
  76.1 1.5 collective-permute-start.13
  78.8 1.5 fusion
  80.3 1.3 collective-permute-start.16
  82.2 3.8 %collective-permute-done.10 = f32[4,64,512]{2,1,0:T(8,128)S(1)} collective-permute-done((f32[4,64,512]{2,1,0:T(8,128)}, f32[4,64,512]{2,1,0:T(8,128)S(1)}, u32[]{:S(2)}, u32[]{:S(2)}) %collective-permute-start.10) | collective-permute-done | bytes 524320 | tf_op jit(solution)/shard_map/ppermute | solution.py:35
  87.1 1.6 collective-permute-start.21
  88.7 6.7 %collective-permute-done.13 = f32[192,512]{1,0:T(8,128)S(1)} collective-permute-done((f32[192,512]{1,0:T(8,128)S(1)}, f32[192,512]{1,0:T(8,128)S(1)}, u32[]{:S(2)}, u32[]{:S(2)}) %collective-permute-start.13) | collective-permute-done | bytes 393248 | tf_op jit(solution)/shard_map/ppermute | solution.py:35
  95.4 2.4 %collective-permute-start.20 = (f32[192,512]{1,0:T(8,128)S(1)}, f32[192,512]{1,0:T(8,128)S(1)}, u32[]{:S(2)}, u32[]{:S(2)}) collective-permute-start(f32[192,512]{1,0:T(8,128)S(1)} %get-tuple-element.130), channel_id=1, source_target_pairs={{0,2},{1,3},{2,0},{3,1},{4,6},{5,7},{6,4},{7,5},{8,10},{9,11},{10,... | collective-permute-start | bytes 1179656 | tf_op jit(solution)/shard_map/ppermute | solution.py:35
  97.8 1.3 add_add_fusion.1
  99.3 2.6 %collective-permute-done.15 = f32[192,512]{1,0:T(8,128)S(1)} collective-permute-done((f32[192,512]{1,0:T(8,128)S(1)}, f32[192,512]{1,0:T(8,128)S(1)}, u32[]{:S(2)}, u32[]{:S(2)}) %collective-permute-start.15) | collective-permute-done | bytes 393248 | tf_op jit(solution)/shard_map/ppermute | solution.py:35
  102.0 5.2 %collective-permute-done.20 = f32[192,512]{1,0:T(8,128)S(1)} collective-permute-done((f32[192,512]{1,0:T(8,128)S(1)}, f32[192,512]{1,0:T(8,128)S(1)}, u32[]{:S(2)}, u32[]{:S(2)}) %collective-permute-start.20) | collective-permute-done | bytes 393248 | tf_op jit(solution)/shard_map/ppermute | solution.py:35
  107.8 1.2 fusion.9
  109.4 1.2 fusion.7
  110.6 7.0 %collective-permute-start.32 = (f32[64,512]{1,0:T(8,128)S(1)}, f32[64,512]{1,0:T(8,128)S(1)}, u32[]{:S(2)}, u32[]{:S(2)}) collective-permute-start(f32[64,512]{1,0:T(8,128)S(1)} %slice.160), channel_id=1, source_target_pairs={{0,32},{1,33},{2,34},{3,35},{4,36},{5,37},{6,38},{7,39},{8,40},{9,... | collective-permute-start | bytes 393224 | tf_op jit(solution)/shard_map/ppermute | solution.py:35
  117.6 1.2 collective-permute-start.30
  119.1 1.9 %collective-permute-done.22 = f32[4,64,512]{2,1,0:T(8,128)S(1)} collective-permute-done((f32[4,64,512]{2,1,0:T(8,128)S(1)}, f32[4,64,512]{2,1,0:T(8,128)S(1)}, u32[]{:S(2)}, u32[]{:S(2)}) %collective-permute-start.22) | collective-permute-done | bytes 524320 | tf_op jit(solution)/shard_map/ppermute | solution.py:35
  120.9 6.0 %collective-permute-start.31 = (f32[128,512]{1,0:T(8,128)S(1)}, f32[128,512]{1,0:T(8,128)S(1)}, u32[]{:S(2)}, u32[]{:S(2)}) collective-permute-start(f32[128,512]{1,0:T(8,128)S(1)} %slice.159), channel_id=1, source_target_pairs={{0,48},{1,49},{2,50},{3,51},{4,52},{5,53},{6,54},{7,55},{8,56},{9,... | collective-permute-start | bytes 786440 | tf_op jit(solution)/shard_map/ppermute | solution.py:35
  128.4 1.5 collective-permute-start.23
  129.9 2.7 %collective-permute-start.29 = (f32[64,512]{1,0:T(8,128)S(1)}, f32[64,512]{1,0:T(8,128)S(1)}, u32[]{:S(2)}, u32[]{:S(2)}) collective-permute-start(f32[64,512]{1,0:T(8,128)S(1)} %get-tuple-element.133), channel_id=1, source_target_pairs={{0,3},{1,0},{2,1},{3,2},{4,7},{5,4},{6,5},{7,6},{8,11},{9,8},{10,9... | collective-permute-start | bytes 393224 | tf_op jit(solution)/shard_map/ppermute | solution.py:35
  133.4 1.9 %collective-permute-start.28 = (f32[64,512]{1,0:T(8,128)S(1)}, f32[64,512]{1,0:T(8,128)S(1)}, u32[]{:S(2)}, u32[]{:S(2)}) collective-permute-start(f32[64,512]{1,0:T(8,128)S(1)} %get-tuple-element.134), channel_id=1, source_target_pairs={{0,2},{1,3},{2,0},{3,1},{4,6},{5,7},{6,4},{7,5},{8,10},{9,11},{10,... | collective-permute-start | bytes 393224 | tf_op jit(solution)/shard_map/ppermute | solution.py:35
  135.3 1.2 collective-permute-start.27
  136.9 2.1 %collective-permute-done.28.refs_6_ = f32[64,512]{1,0:T(8,128)S(1)} collective-permute-done((f32[64,512]{1,0:T(8,128)S(1)}, f32[64,512]{1,0:T(8,128)S(1)}, u32[]{:S(2)}, u32[]{:S(2)}) %collective-permute-start.28) | collective-permute-done | bytes 131104 | tf_op jit(solution)/shard_map/ppermute | solution.py:35
  139.0 2.2 %collective-permute-done.27.refs_5_ = f32[64,512]{1,0:T(8,128)S(1)} collective-permute-done((f32[64,512]{1,0:T(8,128)S(1)}, f32[64,512]{1,0:T(8,128)S(1)}, u32[]{:S(2)}, u32[]{:S(2)}) %collective-permute-start.27) | collective-permute-done | bytes 131104 | tf_op jit(solution)/shard_map/ppermute | solution.py:35
  141.8 3.5 %shard_map.110 = (f32[128,512]{1,0:T(8,128)}, f32[16,512]{1,0:T(8,128)}) custom-call(s32[4]{0:T(128)} %direction_ref.5, f32[64,512]{1,0:T(8,128)} %get-tuple-element.140.refs_0_, f32[64,512]{1,0:T(8,128)} %copy-done.15, f32[64,512]{1,0:T(8,128)} %copy-done.14, f32[64,512]{1,0:T(8,128)} %copy-done.13, f32[64,512]{1,0:T(8,128)} %get-tuple-element.136.refs_4_, ...), custom_call_target="tpu_custom_call" | custom-call | flops 40000000 | bytes 3145728 | tf_op jit(solution)/shard_map/pallas_call | solution.py:369
  145.3 15.8 %collective-permute-start.36 = (f32[16,512]{1,0:T(8,128)}, f32[16,512]{1,0:T(8,128)S(1)}, u32[]{:S(2)}, u32[]{:S(2)}) collective-permute-start(f32[16,512]{1,0:T(8,128)} %get-tuple-element.127), channel_id=1, source_target_pairs={{0,192},{64,0},{128,64},{192,128},{1,193},{65,1},{129,65},{193,129... | collective-permute-start | bytes 98312 | tf_op jit(solution)/shard_map/ppermute | solution.py:376
  161.1 1.7 %collective-permute-start.34 = (f32[16,512]{1,0:T(8,128)}, f32[16,512]{1,0:T(8,128)S(1)}, u32[]{:S(2)}, u32[]{:S(2)}) collective-permute-start(f32[16,512]{1,0:T(8,128)} %get-tuple-element.127), channel_id=1, source_target_pairs={{0,64},{64,128},{128,192},{192,0},{1,65},{65,129},{129,193},{193,1... | collective-permute-start | bytes 98312 | tf_op jit(solution)/shard_map/ppermute | solution.py:376
  162.8 3.4 %shard_map.111.particular_ref = f32[128,512]{1,0:T(8,128)} custom-call(s32[4]{0:T(128)} %direction_ref.5, f32[128,512]{1,0:T(8,128)} %get-tuple-element.128.source_ref, f32[1,512]{1,0:T(1,128)} %bitcast.93, bf16[4,8,128,128]{3,2,1,0:T(8,128)(2,1)} %get-tuple-element.125.refs_12_.high_ref, bf16[4,8,128,128]{3,2,1,0:T(8,128)(2,1)} %get-tuple-element.126.refs_13_.low_ref), custom_call_target="tpu_custom_call" | custom-call | flops 40000000 | bytes 3145728 | tf_op jit(solution)/shard_map/pallas_call | solution.py:378
  166.9 3.5 %shard_map.112 = f32[128,512]{1,0:T(8,128)} custom-call(s32[4]{0:T(128)} %direction_ref.5, s32[1]{0:T(128)} %bitcast.slab_ref, f32[16,512]{1,0:T(8,128)} %select_reduce_fusion.wall_ref, f32[16,512]{1,0:T(8,128)} %copy-done.21, f32[16,512]{1,0:T(8,128)} %copy-done.20, f32[16,512]{1,0:T(8,128)} %copy-done.19, f32[1,512]{1,0:T(1,128)} %bitcast.94, ...), custom_call_target="tpu_custom_call" | custom-call | flops 60000000 | bytes 3145728 | tf_op jit(solution)/shard_map/pallas_call | solution.py:381
  (110 shorter events, 11.4 us)
Async XLA Ops:
  5.1 18.8 %collective-permute-start.4 = (f32[2,192,512]{2,1,0:T(8,128)}, f32[2,192,512]{2,1,0:T(8,128)S(1)}, u32[]{:S(2)}, u32[]{:S(2)}) collective-permute-start(f32[2,192,512]{2,1,0:T(8,128)} %get-tuple-element.74), channel_id=1, source_target_pairs={{0,1},{1,2},{2,3},{3,0},{4,5},{5,6},{6,7},{7,4},{8,9},{9,10},{10,1... | collective-permute-start | bytes 2359304 | tf_op jit(solution)/shard_map/ppermute | solution.py:35
  7.2 18.5 %collective-permute-start.5 = (f32[2,192,512]{2,1,0:T(8,128)}, f32[2,192,512]{2,1,0:T(8,128)S(1)}, u32[]{:S(2)}, u32[]{:S(2)}) collective-permute-start(f32[2,192,512]{2,1,0:T(8,128)} %get-tuple-element.75), channel_id=1, source_target_pairs={{0,3},{1,0},{2,1},{3,2},{4,7},{5,4},{6,5},{7,6},{8,11},{9,8},{10,9... | collective-permute-start | bytes 2359304 | tf_op jit(solution)/shard_map/ppermute | solution.py:35
  8.6 31.8 %collective-permute-start.6 = (f32[2,192,512]{2,1,0:T(8,128)}, f32[2,192,512]{2,1,0:T(8,128)}, u32[]{:S(2)}, u32[]{:S(2)}) collective-permute-start(f32[2,192,512]{2,1,0:T(8,128)} %get-tuple-element.76), channel_id=1, source_target_pairs={{0,4},{1,5},{2,6},{3,7},{4,8},{5,9},{6,10},{7,11},{8,12},{9,13},{1... | collective-permute-start | bytes 2359304 | tf_op jit(solution)/shard_map/ppermute | solution.py:35
  10.0 30.5 %collective-permute-start.7 = (f32[2,192,512]{2,1,0:T(8,128)}, f32[2,192,512]{2,1,0:T(8,128)}, u32[]{:S(2)}, u32[]{:S(2)}) collective-permute-start(f32[2,192,512]{2,1,0:T(8,128)} %get-tuple-element.77), channel_id=1, source_target_pairs={{0,12},{1,13},{2,14},{3,15},{4,0},{5,1},{6,2},{7,3},{8,4},{9,5},{1... | collective-permute-start | bytes 2359304 | tf_op jit(solution)/shard_map/ppermute | solution.py:35
  16.4 32.7 %collective-permute-start = (f32[2,192,512]{2,1,0:T(8,128)}, f32[2,192,512]{2,1,0:T(8,128)S(1)}, u32[]{:S(2)}, u32[]{:S(2)}) collective-permute-start(f32[2,192,512]{2,1,0:T(8,128)} %get-tuple-element.67), channel_id=1, source_target_pairs={{0,3},{1,0},{2,1},{3,2},{4,7},{5,4},{6,5},{7,6},{8,11},{9,8},{10,9... | collective-permute-start | bytes 2359304 | tf_op jit(solution)/shard_map/ppermute | solution.py:35
  23.9 16.5 %copy-start.3 = (f32[2,192,512]{2,1,0:T(8,128)}, f32[2,192,512]{2,1,0:T(8,128)S(1)}, u32[]{:S(2)}) copy-start(f32[2,192,512]{2,1,0:T(8,128)S(1)} %collective-permute-done.4.refs_16_) | copy-start | bytes 2359300
  23.9 25.5 %collective-permute-start.1 = (f32[2,192,512]{2,1,0:T(8,128)}, f32[2,192,512]{2,1,0:T(8,128)S(1)}, u32[]{:S(2)}, u32[]{:S(2)}) collective-permute-start(f32[2,192,512]{2,1,0:T(8,128)} %get-tuple-element.68), channel_id=1, source_target_pairs={{0,1},{1,2},{2,3},{3,0},{4,5},{5,6},{6,7},{7,4},{8,9},{9,10},{10,1... | collective-permute-start | bytes 2359304 | tf_op jit(solution)/shard_map/ppermute | solution.py:35
  26.6 22.9 %collective-permute-start.2 = (f32[2,192,512]{2,1,0:T(8,128)}, f32[2,192,512]{2,1,0:T(8,128)S(1)}, u32[]{:S(2)}, u32[]{:S(2)}) collective-permute-start(f32[2,192,512]{2,1,0:T(8,128)} %get-tuple-element.69), channel_id=1, source_target_pairs={{0,12},{1,13},{2,14},{3,15},{4,0},{5,1},{6,2},{7,3},{8,4},{9,5},{1... | collective-permute-start | bytes 2359304 | tf_op jit(solution)/shard_map/ppermute | solution.py:35
  40.4 17.5 %collective-permute-start.3 = (f32[2,192,512]{2,1,0:T(8,128)}, f32[2,192,512]{2,1,0:T(8,128)S(1)}, u32[]{:S(2)}, u32[]{:S(2)}) collective-permute-start(f32[2,192,512]{2,1,0:T(8,128)} %get-tuple-element.70), channel_id=1, source_target_pairs={{0,4},{1,5},{2,6},{3,7},{4,8},{5,9},{6,10},{7,11},{8,12},{9,13},{1... | collective-permute-start | bytes 2359304 | tf_op jit(solution)/shard_map/ppermute | solution.py:35
  40.5 11.8 %copy-start.27 = (s32[16]{0:T(128)S(1)}, s32[16]{0:T(128)}, u32[]{:S(2)}) copy-start(s32[16]{0:T(128)} %param.21) | copy-start | bytes 196
  46.4 18.6 %collective-permute-start.14 = (f32[2,192,512]{2,1,0:T(8,128)}, f32[2,192,512]{2,1,0:T(8,128)}, u32[]{:S(2)}, u32[]{:S(2)}) collective-permute-start(f32[2,192,512]{2,1,0:T(8,128)} %get-tuple-element.107), channel_id=1, source_target_pairs={{0,3},{1,0},{2,1},{3,2},{4,7},{5,4},{6,5},{7,6},{8,11},{9,8},{10,9... | collective-permute-start | bytes 2359304 | tf_op jit(solution)/shard_map/ppermute | solution.py:35
  49.1 9.9 %copy-start = (f32[2,192,512]{2,1,0:T(8,128)}, f32[2,192,512]{2,1,0:T(8,128)S(1)}, u32[]{:S(2)}) copy-start(f32[2,192,512]{2,1,0:T(8,128)S(1)} %collective-permute-done.refs_16_) | copy-start | bytes 2359300
  49.1 19.8 %collective-permute-start.12 = (f32[2,192,512]{2,1,0:T(8,128)}, f32[2,192,512]{2,1,0:T(8,128)}, u32[]{:S(2)}, u32[]{:S(2)}) collective-permute-start(f32[2,192,512]{2,1,0:T(8,128)} %get-tuple-element.105), channel_id=1, source_target_pairs={{0,1},{1,2},{2,3},{3,0},{4,5},{5,6},{6,7},{7,4},{8,9},{9,10},{10,1... | collective-permute-start | bytes 2359304 | tf_op jit(solution)/shard_map/ppermute | solution.py:35
  49.4 25.5 %collective-permute-start.17 = (f32[2,192,512]{2,1,0:T(8,128)}, f32[2,192,512]{2,1,0:T(8,128)}, u32[]{:S(2)}, u32[]{:S(2)}) collective-permute-start(f32[2,192,512]{2,1,0:T(8,128)} %get-tuple-element.109), channel_id=1, source_target_pairs={{0,4},{1,5},{2,6},{3,7},{4,8},{5,9},{6,10},{7,11},{8,12},{9,13},{1... | collective-permute-start | bytes 2359304 | tf_op jit(solution)/shard_map/ppermute | solution.py:35
  49.5 26.5 %collective-permute-start.19 = (f32[2,192,512]{2,1,0:T(8,128)}, f32[2,192,512]{2,1,0:T(8,128)}, u32[]{:S(2)}, u32[]{:S(2)}) collective-permute-start(f32[2,192,512]{2,1,0:T(8,128)} %get-tuple-element.111), channel_id=1, source_target_pairs={{0,12},{1,13},{2,14},{3,15},{4,0},{5,1},{6,2},{7,3},{8,4},{9,5},{1... | collective-permute-start | bytes 2359304 | tf_op jit(solution)/shard_map/ppermute | solution.py:35
  57.9 22.4 %collective-permute-start.8 = (f32[4,64,512]{2,1,0:T(8,128)}, f32[4,64,512]{2,1,0:T(8,128)}, u32[]{:S(2)}, u32[]{:S(2)}) collective-permute-start(f32[4,64,512]{2,1,0:T(8,128)} %get-tuple-element.88), channel_id=1, source_target_pairs={{0,1},{1,2},{2,3},{3,0},{4,5},{5,6},{6,7},{7,4},{8,9},{9,10},{10,1... | collective-permute-start | bytes 1572872 | tf_op jit(solution)/shard_map/ppermute | solution.py:35
  64.9 34.3 %copy-start.8 = (f32[4,64,512]{2,1,0:T(8,128)S(1)}, f32[4,64,512]{2,1,0:T(8,128)}, u32[]{:S(2)}) copy-start(f32[4,64,512]{2,1,0:T(8,128)} %get-tuple-element.90) | copy-start | bytes 1572868
  64.9 42.3 %copy-start.26 = (f32[4,64,512]{2,1,0:T(8,128)S(1)}, f32[4,64,512]{2,1,0:T(8,128)}, u32[]{:S(2)}) copy-start(f32[4,64,512]{2,1,0:T(8,128)} %get-tuple-element.112) | copy-start | bytes 1572868
  64.9 42.9 %copy-start.7 = (f32[2,192,512]{2,1,0:T(8,128)S(1)}, f32[2,192,512]{2,1,0:T(8,128)}, u32[]{:S(2)}) copy-start(f32[2,192,512]{2,1,0:T(8,128)} %get-tuple-element.115) | copy-start | bytes 2359300
  64.9 44.1 %copy-start.25 = (f32[4,64,512]{2,1,0:T(8,128)S(1)}, f32[4,64,512]{2,1,0:T(8,128)}, u32[]{:S(2)}) copy-start(f32[4,64,512]{2,1,0:T(8,128)} %get-tuple-element.114) | copy-start | bytes 1572868
  64.9 44.4 %copy-start.6 = (f32[2,192,512]{2,1,0:T(8,128)S(1)}, f32[2,192,512]{2,1,0:T(8,128)}, u32[]{:S(2)}) copy-start(f32[2,192,512]{2,1,0:T(8,128)} %get-tuple-element.120) | copy-start | bytes 2359300
  64.9 16.6 %collective-permute-start.9 = (f32[4,64,512]{2,1,0:T(8,128)}, f32[4,64,512]{2,1,0:T(8,128)S(1)}, u32[]{:S(2)}, u32[]{:S(2)}) collective-permute-start(f32[4,64,512]{2,1,0:T(8,128)} %get-tuple-element.89), channel_id=1, source_target_pairs={{0,3},{1,0},{2,1},{3,2},{4,7},{5,4},{6,5},{7,6},{8,11},{9,8},{10,9... | collective-permute-start | bytes 1572872 | tf_op jit(solution)/shard_map/ppermute | solution.py:35
  68.9 17.1 %collective-permute-start.10 = (f32[4,64,512]{2,1,0:T(8,128)}, f32[4,64,512]{2,1,0:T(8,128)S(1)}, u32[]{:S(2)}, u32[]{:S(2)}) collective-permute-start(f32[4,64,512]{2,1,0:T(8,128)} %get-tuple-element.91), channel_id=1, source_target_pairs={{0,4},{1,5},{2,6},{3,7},{4,8},{5,9},{6,10},{7,11},{8,12},{9,13},{1... | collective-permute-start | bytes 1572872 | tf_op jit(solution)/shard_map/ppermute | solution.py:35
  74.9 12.3 %collective-permute-start.11 = (f32[4,64,512]{2,1,0:T(8,128)}, f32[4,64,512]{2,1,0:T(8,128)S(1)}, u32[]{:S(2)}, u32[]{:S(2)}) collective-permute-start(f32[4,64,512]{2,1,0:T(8,128)} %get-tuple-element.92), channel_id=1, source_target_pairs={{0,12},{1,13},{2,14},{3,15},{4,0},{5,1},{6,2},{7,3},{8,4},{9,5},{1... | collective-permute-start | bytes 1572872 | tf_op jit(solution)/shard_map/ppermute | solution.py:35
  76.1 19.3 %collective-permute-start.13 = (f32[192,512]{1,0:T(8,128)S(1)}, f32[192,512]{1,0:T(8,128)S(1)}, u32[]{:S(2)}, u32[]{:S(2)}) collective-permute-start(f32[192,512]{1,0:T(8,128)S(1)} %fusion.5), channel_id=1, source_target_pairs={{0,4},{1,5},{2,6},{3,7},{4,8},{5,9},{6,10},{7,11},{8,12},{9,13},{1... | collective-permute-start | bytes 1179656 | tf_op jit(solution)/shard_map/ppermute | solution.py:35
  80.3 19.0 %collective-permute-start.16 = (f32[192,512]{1,0:T(8,128)S(1)}, f32[192,512]{1,0:T(8,128)S(1)}, u32[]{:S(2)}, u32[]{:S(2)}) collective-permute-start(f32[192,512]{1,0:T(8,128)S(1)} %get-tuple-element.131), channel_id=1, source_target_pairs={{0,12},{1,13},{2,14},{3,15},{4,0},{5,1},{6,2},{7,3},{8,4},{9,5},{1... | collective-permute-start | bytes 1179656 | tf_op jit(solution)/shard_map/ppermute | solution.py:35
  81.6 20.4 %collective-permute-start.15 = (f32[192,512]{1,0:T(8,128)S(1)}, f32[192,512]{1,0:T(8,128)S(1)}, u32[]{:S(2)}, u32[]{:S(2)}) collective-permute-start(f32[192,512]{1,0:T(8,128)S(1)} %get-tuple-element.132), channel_id=1, source_target_pairs={{0,8},{1,9},{2,10},{3,11},{4,12},{5,13},{6,14},{7,15},{8,0},{9,1},... | collective-permute-start | bytes 1179656 | tf_op jit(solution)/shard_map/ppermute | solution.py:35
  86.0 16.0 %collective-permute-start.18 = (f32[192,512]{1,0:T(8,128)S(1)}, f32[192,512]{1,0:T(8,128)S(1)}, u32[]{:S(2)}, u32[]{:S(2)}) collective-permute-start(f32[192,512]{1,0:T(8,128)S(1)} %fusion.2), channel_id=1, source_target_pairs={{0,1},{1,2},{2,3},{3,0},{4,5},{5,6},{6,7},{7,4},{8,9},{9,10},{10,1... | collective-permute-start | bytes 1179656 | tf_op jit(solution)/shard_map/ppermute | solution.py:35
  87.1 14.8 %collective-permute-start.21 = (f32[192,512]{1,0:T(8,128)S(1)}, f32[192,512]{1,0:T(8,128)S(1)}, u32[]{:S(2)}, u32[]{:S(2)}) collective-permute-start(f32[192,512]{1,0:T(8,128)S(1)} %get-tuple-element.129), channel_id=1, source_target_pairs={{0,3},{1,0},{2,1},{3,2},{4,7},{5,4},{6,5},{7,6},{8,11},{9,8},{10,9... | collective-permute-start | bytes 1179656 | tf_op jit(solution)/shard_map/ppermute | solution.py:35
  95.4 11.8 %collective-permute-start.20 = (f32[192,512]{1,0:T(8,128)S(1)}, f32[192,512]{1,0:T(8,128)S(1)}, u32[]{:S(2)}, u32[]{:S(2)}) collective-permute-start(f32[192,512]{1,0:T(8,128)S(1)} %get-tuple-element.130), channel_id=1, source_target_pairs={{0,2},{1,3},{2,0},{3,1},{4,6},{5,7},{6,4},{7,5},{8,10},{9,11},{10,... | collective-permute-start | bytes 1179656 | tf_op jit(solution)/shard_map/ppermute | solution.py:35
  107.2 13.7 %collective-permute-start.22 = (f32[4,64,512]{2,1,0:T(8,128)S(1)}, f32[4,64,512]{2,1,0:T(8,128)S(1)}, u32[]{:S(2)}, u32[]{:S(2)}) collective-permute-start(f32[4,64,512]{2,1,0:T(8,128)S(1)} %copy-done.26), channel_id=1, source_target_pairs={{0,2},{1,3},{2,0},{3,1},{4,6},{5,7},{6,4},{7,5},{8,10},{9,11},{10,... | collective-permute-start | bytes 1572872 | tf_op jit(solution)/shard_map/ppermute | solution.py:35
  109.0 18.6 %collective-permute-start.26 = (f32[4,64,512]{2,1,0:T(8,128)S(1)}, f32[4,64,512]{2,1,0:T(8,128)S(1)}, u32[]{:S(2)}, u32[]{:S(2)}) collective-permute-start(f32[4,64,512]{2,1,0:T(8,128)S(1)} %copy-done.25), channel_id=1, source_target_pairs={{0,8},{1,9},{2,10},{3,11},{4,12},{5,13},{6,14},{7,15},{8,0},{9,1},... | collective-permute-start | bytes 1572872 | tf_op jit(solution)/shard_map/ppermute | solution.py:35
  110.6 17.8 %collective-permute-start.32 = (f32[64,512]{1,0:T(8,128)S(1)}, f32[64,512]{1,0:T(8,128)S(1)}, u32[]{:S(2)}, u32[]{:S(2)}) collective-permute-start(f32[64,512]{1,0:T(8,128)S(1)} %slice.160), channel_id=1, source_target_pairs={{0,32},{1,33},{2,34},{3,35},{4,36},{5,37},{6,38},{7,39},{8,40},{9,... | collective-permute-start | bytes 393224 | tf_op jit(solution)/shard_map/ppermute | solution.py:35
  117.6 12.4 %collective-permute-start.30 = (f32[128,512]{1,0:T(8,128)S(1)}, f32[128,512]{1,0:T(8,128)S(1)}, u32[]{:S(2)}, u32[]{:S(2)}) collective-permute-start(f32[128,512]{1,0:T(8,128)S(1)} %slice.158), channel_id=1, source_target_pairs={{0,16},{1,17},{2,18},{3,19},{4,20},{5,21},{6,22},{7,23},{8,24},{9,... | collective-permute-start | bytes 786440 | tf_op jit(solution)/shard_map/ppermute | solution.py:35
  118.8 9.6 %collective-permute-start.33 = (f32[64,512]{1,0:T(8,128)S(1)}, f32[64,512]{1,0:T(8,128)S(1)}, u32[]{:S(2)}, u32[]{:S(2)}) collective-permute-start(f32[64,512]{1,0:T(8,128)S(1)} %slice.161), channel_id=1, source_target_pairs={{0,32},{1,33},{2,34},{3,35},{4,36},{5,37},{6,38},{7,39},{8,40},{9,... | collective-permute-start | bytes 393224 | tf_op jit(solution)/shard_map/ppermute | solution.py:35
  120.9 12.5 %collective-permute-start.31 = (f32[128,512]{1,0:T(8,128)S(1)}, f32[128,512]{1,0:T(8,128)S(1)}, u32[]{:S(2)}, u32[]{:S(2)}) collective-permute-start(f32[128,512]{1,0:T(8,128)S(1)} %slice.159), channel_id=1, source_target_pairs={{0,48},{1,49},{2,50},{3,51},{4,52},{5,53},{6,54},{7,55},{8,56},{9,... | collective-permute-start | bytes 786440 | tf_op jit(solution)/shard_map/ppermute | solution.py:35
  127.6 7.7 %collective-permute-start.25 = (f32[64,512]{1,0:T(8,128)S(1)}, f32[64,512]{1,0:T(8,128)S(1)}, u32[]{:S(2)}, u32[]{:S(2)}) collective-permute-start(f32[64,512]{1,0:T(8,128)S(1)} %get-tuple-element.137), channel_id=1, source_target_pairs={{0,12},{1,13},{2,14},{3,15},{4,0},{5,1},{6,2},{7,3},{8,4},{9,5},{1... | collective-permute-start | bytes 393224 | tf_op jit(solution)/shard_map/ppermute | solution.py:35
  128.4 12.8 %copy-start.11 = (f32[64,512]{1,0:T(8,128)}, f32[64,512]{1,0:T(8,128)S(1)}, u32[]{:S(2)}) copy-start(f32[64,512]{1,0:T(8,128)S(1)} %collective-permute-done.32.refs_10_) | copy-start | bytes 393220
  128.4 8.1 %collective-permute-start.24 = (f32[64,512]{1,0:T(8,128)S(1)}, f32[64,512]{1,0:T(8,128)S(1)}, u32[]{:S(2)}, u32[]{:S(2)}) collective-permute-start(f32[64,512]{1,0:T(8,128)S(1)} %get-tuple-element.138), channel_id=1, source_target_pairs={{0,8},{1,9},{2,10},{3,11},{4,12},{5,13},{6,14},{7,15},{8,0},{9,1},... | collective-permute-start | bytes 393224 | tf_op jit(solution)/shard_map/ppermute | solution.py:35
  128.4 12.8 %copy-start.12 = (f32[64,512]{1,0:T(8,128)}, f32[64,512]{1,0:T(8,128)S(1)}, u32[]{:S(2)}) copy-start(f32[64,512]{1,0:T(8,128)S(1)} %collective-permute-done.33.refs_11_) | copy-start | bytes 393220
  128.4 8.5 %collective-permute-start.23 = (f32[64,512]{1,0:T(8,128)S(1)}, f32[64,512]{1,0:T(8,128)S(1)}, u32[]{:S(2)}, u32[]{:S(2)}) collective-permute-start(f32[64,512]{1,0:T(8,128)S(1)} %get-tuple-element.139), channel_id=1, source_target_pairs={{0,4},{1,5},{2,6},{3,7},{4,8},{5,9},{6,10},{7,11},{8,12},{9,13},{1... | collective-permute-start | bytes 393224 | tf_op jit(solution)/shard_map/ppermute | solution.py:35
  129.9 11.2 %copy-start.9 = (f32[128,512]{1,0:T(8,128)}, f32[128,512]{1,0:T(8,128)S(1)}, u32[]{:S(2)}) copy-start(f32[128,512]{1,0:T(8,128)S(1)} %collective-permute-done.30.refs_8_) | copy-start | bytes 786436
  129.9 6.9 %collective-permute-start.29 = (f32[64,512]{1,0:T(8,128)S(1)}, f32[64,512]{1,0:T(8,128)S(1)}, u32[]{:S(2)}, u32[]{:S(2)}) collective-permute-start(f32[64,512]{1,0:T(8,128)S(1)} %get-tuple-element.133), channel_id=1, source_target_pairs={{0,3},{1,0},{2,1},{3,2},{4,7},{5,4},{6,5},{7,6},{8,11},{9,8},{10,9... | collective-permute-start | bytes 393224 | tf_op jit(solution)/shard_map/ppermute | solution.py:35
  133.4 5.6 %collective-permute-start.28 = (f32[64,512]{1,0:T(8,128)S(1)}, f32[64,512]{1,0:T(8,128)S(1)}, u32[]{:S(2)}, u32[]{:S(2)}) collective-permute-start(f32[64,512]{1,0:T(8,128)S(1)} %get-tuple-element.134), channel_id=1, source_target_pairs={{0,2},{1,3},{2,0},{3,1},{4,6},{5,7},{6,4},{7,5},{8,10},{9,11},{10,... | collective-permute-start | bytes 393224 | tf_op jit(solution)/shard_map/ppermute | solution.py:35
  135.3 5.8 %collective-permute-start.27 = (f32[64,512]{1,0:T(8,128)S(1)}, f32[64,512]{1,0:T(8,128)S(1)}, u32[]{:S(2)}, u32[]{:S(2)}) collective-permute-start(f32[64,512]{1,0:T(8,128)S(1)} %get-tuple-element.135), channel_id=1, source_target_pairs={{0,1},{1,2},{2,3},{3,0},{4,5},{5,6},{6,7},{7,4},{8,9},{9,10},{10,1... | collective-permute-start | bytes 393224 | tf_op jit(solution)/shard_map/ppermute | solution.py:35
  145.3 21.0 %collective-permute-start.36 = (f32[16,512]{1,0:T(8,128)}, f32[16,512]{1,0:T(8,128)S(1)}, u32[]{:S(2)}, u32[]{:S(2)}) collective-permute-start(f32[16,512]{1,0:T(8,128)} %get-tuple-element.127), channel_id=1, source_target_pairs={{0,192},{64,0},{128,64},{192,128},{1,193},{65,1},{129,65},{193,129... | collective-permute-start | bytes 98312 | tf_op jit(solution)/shard_map/ppermute | solution.py:376
  161.1 5.1 %collective-permute-start.35 = (f32[16,512]{1,0:T(8,128)}, f32[16,512]{1,0:T(8,128)S(1)}, u32[]{:S(2)}, u32[]{:S(2)}) collective-permute-start(f32[16,512]{1,0:T(8,128)} %get-tuple-element.127), channel_id=1, source_target_pairs={{0,128},{64,192},{128,0},{192,64},{1,129},{65,193},{129,1},{193,65... | collective-permute-start | bytes 98312 | tf_op jit(solution)/shard_map/ppermute | solution.py:376
  161.1 5.1 %collective-permute-start.34 = (f32[16,512]{1,0:T(8,128)}, f32[16,512]{1,0:T(8,128)S(1)}, u32[]{:S(2)}, u32[]{:S(2)}) collective-permute-start(f32[16,512]{1,0:T(8,128)} %get-tuple-element.127), channel_id=1, source_target_pairs={{0,64},{64,128},{128,192},{192,0},{1,65},{65,129},{129,193},{193,1... | collective-permute-start | bytes 98312 | tf_op jit(solution)/shard_map/ppermute | solution.py:376
  (17 other events, 78.0 us)

commit v4 on v3

--- a/solution.py
+++ b/solution.py
@@ -144,16 +144,19 @@
     row = lax.broadcasted_iota(jnp.int32, (BLK, BLK), 0)
     column = lax.broadcasted_iota(jnp.int32, (BLK, BLK), 1)
     unit = jnp.where(row == column, 1.0, 0.0).astype(jnp.float32)
-    now = [unit + inscatter_ref[b] for b in range(SHELL)]
-    for k in range(LAYERS):
+
+    def raise_power(k, now):
+        raised = []
         for b in range(SHELL):
             high = now[b].astype(jnp.bfloat16)
             high_ref[b, k] = high
             low_ref[b, k] = (now[b] - high.astype(jnp.float32)).astype(jnp.bfloat16)
-            if k + 1 < LAYERS:
-                now[b] = product(
-                    now[b] * rate_ref[:, pl.ds(b * BLK, BLK)], high_ref[b, 0], low_ref[b, 0]
-                )
+            raised.append(
+                product(now[b] * rate_ref[:, pl.ds(b * BLK, BLK)], high_ref[b, 0], low_ref[b, 0])
+            )
+        return tuple(raised)
+
+    lax.fori_loop(0, LAYERS, raise_power, tuple(unit + inscatter_ref[b] for b in range(SHELL)))
 
 
 def product(face, high, low):
@@ -167,12 +170,12 @@
 
 
 def last_kernel(direction_ref, *refs):
-    halves, wholes, quarters = refs[:8], refs[8:10], refs[10:12]
-    high_ref, low_ref, source_ref, out_ref = refs[12:]
+    halves, wholes = refs[:8], refs[8:10]
+    high_ref, low_ref, source_ref, out_ref = refs[10:]
     for side in range(2):
         rows = pl.ds(side * HALF, HALF)
-        total = quarters[side][...]
-        for part in halves[4 * side : 4 * side + 4]:
+        total = halves[4 * side][...]
+        for part in halves[4 * side + 1 : 4 * side + 4]:
             total += part[...]
         for part in wholes:
             total += part[rows, :]
@@ -248,9 +251,13 @@
 VMEM = pl.BlockSpec(memory_space=pltpu.VMEM)
 
 
-def small_call(kernel, outs, specs, scratch=(), flops=0):
+FIRST = pl.BlockSpec((SHELL, 1, BLK, BLK), lambda i: (0, 0, 0, 0))
+
+
+def small_call(kernel, outs, specs, scratch=(), flops=0, grid=()):
     return pl.pallas_call(
         kernel,
+        grid=grid,
         in_specs=specs,
         out_specs=[VMEM] * len(outs),
         out_shape=[jax.ShapeDtypeStruct(*out) for out in outs],
@@ -305,9 +312,6 @@
             moved.append(send(block, axes[index], signs[index]))
         return moved
 
-    def spread(blocks, axis):
-        return [send(block, axis, step) for block, step in zip(blocks, (1, 2, -1))]
-
     prior = occupation_prior
     split = [((SHELL, LAYERS, BLK, BLK), jnp.bfloat16)] * 2
     high, low = small_call(powers_kernel, split, [VMEM, VMEM], flops=200_000_000)(rate, inscatter)
@@ -354,14 +358,19 @@
     b_own, b_got = lax.optimization_barrier(((kept[2], late[2]), b_got))
     a_sum = a_own[0][0] + a_own[1][0] + a_got[0] + a_got[1] + a_got[2]
     b_sum = b_own[0][0] + b_own[1][0] + b_got[0] + b_got[1] + b_got[2]
-    depth = []
-    for block, step in ((a_sum[:CELL], 1), (b_sum[:CELL], -1), (a_sum[CELL:], 2), (b_sum[CELL:], 2)):
-        depth.append(send(block, 0, step))
-    from_below, from_above, far_a, far_b = depth
+    far_up = send(a_sum[CELL:], 0, 1)
+    far_down = send(b_sum[CELL:], 0, -1)
+    above = jnp.concatenate([a_sum[:HALF] + far_up, a_sum[HALF:CELL]], axis=0)
+    below = jnp.concatenate([b_sum[:HALF], b_sum[HALF:CELL] + far_down], axis=0)
+    from_below = send(above, 0, 1)
+    from_above = send(below, 0, -1)
 
     def ends(ready, got, axis):
         parts = [ready[i] + got[i] for i in range(SIDE)]
-        return [parts[0]] + spread(parts[1:], axis)
+        moved = []
+        for index, step in enumerate((1, 2, -1)):
+            moved.append(send(parts[index + 1], axis, step))
+        return [parts[0]] + moved
 
     halves = ends(ready_a, far_x, 1) + ends(ready_b, far_y, 2)
 
@@ -369,14 +378,14 @@
     source, last = small_call(
         last_kernel,
         [whole, ((LATERAL, WIDTH), jnp.float32)],
-        [SMEM] + [VMEM] * 14,
+        [SMEM] + [VMEM] * 12,
         flops=40_000_000,
-    )(direction, *halves, from_below, from_above, far_a, far_b, high, low)
+    )(direction, *halves, from_below, from_above, high, low)
     faces = [
         lax.ppermute(last, "slab", [(i, (i + k) % 4) for i in range(4)]) for k in (1, 2, 3)
     ]
     (particular,) = small_call(
-        particular_kernel, [whole], [SMEM] + [VMEM] * 4, flops=40_000_000
+        particular_kernel, [whole], [SMEM, VMEM, VMEM, FIRST, FIRST], flops=40_000_000, grid=(1,)
     )(direction, source, rate, high, low)
     (swept,) = small_call(
         finish_kernel,

time: 171 us -> 167 us (0.977)
  waiting for transfers between devices: 42.4 us -> 27 us
  starting transfers between devices: 70.9 us -> 81.4 us
    ppermute x34, waiting for transfers between devices: 42.4 us -> 27 us  [send(): return lax.ppermute(block, 'modes', route(axis, step))]
    ppermute x34, starting transfers between devices: 53.4 us -> 64.2 us  [send(): return lax.ppermute(block, 'modes', route(axis, step))]
  transfers between devices with their start and end apart: 37 -> 37, of which waited for: 12 -> 11; matrix products, arithmetic and copies ran while one was open for 7% -> 7% of each run, Pallas kernels for 18% -> 19%
where the time goes in v4:
time: 167 us; the launch traced here: 166 us
  starting transfers between devices  81.4 us (49%)
  Pallas kernels  42.9 us (26%)
  waiting for transfers between devices  27 us (16%)
  other arithmetic  11.3 us (7%)
  local copies, waits for them, and re-layouts  3.16 us (2%)
    ppermute x34, starting transfers between devices, send(): return lax.ppermute(block, 'modes', route(axis, step))  64.2 us
    pallas_call x5, Pallas kernels, partial_sums(): pl.pallas_call(functools.partial(partial_kernel, jobs, len(addends)), gri...  28.9 us
    ppermute x34, waiting for transfers between devices, send(): return lax.ppermute(block, 'modes', route(axis, step))  27 us
    ppermute x3, starting transfers between devices, per_device(): lax.ppermute(last, 'slab', [(i, (i + k) % 4) for i in range(4)])  17.2 us
    pallas_call x1, Pallas kernels, per_device(): small_call(powers_kernel, split, [VMEM, VMEM], flops=200000000)  4.3 us
    pallas_call x1, Pallas kernels, per_device(): small_call(finish_kernel, [whole], [SMEM, SMEM] + [VMEM] * 8, scratch=[pl...  3.46 us
    pallas_call x1, Pallas kernels, per_device(): small_call(last_kernel, [whole, ((LATERAL, WIDTH), jnp.float32)], [SMEM]...  3.42 us
  transfers between devices with their start and end apart: 37, of which 11 were waited for; matrix products, arithmetic and copies ran while one was open for 7% of the time, Pallas kernels for 19%

profile of v4, /device:TPU:1, one launch (start us, length us, event | category | flops | bytes accessed | tf_op | source)
XLA Modules:
  0.0 166.2 jit_solution(5808359079357073460)
XLA Ops:
  0.0 5.1 %partial_sums.6 = (f32[2,192,512]{2,1,0:T(8,128)}, f32[2,192,512]{2,1,0:T(8,128)}, f32[2,192,512]{2,1,0:T(8,128)}, f32[2,192,512]{2,1,0:T(8,128)}) custom-call(s32[1]{0:T(128)} %bitcast.1.place_ref, s32[4,64]{1,0:T(4,128)} %pattern_ref.9, f32[128,512]{1,0:T(8,128)} %x_ref.8, f32[1,512]{1,0:T(1,128)} %bitcast.87, f32[64,1,512]{2,1,0:T(1,128)} %bitcast.47, ...), custom_call_target="tpu_custom_call" | custom-call | flops 201326592 | bytes 4718592 | tf_op jit(solution)/shard_map/partial_sums/pallas_call | solution.py:107
  5.1 2.1 %collective-permute-start.4 = (f32[2,192,512]{2,1,0:T(8,128)}, f32[2,192,512]{2,1,0:T(8,128)S(1)}, u32[]{:S(2)}, u32[]{:S(2)}) collective-permute-start(f32[2,192,512]{2,1,0:T(8,128)} %get-tuple-element.74), channel_id=1, source_target_pairs={{0,1},{1,2},{2,3},{3,0},{4,5},{5,6},{6,7},{7,4},{8,9},{9,10},{10,1... | collective-permute-start | bytes 2359304 | tf_op jit(solution)/shard_map/ppermute | solution.py:35
  7.2 1.4 collective-permute-start.5
  8.6 1.4 collective-permute-start.6
  10.0 1.4 collective-permute-start.7
  11.4 5.1 %partial_sums.5 = (f32[2,192,512]{2,1,0:T(8,128)}, f32[2,192,512]{2,1,0:T(8,128)}, f32[2,192,512]{2,1,0:T(8,128)}, f32[2,192,512]{2,1,0:T(8,128)}) custom-call(s32[1]{0:T(128)} %bitcast.1.place_ref, s32[4,64]{1,0:T(4,128)} %pattern_ref.9, f32[128,512]{1,0:T(8,128)} %x_ref.8, f32[1,512]{1,0:T(1,128)} %bitcast.88, f32[64,1,512]{2,1,0:T(1,128)} %bitcast.55, ...), custom_call_target="tpu_custom_call" | custom-call | flops 201326592 | bytes 4718592 | tf_op jit(solution)/shard_map/partial_sums/pallas_call | solution.py:107
  16.5 1.4 collective-permute-start
  17.9 6.0 %collective-permute-done.4.refs_16_ = f32[2,192,512]{2,1,0:T(8,128)S(1)} collective-permute-done((f32[2,192,512]{2,1,0:T(8,128)}, f32[2,192,512]{2,1,0:T(8,128)S(1)}, u32[]{:S(2)}, u32[]{:S(2)}) %collective-permute-start.4) | collective-permute-done | bytes 786464 | tf_op jit(solution)/shard_map/ppermute | solution.py:35
  23.9 1.9 %collective-permute-start.1 = (f32[2,192,512]{2,1,0:T(8,128)}, f32[2,192,512]{2,1,0:T(8,128)S(1)}, u32[]{:S(2)}, u32[]{:S(2)}) collective-permute-start(f32[2,192,512]{2,1,0:T(8,128)} %get-tuple-element.68), channel_id=1, source_target_pairs={{0,1},{1,2},{2,3},{3,0},{4,5},{5,6},{6,7},{7,4},{8,9},{9,10},{10,1... | collective-permute-start | bytes 2359304 | tf_op jit(solution)/shard_map/ppermute | solution.py:35
  26.7 3.0 %collective-permute-start.2 = (f32[2,192,512]{2,1,0:T(8,128)}, f32[2,192,512]{2,1,0:T(8,128)S(1)}, u32[]{:S(2)}, u32[]{:S(2)}) collective-permute-start(f32[2,192,512]{2,1,0:T(8,128)} %get-tuple-element.69), channel_id=1, source_target_pairs={{0,12},{1,13},{2,14},{3,15},{4,0},{5,1},{6,2},{7,3},{8,4},{9,5},{1... | collective-permute-start | bytes 2359304 | tf_op jit(solution)/shard_map/ppermute | solution.py:35
  29.6 7.1 %partial_sums.7 = (f32[4,64,512]{2,1,0:T(8,128)}, f32[4,64,512]{2,1,0:T(8,128)}, f32[4,64,512]{2,1,0:T(8,128)}, f32[4,64,512]{2,1,0:T(8,128)}, f32[4,64,512]{2,1...) custom-call(s32[1]{0:T(128)} %bitcast.1.place_ref, s32[4,64]{1,0:T(4,128)} %pattern_ref.9, ...), custom_call_target="tpu_custom_call" | custom-call | flops 268435456 | bytes 6291456 | tf_op jit(solution)/shard_map/partial_sums/pallas_call | solution.py:107
  37.0 1.2 collective-permute-start.8
  38.2 5.8 %partial_sums.9 = (f32[2,192,512]{2,1,0:T(8,128)}, f32[2,192,512]{2,1,0:T(8,128)}, f32[2,192,512]{2,1,0:T(8,128)}, f32[2,192,512]{2,1,0:T(8,128)}) custom-call(s32[1]{0:T(128)} %bitcast.1.place_ref, s32[4,64]{1,0:T(4,128)} %pattern_ref.9, f32[128,512]{1,0:T(8,128)} %x_ref.8, f32[1,512]{1,0:T(1,128)} %bitcast.90, f32[64,1,512]{2,1,0:T(1,128)} %bitcast.71, ...), custom_call_target="tpu_custom_call" | custom-call | flops 201326592 | bytes 4718592 | tf_op jit(solution)/shard_map/partial_sums/pallas_call | solution.py:107
  44.0 1.6 collective-permute-start.9
  45.7 2.7 %collective-permute-start.14 = (f32[2,192,512]{2,1,0:T(8,128)}, f32[2,192,512]{2,1,0:T(8,128)}, u32[]{:S(2)}, u32[]{:S(2)}) collective-permute-start(f32[2,192,512]{2,1,0:T(8,128)} %get-tuple-element.107), channel_id=1, source_target_pairs={{0,3},{1,0},{2,1},{3,2},{4,7},{5,4},{6,5},{7,6},{8,11},{9,8},{10,9... | collective-permute-start | bytes 2359304 | tf_op jit(solution)/shard_map/ppermute | solution.py:35
  48.4 4.3 %shard_map.109 = (bf16[4,8,128,128]{3,2,1,0:T(8,128)(2,1)}, bf16[4,8,128,128]{3,2,1,0:T(8,128)(2,1)}) custom-call(f32[1,512]{1,0:T(1,128)} %bitcast.92, f32[4,128,128]{2,1,0:T(8,128)} %inscatter_ref.1), custom_call_target="tpu_custom_call" | custom-call | flops 200000000 | bytes 3145728 | tf_op jit(solution)/shard_map/pallas_call | solution.py:317
  53.4 1.0 collective-permute-done.3.refs_19_
  55.3 5.8 %partial_sums.8 = (f32[2,192,512]{2,1,0:T(8,128)}, f32[2,192,512]{2,1,0:T(8,128)}, f32[2,192,512]{2,1,0:T(8,128)}, f32[2,192,512]{2,1,0:T(8,128)}) custom-call(s32[1]{0:T(128)} %bitcast.1.place_ref, s32[4,64]{1,0:T(4,128)} %pattern_ref.9, f32[128,512]{1,0:T(8,128)} %x_ref.8, f32[1,512]{1,0:T(1,128)} %bitcast.91, f32[64,1,512]{2,1,0:T(1,128)} %bitcast.79, ...), custom_call_target="tpu_custom_call" | custom-call | flops 201326592 | bytes 4718592 | tf_op jit(solution)/shard_map/partial_sums/pallas_call | solution.py:107
  61.5 2.4 %collective-permute-start.19 = (f32[2,192,512]{2,1,0:T(8,128)}, f32[2,192,512]{2,1,0:T(8,128)S(1)}, u32[]{:S(2)}, u32[]{:S(2)}) collective-permute-start(f32[2,192,512]{2,1,0:T(8,128)} %get-tuple-element.111), channel_id=1, source_target_pairs={{0,12},{1,13},{2,14},{3,15},{4,0},{5,1},{6,2},{7,3},{8,4},{9,5},{1... | collective-permute-start | bytes 2359304 | tf_op jit(solution)/shard_map/ppermute | solution.py:35
  63.9 1.5 add_add_fusion.1
  65.4 5.2 %collective-permute-done.12 = f32[2,192,512]{2,1,0:T(8,128)} collective-permute-done((f32[2,192,512]{2,1,0:T(8,128)}, f32[2,192,512]{2,1,0:T(8,128)}, u32[]{:S(2)}, u32[]{:S(2)}) %collective-permute-start.12) | collective-permute-done | bytes 786464 | tf_op jit(solution)/shard_map/ppermute | solution.py:35
  70.6 5.3 %collective-permute-start.11 = (f32[4,64,512]{2,1,0:T(8,128)}, f32[4,64,512]{2,1,0:T(8,128)S(1)}, u32[]{:S(2)}, u32[]{:S(2)}) collective-permute-start(f32[4,64,512]{2,1,0:T(8,128)} %get-tuple-element.92), channel_id=1, source_target_pairs={{0,12},{1,13},{2,14},{3,15},{4,0},{5,1},{6,2},{7,3},{8,4},{9,5},{1... | collective-permute-start | bytes 1572872 | tf_op jit(solution)/shard_map/ppermute | solution.py:35
  76.0 1.2 fusion.5
  77.2 1.5 fusion.3
  78.7 2.7 %collective-permute-start.16 = (f32[192,512]{1,0:T(8,128)S(1)}, f32[192,512]{1,0:T(8,128)S(1)}, u32[]{:S(2)}, u32[]{:S(2)}) collective-permute-start(f32[192,512]{1,0:T(8,128)S(1)} %get-tuple-element.131), channel_id=1, source_target_pairs={{0,12},{1,13},{2,14},{3,15},{4,0},{5,1},{6,2},{7,3},{8,4},{9,5},{1... | collective-permute-start | bytes 1179656 | tf_op jit(solution)/shard_map/ppermute | solution.py:35
  81.5 1.3 fusion
  82.9 1.0 fusion.2
  84.4 3.8 %collective-permute-done.11 = f32[4,64,512]{2,1,0:T(8,128)S(1)} collective-permute-done((f32[4,64,512]{2,1,0:T(8,128)}, f32[4,64,512]{2,1,0:T(8,128)S(1)}, u32[]{:S(2)}, u32[]{:S(2)}) %collective-permute-start.11) | collective-permute-done | bytes 524320 | tf_op jit(solution)/shard_map/ppermute | solution.py:35
  88.2 2.6 %collective-permute-start.21 = (f32[192,512]{1,0:T(8,128)S(1)}, f32[192,512]{1,0:T(8,128)S(1)}, u32[]{:S(2)}, u32[]{:S(2)}) collective-permute-start(f32[192,512]{1,0:T(8,128)S(1)} %get-tuple-element.129), channel_id=1, source_target_pairs={{0,3},{1,0},{2,1},{3,2},{4,7},{5,4},{6,5},{7,6},{8,11},{9,8},{10,9... | collective-permute-start | bytes 1179656 | tf_op jit(solution)/shard_map/ppermute | solution.py:35
  90.8 2.1 %collective-permute-start.20 = (f32[192,512]{1,0:T(8,128)S(1)}, f32[192,512]{1,0:T(8,128)S(1)}, u32[]{:S(2)}, u32[]{:S(2)}) collective-permute-start(f32[192,512]{1,0:T(8,128)S(1)} %get-tuple-element.130), channel_id=1, source_target_pairs={{0,2},{1,3},{2,0},{3,1},{4,6},{5,7},{6,4},{7,5},{8,10},{9,11},{10,... | collective-permute-start | bytes 1179656 | tf_op jit(solution)/shard_map/ppermute | solution.py:35
  92.9 1.2 add_add_fusion
  94.1 4.0 %collective-permute-done.16 = f32[192,512]{1,0:T(8,128)S(1)} collective-permute-done((f32[192,512]{1,0:T(8,128)S(1)}, f32[192,512]{1,0:T(8,128)S(1)}, u32[]{:S(2)}, u32[]{:S(2)}) %collective-permute-start.16) | collective-permute-done | bytes 393248 | tf_op jit(solution)/shard_map/ppermute | solution.py:35
  98.1 1.0 collective-permute-done.15
  99.1 1.2 fusion.9
  100.3 3.1 %collective-permute-start.30 = (f32[64,512]{1,0:T(8,128)S(1)}, f32[64,512]{1,0:T(8,128)S(1)}, u32[]{:S(2)}, u32[]{:S(2)}) collective-permute-start(f32[64,512]{1,0:T(8,128)S(1)} %slice.167), channel_id=1, source_target_pairs={{0,16},{1,17},{2,18},{3,19},{4,20},{5,21},{6,22},{7,23},{8,24},{9,... | collective-permute-start | bytes 393224 | tf_op jit(solution)/shard_map/ppermute | solution.py:35
  103.7 3.4 %collective-permute-start.32 = (f32[64,512]{1,0:T(8,128)S(1)}, f32[64,512]{1,0:T(8,128)S(1)}, u32[]{:S(2)}, u32[]{:S(2)}) collective-permute-start(f32[64,512]{1,0:T(8,128)S(1)} %get-tuple-element.142), channel_id=1, source_target_pairs={{0,48},{1,49},{2,50},{3,51},{4,52},{5,53},{6,54},{7,55},{8,56},{9,... | collective-permute-start | bytes 393224 | tf_op jit(solution)/shard_map/ppermute | solution.py:35
  107.1 3.7 %collective-permute-start.22 = (f32[4,64,512]{2,1,0:T(8,128)S(1)}, f32[4,64,512]{2,1,0:T(8,128)S(1)}, u32[]{:S(2)}, u32[]{:S(2)}) collective-permute-start(f32[4,64,512]{2,1,0:T(8,128)S(1)} %copy-done.24), channel_id=1, source_target_pairs={{0,2},{1,3},{2,0},{3,1},{4,6},{5,7},{6,4},{7,5},{8,10},{9,11},{10,... | collective-permute-start | bytes 1572872 | tf_op jit(solution)/shard_map/ppermute | solution.py:35
  112.0 2.9 %collective-permute-start.33 = (f32[128,512]{1,0:T(8,128)S(1)}, f32[128,512]{1,0:T(8,128)S(1)}, u32[]{:S(2)}, u32[]{:S(2)}) collective-permute-start(f32[128,512]{1,0:T(8,128)S(1)} %pad_maximum_fusion.1), channel_id=1, source_target_pairs={{0,48},{1,49},{2,50},{3,51},{4,52},{5,53},{6,54},{7,55},{8,56},{9,... | collective-permute-start | bytes 786440 | tf_op jit(solution)/shard_map/ppermute | solution.py:35
  114.8 2.5 %collective-permute-done.22 = f32[4,64,512]{2,1,0:T(8,128)S(1)} collective-permute-done((f32[4,64,512]{2,1,0:T(8,128)S(1)}, f32[4,64,512]{2,1,0:T(8,128)S(1)}, u32[]{:S(2)}, u32[]{:S(2)}) %collective-permute-start.22) | collective-permute-done | bytes 524320 | tf_op jit(solution)/shard_map/ppermute | solution.py:35
  118.1 6.5 %collective-permute-start.25 = (f32[64,512]{1,0:T(8,128)S(1)}, f32[64,512]{1,0:T(8,128)S(1)}, u32[]{:S(2)}, u32[]{:S(2)}) collective-permute-start(f32[64,512]{1,0:T(8,128)S(1)} %get-tuple-element.137), channel_id=1, source_target_pairs={{0,12},{1,13},{2,14},{3,15},{4,0},{5,1},{6,2},{7,3},{8,4},{9,5},{1... | collective-permute-start | bytes 393224 | tf_op jit(solution)/shard_map/ppermute | solution.py:35
  124.5 1.9 %collective-permute-start.24 = (f32[64,512]{1,0:T(8,128)S(1)}, f32[64,512]{1,0:T(8,128)S(1)}, u32[]{:S(2)}, u32[]{:S(2)}) collective-permute-start(f32[64,512]{1,0:T(8,128)S(1)} %get-tuple-element.138), channel_id=1, source_target_pairs={{0,8},{1,9},{2,10},{3,11},{4,12},{5,13},{6,14},{7,15},{8,0},{9,1},... | collective-permute-start | bytes 393224 | tf_op jit(solution)/shard_map/ppermute | solution.py:35
  127.3 2.6 %collective-permute-start.29 = (f32[64,512]{1,0:T(8,128)S(1)}, f32[64,512]{1,0:T(8,128)S(1)}, u32[]{:S(2)}, u32[]{:S(2)}) collective-permute-start(f32[64,512]{1,0:T(8,128)S(1)} %get-tuple-element.133), channel_id=1, source_target_pairs={{0,3},{1,0},{2,1},{3,2},{4,7},{5,4},{6,5},{7,6},{8,11},{9,8},{10,9... | collective-permute-start | bytes 393224 | tf_op jit(solution)/shard_map/ppermute | solution.py:35
  130.3 5.0 %collective-permute-start.27 = (f32[64,512]{1,0:T(8,128)S(1)}, f32[64,512]{1,0:T(8,128)S(1)}, u32[]{:S(2)}, u32[]{:S(2)}) collective-permute-start(f32[64,512]{1,0:T(8,128)S(1)} %get-tuple-element.135), channel_id=1, source_target_pairs={{0,1},{1,2},{2,3},{3,0},{4,5},{5,6},{6,7},{7,4},{8,9},{9,10},{10,1... | collective-permute-start | bytes 393224 | tf_op jit(solution)/shard_map/ppermute | solution.py:35
  135.3 2.0 %collective-permute-done.23.refs_1_ = f32[64,512]{1,0:T(8,128)S(1)} collective-permute-done((f32[64,512]{1,0:T(8,128)S(1)}, f32[64,512]{1,0:T(8,128)S(1)}, u32[]{:S(2)}, u32[]{:S(2)}) %collective-permute-start.23) | collective-permute-done | bytes 131104 | tf_op jit(solution)/shard_map/ppermute | solution.py:35
  138.6 3.4 %shard_map.110 = (f32[128,512]{1,0:T(8,128)}, f32[16,512]{1,0:T(8,128)}) custom-call(s32[4]{0:T(128)} %direction_ref.5, f32[64,512]{1,0:T(8,128)} %get-tuple-element.140.refs_0_, f32[64,512]{1,0:T(8,128)} %copy-done.13, f32[64,512]{1,0:T(8,128)} %copy-done.12, f32[64,512]{1,0:T(8,128)} %copy-done.11, f32[64,512]{1,0:T(8,128)} %get-tuple-element.136.refs_4_, ...), custom_call_target="tpu_custom_call" | custom-call | flops 40000000 | bytes 3145728 | tf_op jit(solution)/shard_map/pallas_call | solution.py:378
  142.0 15.5 %collective-permute-start.36 = (f32[16,512]{1,0:T(8,128)}, f32[16,512]{1,0:T(8,128)S(1)}, u32[]{:S(2)}, u32[]{:S(2)}) collective-permute-start(f32[16,512]{1,0:T(8,128)} %get-tuple-element.127), channel_id=1, source_target_pairs={{0,192},{64,0},{128,64},{192,128},{1,193},{65,1},{129,65},{193,129... | collective-permute-start | bytes 98312 | tf_op jit(solution)/shard_map/ppermute | solution.py:385
  159.3 2.8 %shard_map.111.particular_ref = f32[128,512]{1,0:T(8,128)} custom-call(s32[4]{0:T(128)} %direction_ref.5, f32[128,512]{1,0:T(8,128)} %get-tuple-element.128.source_ref, f32[1,512]{1,0:T(1,128)} %bitcast.93, bf16[4,8,128,128]{3,2,1,0:T(8,128)(2,1)} %get-tuple-element.125.refs_10_.high_ref, bf16[4,8,128,128]{3,2,1,0:T(8,128)(2,1)} %get-tuple-element.126.refs_11_.low_ref), custom_call_target="tpu_custom_call" | custom-call | flops 40000000 | bytes 3145728 | tf_op jit(solution)/shard_map/pallas_call | solution.py:387
  162.7 3.5 %shard_map.112 = f32[128,512]{1,0:T(8,128)} custom-call(s32[4]{0:T(128)} %direction_ref.5, s32[1]{0:T(128)} %bitcast.slab_ref, f32[16,512]{1,0:T(8,128)} %select_reduce_fusion.wall_ref, f32[16,512]{1,0:T(8,128)} %copy-done.19, f32[16,512]{1,0:T(8,128)} %copy-done.18, f32[16,512]{1,0:T(8,128)} %copy-done.17, f32[1,512]{1,0:T(1,128)} %bitcast.94, ...), custom_call_target="tpu_custom_call" | custom-call | flops 60000000 | bytes 3145728 | tf_op jit(solution)/shard_map/pallas_call | solution.py:390
  (108 shorter events, 10.7 us)
Async XLA Ops:
  5.1 18.8 %collective-permute-start.4 = (f32[2,192,512]{2,1,0:T(8,128)}, f32[2,192,512]{2,1,0:T(8,128)S(1)}, u32[]{:S(2)}, u32[]{:S(2)}) collective-permute-start(f32[2,192,512]{2,1,0:T(8,128)} %get-tuple-element.74), channel_id=1, source_target_pairs={{0,1},{1,2},{2,3},{3,0},{4,5},{5,6},{6,7},{7,4},{8,9},{9,10},{10,1... | collective-permute-start | bytes 2359304 | tf_op jit(solution)/shard_map/ppermute | solution.py:35
  7.2 18.5 %collective-permute-start.5 = (f32[2,192,512]{2,1,0:T(8,128)}, f32[2,192,512]{2,1,0:T(8,128)S(1)}, u32[]{:S(2)}, u32[]{:S(2)}) collective-permute-start(f32[2,192,512]{2,1,0:T(8,128)} %get-tuple-element.75), channel_id=1, source_target_pairs={{0,3},{1,0},{2,1},{3,2},{4,7},{5,4},{6,5},{7,6},{8,11},{9,8},{10,9... | collective-permute-start | bytes 2359304 | tf_op jit(solution)/shard_map/ppermute | solution.py:35
  8.6 28.2 %collective-permute-start.6 = (f32[2,192,512]{2,1,0:T(8,128)}, f32[2,192,512]{2,1,0:T(8,128)}, u32[]{:S(2)}, u32[]{:S(2)}) collective-permute-start(f32[2,192,512]{2,1,0:T(8,128)} %get-tuple-element.76), channel_id=1, source_target_pairs={{0,4},{1,5},{2,6},{3,7},{4,8},{5,9},{6,10},{7,11},{8,12},{9,13},{1... | collective-permute-start | bytes 2359304 | tf_op jit(solution)/shard_map/ppermute | solution.py:35
  10.0 27.0 %collective-permute-start.7 = (f32[2,192,512]{2,1,0:T(8,128)}, f32[2,192,512]{2,1,0:T(8,128)}, u32[]{:S(2)}, u32[]{:S(2)}) collective-permute-start(f32[2,192,512]{2,1,0:T(8,128)} %get-tuple-element.77), channel_id=1, source_target_pairs={{0,12},{1,13},{2,14},{3,15},{4,0},{5,1},{6,2},{7,3},{8,4},{9,5},{1... | collective-permute-start | bytes 2359304 | tf_op jit(solution)/shard_map/ppermute | solution.py:35
  16.5 27.5 %collective-permute-start = (f32[2,192,512]{2,1,0:T(8,128)}, f32[2,192,512]{2,1,0:T(8,128)S(1)}, u32[]{:S(2)}, u32[]{:S(2)}) collective-permute-start(f32[2,192,512]{2,1,0:T(8,128)} %get-tuple-element.67), channel_id=1, source_target_pairs={{0,3},{1,0},{2,1},{3,2},{4,7},{5,4},{6,5},{7,6},{8,11},{9,8},{10,9... | collective-permute-start | bytes 2359304 | tf_op jit(solution)/shard_map/ppermute | solution.py:35
  23.9 12.9 %copy-start.3 = (f32[2,192,512]{2,1,0:T(8,128)}, f32[2,192,512]{2,1,0:T(8,128)S(1)}, u32[]{:S(2)}) copy-start(f32[2,192,512]{2,1,0:T(8,128)S(1)} %collective-permute-done.4.refs_16_) | copy-start | bytes 2359300
  23.9 21.7 %collective-permute-start.1 = (f32[2,192,512]{2,1,0:T(8,128)}, f32[2,192,512]{2,1,0:T(8,128)S(1)}, u32[]{:S(2)}, u32[]{:S(2)}) collective-permute-start(f32[2,192,512]{2,1,0:T(8,128)} %get-tuple-element.68), channel_id=1, source_target_pairs={{0,1},{1,2},{2,3},{3,0},{4,5},{5,6},{6,7},{7,4},{8,9},{9,10},{10,1... | collective-permute-start | bytes 2359304 | tf_op jit(solution)/shard_map/ppermute | solution.py:35
  26.7 19.0 %collective-permute-start.2 = (f32[2,192,512]{2,1,0:T(8,128)}, f32[2,192,512]{2,1,0:T(8,128)S(1)}, u32[]{:S(2)}, u32[]{:S(2)}) collective-permute-start(f32[2,192,512]{2,1,0:T(8,128)} %get-tuple-element.69), channel_id=1, source_target_pairs={{0,12},{1,13},{2,14},{3,15},{4,0},{5,1},{6,2},{7,3},{8,4},{9,5},{1... | collective-permute-start | bytes 2359304 | tf_op jit(solution)/shard_map/ppermute | solution.py:35
  36.8 17.6 %collective-permute-start.3 = (f32[2,192,512]{2,1,0:T(8,128)}, f32[2,192,512]{2,1,0:T(8,128)S(1)}, u32[]{:S(2)}, u32[]{:S(2)}) collective-permute-start(f32[2,192,512]{2,1,0:T(8,128)} %get-tuple-element.70), channel_id=1, source_target_pairs={{0,4},{1,5},{2,6},{3,7},{4,8},{5,9},{6,10},{7,11},{8,12},{9,13},{1... | collective-permute-start | bytes 2359304 | tf_op jit(solution)/shard_map/ppermute | solution.py:35
  36.9 11.4 %copy-start.25 = (s32[16]{0:T(128)S(1)}, s32[16]{0:T(128)}, u32[]{:S(2)}) copy-start(s32[16]{0:T(128)} %param.21) | copy-start | bytes 196
  37.0 24.2 %collective-permute-start.8 = (f32[4,64,512]{2,1,0:T(8,128)}, f32[4,64,512]{2,1,0:T(8,128)}, u32[]{:S(2)}, u32[]{:S(2)}) collective-permute-start(f32[4,64,512]{2,1,0:T(8,128)} %get-tuple-element.88), channel_id=1, source_target_pairs={{0,1},{1,2},{2,3},{3,0},{4,5},{5,6},{6,7},{7,4},{8,9},{9,10},{10,1... | collective-permute-start | bytes 1572872 | tf_op jit(solution)/shard_map/ppermute | solution.py:35
  44.0 10.4 %copy-start = (f32[2,192,512]{2,1,0:T(8,128)}, f32[2,192,512]{2,1,0:T(8,128)S(1)}, u32[]{:S(2)}) copy-start(f32[2,192,512]{2,1,0:T(8,128)S(1)} %collective-permute-done.refs_16_) | copy-start | bytes 2359300
  44.0 17.4 %collective-permute-start.9 = (f32[4,64,512]{2,1,0:T(8,128)}, f32[4,64,512]{2,1,0:T(8,128)}, u32[]{:S(2)}, u32[]{:S(2)}) collective-permute-start(f32[4,64,512]{2,1,0:T(8,128)} %get-tuple-element.89), channel_id=1, source_target_pairs={{0,3},{1,0},{2,1},{3,2},{4,7},{5,4},{6,5},{7,6},{8,11},{9,8},{10,9... | collective-permute-start | bytes 1572872 | tf_op jit(solution)/shard_map/ppermute | solution.py:35
  45.6 8.8 %copy-start.1 = (f32[2,192,512]{2,1,0:T(8,128)}, f32[2,192,512]{2,1,0:T(8,128)S(1)}, u32[]{:S(2)}) copy-start(f32[2,192,512]{2,1,0:T(8,128)S(1)} %collective-permute-done.1.refs_17_) | copy-start | bytes 2359300
  45.6 25.0 %collective-permute-start.12 = (f32[2,192,512]{2,1,0:T(8,128)}, f32[2,192,512]{2,1,0:T(8,128)}, u32[]{:S(2)}, u32[]{:S(2)}) collective-permute-start(f32[2,192,512]{2,1,0:T(8,128)} %get-tuple-element.105), channel_id=1, source_target_pairs={{0,1},{1,2},{2,3},{3,0},{4,5},{5,6},{6,7},{7,4},{8,9},{9,10},{10,1... | collective-permute-start | bytes 2359304 | tf_op jit(solution)/shard_map/ppermute | solution.py:35
  45.7 8.8 %copy-start.2 = (f32[2,192,512]{2,1,0:T(8,128)}, f32[2,192,512]{2,1,0:T(8,128)S(1)}, u32[]{:S(2)}) copy-start(f32[2,192,512]{2,1,0:T(8,128)S(1)} %collective-permute-done.2.refs_18_) | copy-start | bytes 2359300
  45.7 31.5 %collective-permute-start.14 = (f32[2,192,512]{2,1,0:T(8,128)}, f32[2,192,512]{2,1,0:T(8,128)}, u32[]{:S(2)}, u32[]{:S(2)}) collective-permute-start(f32[2,192,512]{2,1,0:T(8,128)} %get-tuple-element.107), channel_id=1, source_target_pairs={{0,3},{1,0},{2,1},{3,2},{4,7},{5,4},{6,5},{7,6},{8,11},{9,8},{10,9... | collective-permute-start | bytes 2359304 | tf_op jit(solution)/shard_map/ppermute | solution.py:35
  54.4 29.6 %collective-permute-start.10 = (f32[4,64,512]{2,1,0:T(8,128)}, f32[4,64,512]{2,1,0:T(8,128)}, u32[]{:S(2)}, u32[]{:S(2)}) collective-permute-start(f32[4,64,512]{2,1,0:T(8,128)} %get-tuple-element.91), channel_id=1, source_target_pairs={{0,4},{1,5},{2,6},{3,7},{4,8},{5,9},{6,10},{7,11},{8,12},{9,13},{1... | collective-permute-start | bytes 1572872 | tf_op jit(solution)/shard_map/ppermute | solution.py:35
  61.1 31.8 %copy-start.8 = (f32[4,64,512]{2,1,0:T(8,128)S(1)}, f32[4,64,512]{2,1,0:T(8,128)}, u32[]{:S(2)}) copy-start(f32[4,64,512]{2,1,0:T(8,128)} %get-tuple-element.90) | copy-start | bytes 1572868
  61.1 38.0 %copy-start.7 = (f32[2,192,512]{2,1,0:T(8,128)S(1)}, f32[2,192,512]{2,1,0:T(8,128)}, u32[]{:S(2)}) copy-start(f32[2,192,512]{2,1,0:T(8,128)} %get-tuple-element.115) | copy-start | bytes 2359300
  61.1 42.3 %copy-start.6 = (f32[2,192,512]{2,1,0:T(8,128)S(1)}, f32[2,192,512]{2,1,0:T(8,128)}, u32[]{:S(2)}) copy-start(f32[2,192,512]{2,1,0:T(8,128)} %get-tuple-element.120) | copy-start | bytes 2359300
  61.1 21.6 %collective-permute-start.17 = (f32[2,192,512]{2,1,0:T(8,128)}, f32[2,192,512]{2,1,0:T(8,128)S(1)}, u32[]{:S(2)}, u32[]{:S(2)}) collective-permute-start(f32[2,192,512]{2,1,0:T(8,128)} %get-tuple-element.109), channel_id=1, source_target_pairs={{0,4},{1,5},{2,6},{3,7},{4,8},{5,9},{6,10},{7,11},{8,12},{9,13},{1... | collective-permute-start | bytes 2359304 | tf_op jit(solution)/shard_map/ppermute | solution.py:35
  61.5 45.6 %copy-start.24 = (f32[4,64,512]{2,1,0:T(8,128)S(1)}, f32[4,64,512]{2,1,0:T(8,128)}, u32[]{:S(2)}) copy-start(f32[4,64,512]{2,1,0:T(8,128)} %get-tuple-element.112) | copy-start | bytes 1572868
  61.5 49.3 %copy-start.23 = (f32[4,64,512]{2,1,0:T(8,128)S(1)}, f32[4,64,512]{2,1,0:T(8,128)}, u32[]{:S(2)}) copy-start(f32[4,64,512]{2,1,0:T(8,128)} %get-tuple-element.114) | copy-start | bytes 1572868
  61.5 17.3 %collective-permute-start.19 = (f32[2,192,512]{2,1,0:T(8,128)}, f32[2,192,512]{2,1,0:T(8,128)S(1)}, u32[]{:S(2)}, u32[]{:S(2)}) collective-permute-start(f32[2,192,512]{2,1,0:T(8,128)} %get-tuple-element.111), channel_id=1, source_target_pairs={{0,12},{1,13},{2,14},{3,15},{4,0},{5,1},{6,2},{7,3},{8,4},{9,5},{1... | collective-permute-start | bytes 2359304 | tf_op jit(solution)/shard_map/ppermute | solution.py:35
  70.6 17.6 %collective-permute-start.11 = (f32[4,64,512]{2,1,0:T(8,128)}, f32[4,64,512]{2,1,0:T(8,128)S(1)}, u32[]{:S(2)}, u32[]{:S(2)}) collective-permute-start(f32[4,64,512]{2,1,0:T(8,128)} %get-tuple-element.92), channel_id=1, source_target_pairs={{0,12},{1,13},{2,14},{3,15},{4,0},{5,1},{6,2},{7,3},{8,4},{9,5},{1... | collective-permute-start | bytes 1572872 | tf_op jit(solution)/shard_map/ppermute | solution.py:35
  77.1 13.6 %collective-permute-start.13 = (f32[192,512]{1,0:T(8,128)S(1)}, f32[192,512]{1,0:T(8,128)S(1)}, u32[]{:S(2)}, u32[]{:S(2)}) collective-permute-start(f32[192,512]{1,0:T(8,128)S(1)} %fusion.5), channel_id=1, source_target_pairs={{0,4},{1,5},{2,6},{3,7},{4,8},{5,9},{6,10},{7,11},{8,12},{9,13},{1... | collective-permute-start | bytes 1179656 | tf_op jit(solution)/shard_map/ppermute | solution.py:35
  78.7 19.3 %collective-permute-start.16 = (f32[192,512]{1,0:T(8,128)S(1)}, f32[192,512]{1,0:T(8,128)S(1)}, u32[]{:S(2)}, u32[]{:S(2)}) collective-permute-start(f32[192,512]{1,0:T(8,128)S(1)} %get-tuple-element.131), channel_id=1, source_target_pairs={{0,12},{1,13},{2,14},{3,15},{4,0},{5,1},{6,2},{7,3},{8,4},{9,5},{1... | collective-permute-start | bytes 1179656 | tf_op jit(solution)/shard_map/ppermute | solution.py:35
  82.7 16.3 %collective-permute-start.15 = (f32[192,512]{1,0:T(8,128)S(1)}, f32[192,512]{1,0:T(8,128)S(1)}, u32[]{:S(2)}, u32[]{:S(2)}) collective-permute-start(f32[192,512]{1,0:T(8,128)S(1)} %get-tuple-element.132), channel_id=1, source_target_pairs={{0,8},{1,9},{2,10},{3,11},{4,12},{5,13},{6,14},{7,15},{8,0},{9,1},... | collective-permute-start | bytes 1179656 | tf_op jit(solution)/shard_map/ppermute | solution.py:35
  84.0 19.4 %collective-permute-start.18 = (f32[192,512]{1,0:T(8,128)S(1)}, f32[192,512]{1,0:T(8,128)S(1)}, u32[]{:S(2)}, u32[]{:S(2)}) collective-permute-start(f32[192,512]{1,0:T(8,128)S(1)} %fusion.2), channel_id=1, source_target_pairs={{0,1},{1,2},{2,3},{3,0},{4,5},{5,6},{6,7},{7,4},{8,9},{9,10},{10,1... | collective-permute-start | bytes 1179656 | tf_op jit(solution)/shard_map/ppermute | solution.py:35
  88.2 15.2 %collective-permute-start.21 = (f32[192,512]{1,0:T(8,128)S(1)}, f32[192,512]{1,0:T(8,128)S(1)}, u32[]{:S(2)}, u32[]{:S(2)}) collective-permute-start(f32[192,512]{1,0:T(8,128)S(1)} %get-tuple-element.129), channel_id=1, source_target_pairs={{0,3},{1,0},{2,1},{3,2},{4,7},{5,4},{6,5},{7,6},{8,11},{9,8},{10,9... | collective-permute-start | bytes 1179656 | tf_op jit(solution)/shard_map/ppermute | solution.py:35
  90.8 12.6 %collective-permute-start.20 = (f32[192,512]{1,0:T(8,128)S(1)}, f32[192,512]{1,0:T(8,128)S(1)}, u32[]{:S(2)}, u32[]{:S(2)}) collective-permute-start(f32[192,512]{1,0:T(8,128)S(1)} %get-tuple-element.130), channel_id=1, source_target_pairs={{0,2},{1,3},{2,0},{3,1},{4,6},{5,7},{6,4},{7,5},{8,10},{9,11},{10,... | collective-permute-start | bytes 1179656 | tf_op jit(solution)/shard_map/ppermute | solution.py:35
  100.3 10.5 %collective-permute-start.30 = (f32[64,512]{1,0:T(8,128)S(1)}, f32[64,512]{1,0:T(8,128)S(1)}, u32[]{:S(2)}, u32[]{:S(2)}) collective-permute-start(f32[64,512]{1,0:T(8,128)S(1)} %slice.167), channel_id=1, source_target_pairs={{0,16},{1,17},{2,18},{3,19},{4,20},{5,21},{6,22},{7,23},{8,24},{9,... | collective-permute-start | bytes 393224 | tf_op jit(solution)/shard_map/ppermute | solution.py:35
  103.7 8.3 %collective-permute-start.32 = (f32[64,512]{1,0:T(8,128)S(1)}, f32[64,512]{1,0:T(8,128)S(1)}, u32[]{:S(2)}, u32[]{:S(2)}) collective-permute-start(f32[64,512]{1,0:T(8,128)S(1)} %get-tuple-element.142), channel_id=1, source_target_pairs={{0,48},{1,49},{2,50},{3,51},{4,52},{5,53},{6,54},{7,55},{8,56},{9,... | collective-permute-start | bytes 393224 | tf_op jit(solution)/shard_map/ppermute | solution.py:35
  107.1 10.3 %collective-permute-start.22 = (f32[4,64,512]{2,1,0:T(8,128)S(1)}, f32[4,64,512]{2,1,0:T(8,128)S(1)}, u32[]{:S(2)}, u32[]{:S(2)}) collective-permute-start(f32[4,64,512]{2,1,0:T(8,128)S(1)} %copy-done.24), channel_id=1, source_target_pairs={{0,2},{1,3},{2,0},{3,1},{4,6},{5,7},{6,4},{7,5},{8,10},{9,11},{10,... | collective-permute-start | bytes 1572872 | tf_op jit(solution)/shard_map/ppermute | solution.py:35
  110.8 15.7 %collective-permute-start.26 = (f32[4,64,512]{2,1,0:T(8,128)S(1)}, f32[4,64,512]{2,1,0:T(8,128)S(1)}, u32[]{:S(2)}, u32[]{:S(2)}) collective-permute-start(f32[4,64,512]{2,1,0:T(8,128)S(1)} %copy-done.23), channel_id=1, source_target_pairs={{0,8},{1,9},{2,10},{3,11},{4,12},{5,13},{6,14},{7,15},{8,0},{9,1},... | collective-permute-start | bytes 1572872 | tf_op jit(solution)/shard_map/ppermute | solution.py:35
  110.8 16.4 %collective-permute-start.31 = (f32[128,512]{1,0:T(8,128)S(1)}, f32[128,512]{1,0:T(8,128)S(1)}, u32[]{:S(2)}, u32[]{:S(2)}) collective-permute-start(f32[128,512]{1,0:T(8,128)S(1)} %pad_maximum_fusion), channel_id=1, source_target_pairs={{0,16},{1,17},{2,18},{3,19},{4,20},{5,21},{6,22},{7,23},{8,24},{9,... | collective-permute-start | bytes 786440 | tf_op jit(solution)/shard_map/ppermute | solution.py:35
  112.0 17.9 %collective-permute-start.33 = (f32[128,512]{1,0:T(8,128)S(1)}, f32[128,512]{1,0:T(8,128)S(1)}, u32[]{:S(2)}, u32[]{:S(2)}) collective-permute-start(f32[128,512]{1,0:T(8,128)S(1)} %pad_maximum_fusion.1), channel_id=1, source_target_pairs={{0,48},{1,49},{2,50},{3,51},{4,52},{5,53},{6,54},{7,55},{8,56},{9,... | collective-permute-start | bytes 786440 | tf_op jit(solution)/shard_map/ppermute | solution.py:35
  118.1 12.2 %collective-permute-start.25 = (f32[64,512]{1,0:T(8,128)S(1)}, f32[64,512]{1,0:T(8,128)S(1)}, u32[]{:S(2)}, u32[]{:S(2)}) collective-permute-start(f32[64,512]{1,0:T(8,128)S(1)} %get-tuple-element.137), channel_id=1, source_target_pairs={{0,12},{1,13},{2,14},{3,15},{4,0},{5,1},{6,2},{7,3},{8,4},{9,5},{1... | collective-permute-start | bytes 393224 | tf_op jit(solution)/shard_map/ppermute | solution.py:35
  124.5 10.8 %collective-permute-start.24 = (f32[64,512]{1,0:T(8,128)S(1)}, f32[64,512]{1,0:T(8,128)S(1)}, u32[]{:S(2)}, u32[]{:S(2)}) collective-permute-start(f32[64,512]{1,0:T(8,128)S(1)} %get-tuple-element.138), channel_id=1, source_target_pairs={{0,8},{1,9},{2,10},{3,11},{4,12},{5,13},{6,14},{7,15},{8,0},{9,1},... | collective-permute-start | bytes 393224 | tf_op jit(solution)/shard_map/ppermute | solution.py:35
  126.4 10.8 %collective-permute-start.23 = (f32[64,512]{1,0:T(8,128)S(1)}, f32[64,512]{1,0:T(8,128)S(1)}, u32[]{:S(2)}, u32[]{:S(2)}) collective-permute-start(f32[64,512]{1,0:T(8,128)S(1)} %get-tuple-element.139), channel_id=1, source_target_pairs={{0,4},{1,5},{2,6},{3,7},{4,8},{5,9},{6,10},{7,11},{8,12},{9,13},{1... | collective-permute-start | bytes 393224 | tf_op jit(solution)/shard_map/ppermute | solution.py:35
  127.3 10.7 %copy-start.9 = (f32[128,512]{1,0:T(8,128)}, f32[128,512]{1,0:T(8,128)S(1)}, u32[]{:S(2)}) copy-start(f32[128,512]{1,0:T(8,128)S(1)} %collective-permute-done.31.refs_8_) | copy-start | bytes 786436
  127.3 10.1 %collective-permute-start.29 = (f32[64,512]{1,0:T(8,128)S(1)}, f32[64,512]{1,0:T(8,128)S(1)}, u32[]{:S(2)}, u32[]{:S(2)}) collective-permute-start(f32[64,512]{1,0:T(8,128)S(1)} %get-tuple-element.133), channel_id=1, source_target_pairs={{0,3},{1,0},{2,1},{3,2},{4,7},{5,4},{6,5},{7,6},{8,11},{9,8},{10,9... | collective-permute-start | bytes 393224 | tf_op jit(solution)/shard_map/ppermute | solution.py:35
  129.9 7.5 %collective-permute-start.28 = (f32[64,512]{1,0:T(8,128)S(1)}, f32[64,512]{1,0:T(8,128)S(1)}, u32[]{:S(2)}, u32[]{:S(2)}) collective-permute-start(f32[64,512]{1,0:T(8,128)S(1)} %get-tuple-element.134), channel_id=1, source_target_pairs={{0,2},{1,3},{2,0},{3,1},{4,6},{5,7},{6,4},{7,5},{8,10},{9,11},{10,... | collective-permute-start | bytes 393224 | tf_op jit(solution)/shard_map/ppermute | solution.py:35
  130.3 7.6 %collective-permute-start.27 = (f32[64,512]{1,0:T(8,128)S(1)}, f32[64,512]{1,0:T(8,128)S(1)}, u32[]{:S(2)}, u32[]{:S(2)}) collective-permute-start(f32[64,512]{1,0:T(8,128)S(1)} %get-tuple-element.135), channel_id=1, source_target_pairs={{0,1},{1,2},{2,3},{3,0},{4,5},{5,6},{6,7},{7,4},{8,9},{9,10},{10,1... | collective-permute-start | bytes 393224 | tf_op jit(solution)/shard_map/ppermute | solution.py:35
  142.0 20.1 %collective-permute-start.36 = (f32[16,512]{1,0:T(8,128)}, f32[16,512]{1,0:T(8,128)S(1)}, u32[]{:S(2)}, u32[]{:S(2)}) collective-permute-start(f32[16,512]{1,0:T(8,128)} %get-tuple-element.127), channel_id=1, source_target_pairs={{0,192},{64,0},{128,64},{192,128},{1,193},{65,1},{129,65},{193,129... | collective-permute-start | bytes 98312 | tf_op jit(solution)/shard_map/ppermute | solution.py:385
  157.5 4.5 %collective-permute-start.35 = (f32[16,512]{1,0:T(8,128)}, f32[16,512]{1,0:T(8,128)S(1)}, u32[]{:S(2)}, u32[]{:S(2)}) collective-permute-start(f32[16,512]{1,0:T(8,128)} %get-tuple-element.127), channel_id=1, source_target_pairs={{0,128},{64,192},{128,0},{192,64},{1,129},{65,193},{129,1},{193,65... | collective-permute-start | bytes 98312 | tf_op jit(solution)/shard_map/ppermute | solution.py:385
  158.3 3.8 %collective-permute-start.34 = (f32[16,512]{1,0:T(8,128)}, f32[16,512]{1,0:T(8,128)S(1)}, u32[]{:S(2)}, u32[]{:S(2)}) collective-permute-start(f32[16,512]{1,0:T(8,128)} %get-tuple-element.127), channel_id=1, source_target_pairs={{0,64},{64,128},{128,192},{192,0},{1,65},{65,129},{129,193},{193,1... | collective-permute-start | bytes 98312 | tf_op jit(solution)/shard_map/ppermute | solution.py:385
  (15 other events, 49.2 us)

commit v5 on v4

--- a/solution.py
+++ b/solution.py
@@ -87,7 +87,7 @@
             n += 1
 
 
-def partial_sums(jobs, units, addends, place, pattern, prior, weights, slope, coupling):
+def partial_sums(jobs, units, addends, place, pattern, prior, weights, slope, coupling, room=28 << 20):
     segments = [segment for job in jobs for segment in job]
     slope_specs = [
         pl.BlockSpec(
@@ -128,6 +128,7 @@
             bytes_accessed=sum(heights) * units * WIDTH * 6,
             transcendentals=0,
         ),
+        compiler_params=pltpu.CompilerParams(vmem_limit_bytes=room),
         name="partial_sums",
     )(
         place,
@@ -227,10 +228,11 @@
         for b in range(SHELL):
             lanes = pl.ds(b * BLK, BLK)
             up = direction_ref[b] == 1
-            k = jnp.where(up, 2 - n, n)
+            there = jnp.where(up, n, 3 - n)
             active = jnp.where(
-                up, (k + 1 <= slab).astype(jnp.int32), (k + 1 > slab).astype(jnp.int32)
-            )
+                up, (there < slab).astype(jnp.int32), (there > slab).astype(jnp.int32)
+            )
+            k = jnp.maximum((there ^ slab) - 1, 0)
             moved = faces[k, :, lanes] + product(
                 now[b] * rate_ref[:, lanes], high_ref[b, LAYERS - 1], low_ref[b, LAYERS - 1]
             )
@@ -263,6 +265,7 @@
         out_shape=[jax.ShapeDtypeStruct(*out) for out in outs],
         scratch_shapes=list(scratch),
         cost_estimate=pl.CostEstimate(flops=flops, bytes_accessed=3 << 20, transcendentals=0),
+        compiler_params=pltpu.CompilerParams(vmem_limit_bytes=16 << 20),
     )
 
 
@@ -293,7 +296,7 @@
         coupling=coupling,
     )
 
-    def ring_sums(low_step, high_step, prior, addends=()):
+    def ring_sums(low_step, high_step, prior, addends=(), **room):
         jobs = [
             (
                 (0, CELL, 1 if upper else 3, upper, pair, step),
@@ -302,7 +305,7 @@
             for upper in (True, False)
             for pair, step in ((0, low_step), (2, high_step))
         ]
-        return make(tuple(jobs), 2, addends, prior=prior)
+        return make(tuple(jobs), 2, addends, prior=prior, **room)
 
     def ring(blocks, step):
         axes = (2, 2, 1, 1)
@@ -320,7 +323,7 @@
     inflow = jnp.where(ahead, inflow_low, inflow_high)
     wall = jnp.sum(jnp.where(picks[:, :, None], inflow[None, :, :], 0.0), axis=1)
 
-    far_got = ring(ring_sums(2, 2, prior), 1)
+    far_got = ring(ring_sums(2, 2, prior, room=62 << 20), 1)
     direct = ring_sums(3, 1, prior)
     early = ring(direct, -1)
     after, _ = lax.optimization_barrier((prior, direct))
@@ -382,7 +385,7 @@
         flops=40_000_000,
     )(direction, *halves, from_below, from_above, high, low)
     faces = [
-        lax.ppermute(last, "slab", [(i, (i + k) % 4) for i in range(4)]) for k in (1, 2, 3)
+        lax.ppermute(last, "slab", [(i, i ^ k) for i in range(4)]) for k in (1, 2, 3)
     ]
     (particular,) = small_call(
         particular_kernel, [whole], [SMEM, VMEM, VMEM, FIRST, FIRST], flops=40_000_000, grid=(1,)

time: 167 us -> 150 us (0.90)
  waiting for transfers between devices: 27 us -> 50.4 us
  Pallas kernels: 42.9 us -> 23.8 us
  starting transfers between devices: 81.4 us -> 70.5 us
  other arithmetic: 11.3 us -> 1.43 us
    ppermute x34, waiting for transfers between devices: 27 us -> 49.6 us  [send(): return lax.ppermute(block, 'modes', route(axis, step))]
    pallas_call x5, Pallas kernels: 28.9 us -> 16.5 us  [partial_sums(): pl.pallas_call(functools.partial(partial_kernel, jobs, len(addends)), gri...]
    ppermute x3, starting transfers between devices: 17.2 us -> 10.4 us  [per_device(): lax.ppermute(last, 'slab', [(i, i ^ k) for i in range(4)])]
    ppermute x34, starting transfers between devices: 64.2 us -> 60.1 us  [send(): return lax.ppermute(block, 'modes', route(axis, step))]
    pallas_call x1, Pallas kernels: 3.42 us -> 1.23 us  [per_device(): small_call(last_kernel, [whole, ((LATERAL, WIDTH), jnp.float32)], [SMEM]...]
    pallas_call x1, Pallas kernels: 4.3 us -> 2.23 us  [per_device(): small_call(powers_kernel, split, [VMEM, VMEM], flops=200000000)]
    unnamed x52 -> x22, local copies, waits for them, and re-layouts: 3.05 us -> 3.42 us
  transfers between devices with their start and end apart: 37 -> 37, of which waited for: 11 -> 16; matrix products, arithmetic and copies ran while one was open for 7% -> 1% of each run, Pallas kernels for 19% -> 10%
where the time goes in v5:
time: 150 us
  starting transfers between devices  70.5 us (47%)
  waiting for transfers between devices  50.4 us (34%)
  Pallas kernels  23.8 us (16%)
  local copies, waits for them, and re-layouts  3.52 us (2%)
    ppermute x34, starting transfers between devices, send(): return lax.ppermute(block, 'modes', route(axis, step))  60.1 us
    ppermute x34, waiting for transfers between devices, send(): return lax.ppermute(block, 'modes', route(axis, step))  49.6 us
    pallas_call x5, Pallas kernels, partial_sums(): pl.pallas_call(functools.partial(partial_kernel, jobs, len(addends)), gri...  16.5 us
    ppermute x3, starting transfers between devices, per_device(): lax.ppermute(last, 'slab', [(i, i ^ k) for i in range(4)])  10.4 us
    unnamed x22, local copies, waits for them, and re-layouts  3.42 us
  transfers between devices with their start and end apart: 37, of which 16 were waited for; matrix products, arithmetic and copies ran while one was open for 1% of the time, Pallas kernels for 10%

profile of v5, /device:TPU:1, one launch (start us, length us, event | category | flops | bytes accessed | tf_op | source)
XLA Modules:
  0.0 150.1 jit_solution(15590616989037160727)
XLA Ops:
  0.0 5.2 %partial_sums.6 = (f32[2,192,512]{2,1,0:T(8,128)}, f32[2,192,512]{2,1,0:T(8,128)}, f32[2,192,512]{2,1,0:T(8,128)}, f32[2,192,512]{2,1,0:T(8,128)}) custom-call(s32[1]{0:T(128)} %bitcast.1.place_ref, s32[4,64]{1,0:T(4,128)} %pattern_ref.9, f32[128,512]{1,0:T(8,128)} %x_ref.8, f32[1,512]{1,0:T(1,128)} %bitcast.87, f32[64,1,512]{2,1,0:T(1,128)} %bitcast.47, ...), custom_call_target="tpu_custom_call" | custom-call | flops 201326592 | bytes 4718592 | tf_op jit(solution)/shard_map/partial_sums/pallas_call | solution.py:107
  5.3 2.1 %collective-permute-start.4 = (f32[2,192,512]{2,1,0:T(8,128)}, f32[2,192,512]{2,1,0:T(8,128)S(1)}, u32[]{:S(2)}, u32[]{:S(2)}) collective-permute-start(f32[2,192,512]{2,1,0:T(8,128)} %get-tuple-element.74), channel_id=1, source_target_pairs={{0,1},{1,2},{2,3},{3,0},{4,5},{5,6},{6,7},{7,4},{8,9},{9,10},{10,1... | collective-permute-start | bytes 2359304 | tf_op jit(solution)/shard_map/ppermute | solution.py:35
  7.4 1.4 collective-permute-start.5
  8.7 1.4 collective-permute-start.6
  10.1 1.4 collective-permute-start.7
  11.6 3.4 %copy-done = bf16[4,64,128,128]{3,2,1,0:T(8,128)(2,1)S(1)} copy-done((bf16[4,64,128,128]{3,2,1,0:T(8,128)(2,1)S(1)}, bf16[4,64,128,128]{3,2,1,0:T(8,128)(2,1)}, u32[]{:S(2)}) %copy-start) | copy-done | bytes 8388632
  15.0 2.5 %partial_sums.5 = (f32[2,192,512]{2,1,0:T(8,128)S(1)}, f32[2,192,512]{2,1,0:T(8,128)S(1)}, f32[2,192,512]{2,1,0:T(8,128)S(1)}, f32[2,192,512]{2,1,0:T(8,128)S(1)}) custom-call(s32[1]{0:T(128)} %bitcast.1.place_ref, s32[4,64]{1,0:T(4,128)S(1)} %copy-done.3, f32[128,512]{1,0:T(8,128)S(1)} %copy-done.2, f32[1,512]{1,0:T(1,128)S(1)} %bitcast.88, ...), custom_call_target="tpu_custom_call" | custom-call | flops 201326592 | bytes 4718592 | tf_op jit(solution)/shard_map/partial_sums/pallas_call | solution.py:107
  17.4 1.4 collective-permute-start
  18.8 5.2 %collective-permute-done.4.refs_16_ = f32[2,192,512]{2,1,0:T(8,128)S(1)} collective-permute-done((f32[2,192,512]{2,1,0:T(8,128)}, f32[2,192,512]{2,1,0:T(8,128)S(1)}, u32[]{:S(2)}, u32[]{:S(2)}) %collective-permute-start.4) | collective-permute-done | bytes 786464 | tf_op jit(solution)/shard_map/ppermute | solution.py:35
  23.9 1.9 %collective-permute-start.1 = (f32[2,192,512]{2,1,0:T(8,128)S(1)}, f32[2,192,512]{2,1,0:T(8,128)S(1)}, u32[]{:S(2)}, u32[]{:S(2)}) collective-permute-start(f32[2,192,512]{2,1,0:T(8,128)S(1)} %get-tuple-element.68), channel_id=1, source_target_pairs={{0,1},{1,2},{2,3},{3,0},{4,5},{5,6},{6,7},{7,4},{8,9},{9,10},{10,1... | collective-permute-start | bytes 2359304 | tf_op jit(solution)/shard_map/ppermute | solution.py:35
  25.8 2.9 %collective-permute-start.2 = (f32[2,192,512]{2,1,0:T(8,128)S(1)}, f32[2,192,512]{2,1,0:T(8,128)S(1)}, u32[]{:S(2)}, u32[]{:S(2)}) collective-permute-start(f32[2,192,512]{2,1,0:T(8,128)S(1)} %get-tuple-element.69), channel_id=1, source_target_pairs={{0,12},{1,13},{2,14},{3,15},{4,0},{5,1},{6,2},{7,3},{8,4},{9,5},{1... | collective-permute-start | bytes 2359304 | tf_op jit(solution)/shard_map/ppermute | solution.py:35
  28.7 3.4 %partial_sums.7 = (f32[4,64,512]{2,1,0:T(8,128)S(1)}, f32[4,64,512]{2,1,0:T(8,128)S(1)}, f32[4,64,512]{2,1,0:T(8,128)S(1)}, f32[4,64,512]{2,1,0:T(8,128)S(1)}, f...) custom-call(s32[1]{0:T(128)} %bitcast.1.place_ref, ...), custom_call_target="tpu_custom_call" | custom-call | flops 268435456 | bytes 6291456 | tf_op jit(solution)/shard_map/partial_sums/pallas_call | solution.py:107
  32.4 1.3 collective-permute-start.8
  33.7 2.7 %partial_sums.9 = (f32[2,192,512]{2,1,0:T(8,128)S(1)}, f32[2,192,512]{2,1,0:T(8,128)S(1)}, f32[2,192,512]{2,1,0:T(8,128)S(1)}, f32[2,192,512]{2,1,0:T(8,128)S(1)}) custom-call(s32[1]{0:T(128)} %bitcast.1.place_ref, s32[4,64]{1,0:T(4,128)S(1)} %copy-done.3, f32[128,512]{1,0:T(8,128)S(1)} %copy-done.2, f32[1,512]{1,0:T(1,128)S(1)} %bitcast.90, ...), custom_call_target="tpu_custom_call" | custom-call | flops 201326592 | bytes 4718592 | tf_op jit(solution)/shard_map/partial_sums/pallas_call | solution.py:107
  36.4 5.9 %collective-permute-done.refs_16_ = f32[2,192,512]{2,1,0:T(8,128)S(1)} collective-permute-done((f32[2,192,512]{2,1,0:T(8,128)S(1)}, f32[2,192,512]{2,1,0:T(8,128)S(1)}, u32[]{:S(2)}, u32[]{:S(2)}) %collective-permute-start) | collective-permute-done | bytes 786464 | tf_op jit(solution)/shard_map/ppermute | solution.py:35
  42.3 1.1 collective-permute-start.9
  43.8 2.5 %collective-permute-start.14 = (f32[2,192,512]{2,1,0:T(8,128)S(1)}, f32[2,192,512]{2,1,0:T(8,128)S(1)}, u32[]{:S(2)}, u32[]{:S(2)}) collective-permute-start(f32[2,192,512]{2,1,0:T(8,128)S(1)} %get-tuple-element.107), channel_id=1, source_target_pairs={{0,3},{1,0},{2,1},{3,2},{4,7},{5,4},{6,5},{7,6},{8,11},{9,8},{10,9... | collective-permute-start | bytes 2359304 | tf_op jit(solution)/shard_map/ppermute | solution.py:35
  46.4 2.2 %shard_map.109 = (bf16[4,8,128,128]{3,2,1,0:T(8,128)(2,1)S(1)}, bf16[4,8,128,128]{3,2,1,0:T(8,128)(2,1)S(1)}) custom-call(f32[1,512]{1,0:T(1,128)S(1)} %bitcast.92, f32[4,128,128]{2,1,0:T(8,128)S(1)} %copy-done.7), custom_call_target="tpu_custom_call" | custom-call | flops 200000000 | bytes 3145728 | tf_op jit(solution)/shard_map/pallas_call | solution.py:320
  49.4 2.6 %collective-permute-start.10 = (f32[4,64,512]{2,1,0:T(8,128)S(1)}, f32[4,64,512]{2,1,0:T(8,128)S(1)}, u32[]{:S(2)}, u32[]{:S(2)}) collective-permute-start(f32[4,64,512]{2,1,0:T(8,128)S(1)} %get-tuple-element.91), channel_id=1, source_target_pairs={{0,4},{1,5},{2,6},{3,7},{4,8},{5,9},{6,10},{7,11},{8,12},{9,13},{1... | collective-permute-start | bytes 1572872 | tf_op jit(solution)/shard_map/ppermute | solution.py:35
  51.9 2.7 %partial_sums.8 = (f32[2,192,512]{2,1,0:T(8,128)S(1)}, f32[2,192,512]{2,1,0:T(8,128)S(1)}, f32[2,192,512]{2,1,0:T(8,128)S(1)}, f32[2,192,512]{2,1,0:T(8,128)S(1)}) custom-call(s32[1]{0:T(128)} %bitcast.1.place_ref, s32[4,64]{1,0:T(4,128)S(1)} %copy-done.3, f32[128,512]{1,0:T(8,128)S(1)} %copy-done.2, f32[1,512]{1,0:T(1,128)S(1)} %bitcast.91, ...), custom_call_target="tpu_custom_call" | custom-call | flops 201326592 | bytes 4718592 | tf_op jit(solution)/shard_map/partial_sums/pallas_call | solution.py:107
  54.6 2.7 %collective-permute-start.17 = (f32[2,192,512]{2,1,0:T(8,128)S(1)}, f32[2,192,512]{2,1,0:T(8,128)S(1)}, u32[]{:S(2)}, u32[]{:S(2)}) collective-permute-start(f32[2,192,512]{2,1,0:T(8,128)S(1)} %get-tuple-element.109), channel_id=1, source_target_pairs={{0,4},{1,5},{2,6},{3,7},{4,8},{5,9},{6,10},{7,11},{8,12},{9,13},{1... | collective-permute-start | bytes 2359304 | tf_op jit(solution)/shard_map/ppermute | solution.py:35
  57.3 1.4 collective-permute-start.19
  58.9 11.3 %collective-permute-done.12 = f32[2,192,512]{2,1,0:T(8,128)S(1)} collective-permute-done((f32[2,192,512]{2,1,0:T(8,128)S(1)}, f32[2,192,512]{2,1,0:T(8,128)S(1)}, u32[]{:S(2)}, u32[]{:S(2)}) %collective-permute-start.12) | collective-permute-done | bytes 786464 | tf_op jit(solution)/shard_map/ppermute | solution.py:35
  70.3 5.3 %collective-permute-start.11 = (f32[4,64,512]{2,1,0:T(8,128)S(1)}, f32[4,64,512]{2,1,0:T(8,128)S(1)}, u32[]{:S(2)}, u32[]{:S(2)}) collective-permute-start(f32[4,64,512]{2,1,0:T(8,128)S(1)} %get-tuple-element.92), channel_id=1, source_target_pairs={{0,12},{1,13},{2,14},{3,15},{4,0},{5,1},{6,2},{7,3},{8,4},{9,5},{1... | collective-permute-start | bytes 1572872 | tf_op jit(solution)/shard_map/ppermute | solution.py:35
  75.9 2.7 %collective-permute-start.16 = (f32[192,512]{1,0:T(8,128)S(1)}, f32[192,512]{1,0:T(8,128)S(1)}, u32[]{:S(2)}, u32[]{:S(2)}) collective-permute-start(f32[192,512]{1,0:T(8,128)S(1)} %get-tuple-element.131), channel_id=1, source_target_pairs={{0,12},{1,13},{2,14},{3,15},{4,0},{5,1},{6,2},{7,3},{8,4},{9,5},{1... | collective-permute-start | bytes 1179656 | tf_op jit(solution)/shard_map/ppermute | solution.py:35
  79.6 7.0 %collective-permute-done.11 = f32[4,64,512]{2,1,0:T(8,128)S(1)} collective-permute-done((f32[4,64,512]{2,1,0:T(8,128)S(1)}, f32[4,64,512]{2,1,0:T(8,128)S(1)}, u32[]{:S(2)}, u32[]{:S(2)}) %collective-permute-start.11) | collective-permute-done | bytes 524320 | tf_op jit(solution)/shard_map/ppermute | solution.py:35
  86.6 0.8 collective-permute-start.21
  87.4 1.4 collective-permute-done.13
  89.6 5.5 %collective-permute-done.16 = f32[192,512]{1,0:T(8,128)S(1)} collective-permute-done((f32[192,512]{1,0:T(8,128)S(1)}, f32[192,512]{1,0:T(8,128)S(1)}, u32[]{:S(2)}, u32[]{:S(2)}) %collective-permute-start.16) | collective-permute-done | bytes 393248 | tf_op jit(solution)/shard_map/ppermute | solution.py:35
  95.8 3.1 %collective-permute-start.30 = (f32[64,512]{1,0:T(8,128)S(1)}, f32[64,512]{1,0:T(8,128)S(1)}, u32[]{:S(2)}, u32[]{:S(2)}) collective-permute-start(f32[64,512]{1,0:T(8,128)S(1)} %slice.167), channel_id=1, source_target_pairs={{0,16},{1,17},{2,18},{3,19},{4,20},{5,21},{6,22},{7,23},{8,24},{9,... | collective-permute-start | bytes 393224 | tf_op jit(solution)/shard_map/ppermute | solution.py:35
  98.8 1.5 %collective-permute-done.20 = f32[192,512]{1,0:T(8,128)S(1)} collective-permute-done((f32[192,512]{1,0:T(8,128)S(1)}, f32[192,512]{1,0:T(8,128)S(1)}, u32[]{:S(2)}, u32[]{:S(2)}) %collective-permute-start.20) | collective-permute-done | bytes 393248 | tf_op jit(solution)/shard_map/ppermute | solution.py:35
  100.6 6.1 %collective-permute-start.32 = (f32[64,512]{1,0:T(8,128)S(1)}, f32[64,512]{1,0:T(8,128)S(1)}, u32[]{:S(2)}, u32[]{:S(2)}) collective-permute-start(f32[64,512]{1,0:T(8,128)S(1)} %get-tuple-element.142), channel_id=1, source_target_pairs={{0,48},{1,49},{2,50},{3,51},{4,52},{5,53},{6,54},{7,55},{8,56},{9,... | collective-permute-start | bytes 393224 | tf_op jit(solution)/shard_map/ppermute | solution.py:35
  106.7 1.1 collective-permute-start.22
  108.0 2.0 %collective-permute-done.32 = f32[64,512]{1,0:T(8,128)S(1)} collective-permute-done((f32[64,512]{1,0:T(8,128)S(1)}, f32[64,512]{1,0:T(8,128)S(1)}, u32[]{:S(2)}, u32[]{:S(2)}) %collective-permute-start.32) | collective-permute-done | bytes 131104 | tf_op jit(solution)/shard_map/ppermute | solution.py:35
  110.0 4.1 %collective-permute-start.33 = (f32[128,512]{1,0:T(8,128)S(1)}, f32[128,512]{1,0:T(8,128)S(1)}, u32[]{:S(2)}, u32[]{:S(2)}) collective-permute-start(f32[128,512]{1,0:T(8,128)S(1)} %pad_maximum_fusion.1), channel_id=1, source_target_pairs={{0,48},{1,49},{2,50},{3,51},{4,52},{5,53},{6,54},{7,55},{8,56},{9,... | collective-permute-start | bytes 786440 | tf_op jit(solution)/shard_map/ppermute | solution.py:35
  114.1 2.1 %collective-permute-done.22 = f32[4,64,512]{2,1,0:T(8,128)S(1)} collective-permute-done((f32[4,64,512]{2,1,0:T(8,128)S(1)}, f32[4,64,512]{2,1,0:T(8,128)S(1)}, u32[]{:S(2)}, u32[]{:S(2)}) %collective-permute-start.22) | collective-permute-done | bytes 524320 | tf_op jit(solution)/shard_map/ppermute | solution.py:35
  116.3 8.7 %collective-permute-start.25 = (f32[64,512]{1,0:T(8,128)S(1)}, f32[64,512]{1,0:T(8,128)S(1)}, u32[]{:S(2)}, u32[]{:S(2)}) collective-permute-start(f32[64,512]{1,0:T(8,128)S(1)} %get-tuple-element.137), channel_id=1, source_target_pairs={{0,12},{1,13},{2,14},{3,15},{4,0},{5,1},{6,2},{7,3},{8,4},{9,5},{1... | collective-permute-start | bytes 393224 | tf_op jit(solution)/shard_map/ppermute | solution.py:35
  125.0 1.2 collective-permute-start.24
  126.4 0.8 collective-permute-start.28
  127.2 1.1 collective-permute-done.25.refs_3_
  128.3 3.2 %collective-permute-done.24.refs_2_ = f32[64,512]{1,0:T(8,128)S(1)} collective-permute-done((f32[64,512]{1,0:T(8,128)S(1)}, f32[64,512]{1,0:T(8,128)S(1)}, u32[]{:S(2)}, u32[]{:S(2)}) %collective-permute-start.24) | collective-permute-done | bytes 131104 | tf_op jit(solution)/shard_map/ppermute | solution.py:35
  131.6 1.3 collective-permute-done.23.refs_1_
  133.7 1.2 shard_map.110
  134.9 9.6 %collective-permute-start.36 = (f32[16,512]{1,0:T(8,128)S(1)}, f32[16,512]{1,0:T(8,128)S(1)}, u32[]{:S(2)}, u32[]{:S(2)}) collective-permute-start(f32[16,512]{1,0:T(8,128)S(1)} %get-tuple-element.127), channel_id=1, source_target_pairs={{0,192},{64,128},{128,64},{192,0},{1,193},{65,129},{129,65},{193,1... | collective-permute-start | bytes 98312 | tf_op jit(solution)/shard_map/ppermute | solution.py:388
  144.5 0.9 collective-permute-start.35
  145.3 1.6 %shard_map.111.particular_ref = f32[128,512]{1,0:T(8,128)S(1)} custom-call(s32[4]{0:T(128)S(1)} %copy-done.6, f32[128,512]{1,0:T(8,128)S(1)} %get-tuple-element.128.source_ref, f32[1,512]{1,0:T(1,128)S(1)} %bitcast.93, bf16[4,8,128,128]{3,2,1,0:T(8,128)(2,1)S(1)} %get-tuple-element.125.refs_10_.high_ref, ...), custom_call_target="tpu_custom_call" | custom-call | flops 40000000 | bytes 3145728 | tf_op jit(solution)/shard_map/pallas_call | solution.py:390
  146.9 0.8 collective-permute-done.35.two_ref
  147.8 2.3 %shard_map.112 = f32[128,512]{1,0:T(8,128)} custom-call(s32[4]{0:T(128)S(1)} %copy-done.6, s32[1]{0:T(128)} %bitcast.slab_ref, f32[16,512]{1,0:T(8,128)S(1)} %select_reduce_fusion.wall_ref, f32[16,512]{1,0:T(8,128)S(1)} %collective-permute-done.34.one_ref, f32[16,512]{1,0:T(8,128)S(1)} %collective-permute-done.35.two_ref, ...), custom_call_target="tpu_custom_call" | custom-call | flops 60000000 | bytes 3145728 | tf_op jit(solution)/shard_map/pallas_call | solution.py:393
  (78 shorter events, 5.7 us)
Async XLA Ops:
  0.0 11.6 %copy-start.1 = (f32[32768]{0:T(1024)S(1)}, f32[32768]{0:T(1024)}, u32[]{:S(2)}) copy-start(f32[32768]{0:T(1024)} %param.15) | copy-start | bytes 393220
  0.0 11.6 %copy-start.2 = (f32[128,512]{1,0:T(8,128)S(1)}, f32[128,512]{1,0:T(8,128)}, u32[]{:S(2)}) copy-start(f32[128,512]{1,0:T(8,128)} %x_ref.8) | copy-start | bytes 786436
  0.0 11.6 %copy-start.3 = (s32[4,64]{1,0:T(4,128)S(1)}, s32[4,64]{1,0:T(4,128)}, u32[]{:S(2)}) copy-start(s32[4,64]{1,0:T(4,128)} %pattern_ref.9) | copy-start | bytes 3076
  0.0 11.6 %copy-start.4 = (f32[512]{0:T(512)S(1)}, f32[512]{0:T(512)}, u32[]{:S(2)}) copy-start(f32[512]{0:T(512)} %param.14) | copy-start | bytes 6148
  5.3 18.7 %collective-permute-start.4 = (f32[2,192,512]{2,1,0:T(8,128)}, f32[2,192,512]{2,1,0:T(8,128)S(1)}, u32[]{:S(2)}, u32[]{:S(2)}) collective-permute-start(f32[2,192,512]{2,1,0:T(8,128)} %get-tuple-element.74), channel_id=1, source_target_pairs={{0,1},{1,2},{2,3},{3,0},{4,5},{5,6},{6,7},{7,4},{8,9},{9,10},{10,1... | collective-permute-start | bytes 2359304 | tf_op jit(solution)/shard_map/ppermute | solution.py:35
  7.4 18.4 %collective-permute-start.5 = (f32[2,192,512]{2,1,0:T(8,128)}, f32[2,192,512]{2,1,0:T(8,128)S(1)}, u32[]{:S(2)}, u32[]{:S(2)}) collective-permute-start(f32[2,192,512]{2,1,0:T(8,128)} %get-tuple-element.75), channel_id=1, source_target_pairs={{0,3},{1,0},{2,1},{3,2},{4,7},{5,4},{6,5},{7,6},{8,11},{9,8},{10,9... | collective-permute-start | bytes 2359304 | tf_op jit(solution)/shard_map/ppermute | solution.py:35
  8.7 23.5 %collective-permute-start.6 = (f32[2,192,512]{2,1,0:T(8,128)}, f32[2,192,512]{2,1,0:T(8,128)S(1)}, u32[]{:S(2)}, u32[]{:S(2)}) collective-permute-start(f32[2,192,512]{2,1,0:T(8,128)} %get-tuple-element.76), channel_id=1, source_target_pairs={{0,4},{1,5},{2,6},{3,7},{4,8},{5,9},{6,10},{7,11},{8,12},{9,13},{1... | collective-permute-start | bytes 2359304 | tf_op jit(solution)/shard_map/ppermute | solution.py:35
  10.1 22.3 %collective-permute-start.7 = (f32[2,192,512]{2,1,0:T(8,128)}, f32[2,192,512]{2,1,0:T(8,128)S(1)}, u32[]{:S(2)}, u32[]{:S(2)}) collective-permute-start(f32[2,192,512]{2,1,0:T(8,128)} %get-tuple-element.77), channel_id=1, source_target_pairs={{0,12},{1,13},{2,14},{3,15},{4,0},{5,1},{6,2},{7,3},{8,4},{9,5},{1... | collective-permute-start | bytes 2359304 | tf_op jit(solution)/shard_map/ppermute | solution.py:35
  11.6 3.4 %copy-start = (bf16[4,64,128,128]{3,2,1,0:T(8,128)(2,1)S(1)}, bf16[4,64,128,128]{3,2,1,0:T(8,128)(2,1)}, u32[]{:S(2)}) copy-start(bf16[4,64,128,128]{3,2,1,0:T(8,128)(2,1)} %refs_15_.9) | copy-start | bytes 25165828
  17.4 24.8 %collective-permute-start = (f32[2,192,512]{2,1,0:T(8,128)S(1)}, f32[2,192,512]{2,1,0:T(8,128)S(1)}, u32[]{:S(2)}, u32[]{:S(2)}) collective-permute-start(f32[2,192,512]{2,1,0:T(8,128)S(1)} %get-tuple-element.67), channel_id=1, source_target_pairs={{0,3},{1,0},{2,1},{3,2},{4,7},{5,4},{6,5},{7,6},{8,11},{9,8},{10,9... | collective-permute-start | bytes 2359304 | tf_op jit(solution)/shard_map/ppermute | solution.py:35
  23.9 19.4 %collective-permute-start.1 = (f32[2,192,512]{2,1,0:T(8,128)S(1)}, f32[2,192,512]{2,1,0:T(8,128)S(1)}, u32[]{:S(2)}, u32[]{:S(2)}) collective-permute-start(f32[2,192,512]{2,1,0:T(8,128)S(1)} %get-tuple-element.68), channel_id=1, source_target_pairs={{0,1},{1,2},{2,3},{3,0},{4,5},{5,6},{6,7},{7,4},{8,9},{9,10},{10,1... | collective-permute-start | bytes 2359304 | tf_op jit(solution)/shard_map/ppermute | solution.py:35
  25.8 18.0 %collective-permute-start.2 = (f32[2,192,512]{2,1,0:T(8,128)S(1)}, f32[2,192,512]{2,1,0:T(8,128)S(1)}, u32[]{:S(2)}, u32[]{:S(2)}) collective-permute-start(f32[2,192,512]{2,1,0:T(8,128)S(1)} %get-tuple-element.69), channel_id=1, source_target_pairs={{0,12},{1,13},{2,14},{3,15},{4,0},{5,1},{6,2},{7,3},{8,4},{9,5},{1... | collective-permute-start | bytes 2359304 | tf_op jit(solution)/shard_map/ppermute | solution.py:35
  28.7 3.4 %copy-start.6 = (s32[4]{0:T(128)S(1)}, s32[4]{0:T(128)}, u32[]{:S(2)}) copy-start(s32[4]{0:T(128)} %direction_ref.5) | copy-start | bytes 52
  32.2 17.2 %collective-permute-start.3 = (f32[2,192,512]{2,1,0:T(8,128)S(1)}, f32[2,192,512]{2,1,0:T(8,128)S(1)}, u32[]{:S(2)}, u32[]{:S(2)}) collective-permute-start(f32[2,192,512]{2,1,0:T(8,128)S(1)} %get-tuple-element.70), channel_id=1, source_target_pairs={{0,4},{1,5},{2,6},{3,7},{4,8},{5,9},{6,10},{7,11},{8,12},{9,13},{1... | collective-permute-start | bytes 2359304 | tf_op jit(solution)/shard_map/ppermute | solution.py:35
  32.4 11.4 %copy-start.8 = (f32[4,512]{1,0:T(4,128)S(1)}, f32[4,512]{1,0:T(4,128)}, u32[]{:S(2)}) copy-start(f32[4,512]{1,0:T(4,128)} %param.19) | copy-start | bytes 24580
  32.4 11.4 %copy-start.9 = (f32[4,512]{1,0:T(4,128)S(1)}, f32[4,512]{1,0:T(4,128)}, u32[]{:S(2)}) copy-start(f32[4,512]{1,0:T(4,128)} %param.20) | copy-start | bytes 24580
  32.4 14.0 %copy-start.10 = (s32[16]{0:T(128)S(1)}, s32[16]{0:T(128)}, u32[]{:S(2)}) copy-start(s32[16]{0:T(128)} %param.21) | copy-start | bytes 196
  32.4 14.0 %copy-start.5 = (f32[512]{0:T(512)S(1)}, f32[512]{0:T(512)}, u32[]{:S(2)}) copy-start(f32[512]{0:T(512)} %param.17) | copy-start | bytes 6148
  32.4 13.9 %copy-start.7 = (f32[4,128,128]{2,1,0:T(8,128)S(1)}, f32[4,128,128]{2,1,0:T(8,128)}, u32[]{:S(2)}) copy-start(f32[4,128,128]{2,1,0:T(8,128)} %inscatter_ref.1) | copy-start | bytes 786436
  32.4 22.2 %collective-permute-start.8 = (f32[4,64,512]{2,1,0:T(8,128)S(1)}, f32[4,64,512]{2,1,0:T(8,128)S(1)}, u32[]{:S(2)}, u32[]{:S(2)}) collective-permute-start(f32[4,64,512]{2,1,0:T(8,128)S(1)} %get-tuple-element.88), channel_id=1, source_target_pairs={{0,1},{1,2},{2,3},{3,0},{4,5},{5,6},{6,7},{7,4},{8,9},{9,10},{10,1... | collective-permute-start | bytes 1572872 | tf_op jit(solution)/shard_map/ppermute | solution.py:35
  42.3 15.0 %collective-permute-start.9 = (f32[4,64,512]{2,1,0:T(8,128)S(1)}, f32[4,64,512]{2,1,0:T(8,128)S(1)}, u32[]{:S(2)}, u32[]{:S(2)}) collective-permute-start(f32[4,64,512]{2,1,0:T(8,128)S(1)} %get-tuple-element.89), channel_id=1, source_target_pairs={{0,3},{1,0},{2,1},{3,2},{4,7},{5,4},{6,5},{7,6},{8,11},{9,8},{10,9... | collective-permute-start | bytes 1572872 | tf_op jit(solution)/shard_map/ppermute | solution.py:35
  43.4 26.9 %collective-permute-start.12 = (f32[2,192,512]{2,1,0:T(8,128)S(1)}, f32[2,192,512]{2,1,0:T(8,128)S(1)}, u32[]{:S(2)}, u32[]{:S(2)}) collective-permute-start(f32[2,192,512]{2,1,0:T(8,128)S(1)} %get-tuple-element.105), channel_id=1, source_target_pairs={{0,1},{1,2},{2,3},{3,0},{4,5},{5,6},{6,7},{7,4},{8,9},{9,10},{10,1... | collective-permute-start | bytes 2359304 | tf_op jit(solution)/shard_map/ppermute | solution.py:35
  43.8 31.8 %collective-permute-start.14 = (f32[2,192,512]{2,1,0:T(8,128)S(1)}, f32[2,192,512]{2,1,0:T(8,128)S(1)}, u32[]{:S(2)}, u32[]{:S(2)}) collective-permute-start(f32[2,192,512]{2,1,0:T(8,128)S(1)} %get-tuple-element.107), channel_id=1, source_target_pairs={{0,3},{1,0},{2,1},{3,2},{4,7},{5,4},{6,5},{7,6},{8,11},{9,8},{10,9... | collective-permute-start | bytes 2359304 | tf_op jit(solution)/shard_map/ppermute | solution.py:35
  49.4 30.1 %collective-permute-start.10 = (f32[4,64,512]{2,1,0:T(8,128)S(1)}, f32[4,64,512]{2,1,0:T(8,128)S(1)}, u32[]{:S(2)}, u32[]{:S(2)}) collective-permute-start(f32[4,64,512]{2,1,0:T(8,128)S(1)} %get-tuple-element.91), channel_id=1, source_target_pairs={{0,4},{1,5},{2,6},{3,7},{4,8},{5,9},{6,10},{7,11},{8,12},{9,13},{1... | collective-permute-start | bytes 1572872 | tf_op jit(solution)/shard_map/ppermute | solution.py:35
  54.6 24.2 %collective-permute-start.17 = (f32[2,192,512]{2,1,0:T(8,128)S(1)}, f32[2,192,512]{2,1,0:T(8,128)S(1)}, u32[]{:S(2)}, u32[]{:S(2)}) collective-permute-start(f32[2,192,512]{2,1,0:T(8,128)S(1)} %get-tuple-element.109), channel_id=1, source_target_pairs={{0,4},{1,5},{2,6},{3,7},{4,8},{5,9},{6,10},{7,11},{8,12},{9,13},{1... | collective-permute-start | bytes 2359304 | tf_op jit(solution)/shard_map/ppermute | solution.py:35
  57.3 18.6 %collective-permute-start.19 = (f32[2,192,512]{2,1,0:T(8,128)S(1)}, f32[2,192,512]{2,1,0:T(8,128)S(1)}, u32[]{:S(2)}, u32[]{:S(2)}) collective-permute-start(f32[2,192,512]{2,1,0:T(8,128)S(1)} %get-tuple-element.111), channel_id=1, source_target_pairs={{0,12},{1,13},{2,14},{3,15},{4,0},{5,1},{6,2},{7,3},{8,4},{9,5},{1... | collective-permute-start | bytes 2359304 | tf_op jit(solution)/shard_map/ppermute | solution.py:35
  70.3 16.4 %collective-permute-start.11 = (f32[4,64,512]{2,1,0:T(8,128)S(1)}, f32[4,64,512]{2,1,0:T(8,128)S(1)}, u32[]{:S(2)}, u32[]{:S(2)}) collective-permute-start(f32[4,64,512]{2,1,0:T(8,128)S(1)} %get-tuple-element.92), channel_id=1, source_target_pairs={{0,12},{1,13},{2,14},{3,15},{4,0},{5,1},{6,2},{7,3},{8,4},{9,5},{1... | collective-permute-start | bytes 1572872 | tf_op jit(solution)/shard_map/ppermute | solution.py:35
  75.7 13.1 %collective-permute-start.13 = (f32[192,512]{1,0:T(8,128)S(1)}, f32[192,512]{1,0:T(8,128)S(1)}, u32[]{:S(2)}, u32[]{:S(2)}) collective-permute-start(f32[192,512]{1,0:T(8,128)S(1)} %fusion.5), channel_id=1, source_target_pairs={{0,4},{1,5},{2,6},{3,7},{4,8},{5,9},{6,10},{7,11},{8,12},{9,13},{1... | collective-permute-start | bytes 1179656 | tf_op jit(solution)/shard_map/ppermute | solution.py:35
  75.9 19.1 %collective-permute-start.16 = (f32[192,512]{1,0:T(8,128)S(1)}, f32[192,512]{1,0:T(8,128)S(1)}, u32[]{:S(2)}, u32[]{:S(2)}) collective-permute-start(f32[192,512]{1,0:T(8,128)S(1)} %get-tuple-element.131), channel_id=1, source_target_pairs={{0,12},{1,13},{2,14},{3,15},{4,0},{5,1},{6,2},{7,3},{8,4},{9,5},{1... | collective-permute-start | bytes 1179656 | tf_op jit(solution)/shard_map/ppermute | solution.py:35
  78.8 16.7 %collective-permute-start.15 = (f32[192,512]{1,0:T(8,128)S(1)}, f32[192,512]{1,0:T(8,128)S(1)}, u32[]{:S(2)}, u32[]{:S(2)}) collective-permute-start(f32[192,512]{1,0:T(8,128)S(1)} %get-tuple-element.132), channel_id=1, source_target_pairs={{0,8},{1,9},{2,10},{3,11},{4,12},{5,13},{6,14},{7,15},{8,0},{9,1},... | collective-permute-start | bytes 1179656 | tf_op jit(solution)/shard_map/ppermute | solution.py:35
  79.5 19.3 %collective-permute-start.18 = (f32[192,512]{1,0:T(8,128)S(1)}, f32[192,512]{1,0:T(8,128)S(1)}, u32[]{:S(2)}, u32[]{:S(2)}) collective-permute-start(f32[192,512]{1,0:T(8,128)S(1)} %fusion.2), channel_id=1, source_target_pairs={{0,1},{1,2},{2,3},{3,0},{4,5},{5,6},{6,7},{7,4},{8,9},{9,10},{10,1... | collective-permute-start | bytes 1179656 | tf_op jit(solution)/shard_map/ppermute | solution.py:35
  86.6 12.2 %collective-permute-start.21 = (f32[192,512]{1,0:T(8,128)S(1)}, f32[192,512]{1,0:T(8,128)S(1)}, u32[]{:S(2)}, u32[]{:S(2)}) collective-permute-start(f32[192,512]{1,0:T(8,128)S(1)} %get-tuple-element.129), channel_id=1, source_target_pairs={{0,3},{1,0},{2,1},{3,2},{4,7},{5,4},{6,5},{7,6},{8,11},{9,8},{10,9... | collective-permute-start | bytes 1179656 | tf_op jit(solution)/shard_map/ppermute | solution.py:35
  88.8 11.6 %collective-permute-start.20 = (f32[192,512]{1,0:T(8,128)S(1)}, f32[192,512]{1,0:T(8,128)S(1)}, u32[]{:S(2)}, u32[]{:S(2)}) collective-permute-start(f32[192,512]{1,0:T(8,128)S(1)} %get-tuple-element.130), channel_id=1, source_target_pairs={{0,2},{1,3},{2,0},{3,1},{4,6},{5,7},{6,4},{7,5},{8,10},{9,11},{10,... | collective-permute-start | bytes 1179656 | tf_op jit(solution)/shard_map/ppermute | solution.py:35
  95.8 12.1 %collective-permute-start.30 = (f32[64,512]{1,0:T(8,128)S(1)}, f32[64,512]{1,0:T(8,128)S(1)}, u32[]{:S(2)}, u32[]{:S(2)}) collective-permute-start(f32[64,512]{1,0:T(8,128)S(1)} %slice.167), channel_id=1, source_target_pairs={{0,16},{1,17},{2,18},{3,19},{4,20},{5,21},{6,22},{7,23},{8,24},{9,... | collective-permute-start | bytes 393224 | tf_op jit(solution)/shard_map/ppermute | solution.py:35
  100.6 9.4 %collective-permute-start.32 = (f32[64,512]{1,0:T(8,128)S(1)}, f32[64,512]{1,0:T(8,128)S(1)}, u32[]{:S(2)}, u32[]{:S(2)}) collective-permute-start(f32[64,512]{1,0:T(8,128)S(1)} %get-tuple-element.142), channel_id=1, source_target_pairs={{0,48},{1,49},{2,50},{3,51},{4,52},{5,53},{6,54},{7,55},{8,56},{9,... | collective-permute-start | bytes 393224 | tf_op jit(solution)/shard_map/ppermute | solution.py:35
  106.7 9.5 %collective-permute-start.22 = (f32[4,64,512]{2,1,0:T(8,128)S(1)}, f32[4,64,512]{2,1,0:T(8,128)S(1)}, u32[]{:S(2)}, u32[]{:S(2)}) collective-permute-start(f32[4,64,512]{2,1,0:T(8,128)S(1)} %get-tuple-element.112), channel_id=1, source_target_pairs={{0,2},{1,3},{2,0},{3,1},{4,6},{5,7},{6,4},{7,5},{8,10},{9,11},{10,... | collective-permute-start | bytes 1572872 | tf_op jit(solution)/shard_map/ppermute | solution.py:35
  107.8 18.4 %collective-permute-start.26 = (f32[4,64,512]{2,1,0:T(8,128)S(1)}, f32[4,64,512]{2,1,0:T(8,128)S(1)}, u32[]{:S(2)}, u32[]{:S(2)}) collective-permute-start(f32[4,64,512]{2,1,0:T(8,128)S(1)} %get-tuple-element.114), channel_id=1, source_target_pairs={{0,8},{1,9},{2,10},{3,11},{4,12},{5,13},{6,14},{7,15},{8,0},{9,1},... | collective-permute-start | bytes 1572872 | tf_op jit(solution)/shard_map/ppermute | solution.py:35
  107.9 18.4 %collective-permute-start.31 = (f32[128,512]{1,0:T(8,128)S(1)}, f32[128,512]{1,0:T(8,128)S(1)}, u32[]{:S(2)}, u32[]{:S(2)}) collective-permute-start(f32[128,512]{1,0:T(8,128)S(1)} %pad_maximum_fusion), channel_id=1, source_target_pairs={{0,16},{1,17},{2,18},{3,19},{4,20},{5,21},{6,22},{7,23},{8,24},{9,... | collective-permute-start | bytes 786440 | tf_op jit(solution)/shard_map/ppermute | solution.py:35
  110.0 16.3 %collective-permute-start.33 = (f32[128,512]{1,0:T(8,128)S(1)}, f32[128,512]{1,0:T(8,128)S(1)}, u32[]{:S(2)}, u32[]{:S(2)}) collective-permute-start(f32[128,512]{1,0:T(8,128)S(1)} %pad_maximum_fusion.1), channel_id=1, source_target_pairs={{0,48},{1,49},{2,50},{3,51},{4,52},{5,53},{6,54},{7,55},{8,56},{9,... | collective-permute-start | bytes 786440 | tf_op jit(solution)/shard_map/ppermute | solution.py:35
  116.3 12.0 %collective-permute-start.25 = (f32[64,512]{1,0:T(8,128)S(1)}, f32[64,512]{1,0:T(8,128)S(1)}, u32[]{:S(2)}, u32[]{:S(2)}) collective-permute-start(f32[64,512]{1,0:T(8,128)S(1)} %get-tuple-element.137), channel_id=1, source_target_pairs={{0,12},{1,13},{2,14},{3,15},{4,0},{5,1},{6,2},{7,3},{8,4},{9,5},{1... | collective-permute-start | bytes 393224 | tf_op jit(solution)/shard_map/ppermute | solution.py:35
  125.0 6.6 %collective-permute-start.24 = (f32[64,512]{1,0:T(8,128)S(1)}, f32[64,512]{1,0:T(8,128)S(1)}, u32[]{:S(2)}, u32[]{:S(2)}) collective-permute-start(f32[64,512]{1,0:T(8,128)S(1)} %get-tuple-element.138), channel_id=1, source_target_pairs={{0,8},{1,9},{2,10},{3,11},{4,12},{5,13},{6,14},{7,15},{8,0},{9,1},... | collective-permute-start | bytes 393224 | tf_op jit(solution)/shard_map/ppermute | solution.py:35
  126.2 6.7 %collective-permute-start.23 = (f32[64,512]{1,0:T(8,128)S(1)}, f32[64,512]{1,0:T(8,128)S(1)}, u32[]{:S(2)}, u32[]{:S(2)}) collective-permute-start(f32[64,512]{1,0:T(8,128)S(1)} %get-tuple-element.139), channel_id=1, source_target_pairs={{0,4},{1,5},{2,6},{3,7},{4,8},{5,9},{6,10},{7,11},{8,12},{9,13},{1... | collective-permute-start | bytes 393224 | tf_op jit(solution)/shard_map/ppermute | solution.py:35
  126.3 6.6 %collective-permute-start.29 = (f32[64,512]{1,0:T(8,128)S(1)}, f32[64,512]{1,0:T(8,128)S(1)}, u32[]{:S(2)}, u32[]{:S(2)}) collective-permute-start(f32[64,512]{1,0:T(8,128)S(1)} %get-tuple-element.133), channel_id=1, source_target_pairs={{0,3},{1,0},{2,1},{3,2},{4,7},{5,4},{6,5},{7,6},{8,11},{9,8},{10,9... | collective-permute-start | bytes 393224 | tf_op jit(solution)/shard_map/ppermute | solution.py:35
  126.4 6.5 %collective-permute-start.28 = (f32[64,512]{1,0:T(8,128)S(1)}, f32[64,512]{1,0:T(8,128)S(1)}, u32[]{:S(2)}, u32[]{:S(2)}) collective-permute-start(f32[64,512]{1,0:T(8,128)S(1)} %get-tuple-element.134), channel_id=1, source_target_pairs={{0,2},{1,3},{2,0},{3,1},{4,6},{5,7},{6,4},{7,5},{8,10},{9,11},{10,... | collective-permute-start | bytes 393224 | tf_op jit(solution)/shard_map/ppermute | solution.py:35
  128.3 5.3 %collective-permute-start.27 = (f32[64,512]{1,0:T(8,128)S(1)}, f32[64,512]{1,0:T(8,128)S(1)}, u32[]{:S(2)}, u32[]{:S(2)}) collective-permute-start(f32[64,512]{1,0:T(8,128)S(1)} %get-tuple-element.135), channel_id=1, source_target_pairs={{0,1},{1,2},{2,3},{3,0},{4,5},{5,6},{6,7},{7,4},{8,9},{9,10},{10,1... | collective-permute-start | bytes 393224 | tf_op jit(solution)/shard_map/ppermute | solution.py:35
  134.9 12.0 %collective-permute-start.36 = (f32[16,512]{1,0:T(8,128)S(1)}, f32[16,512]{1,0:T(8,128)S(1)}, u32[]{:S(2)}, u32[]{:S(2)}) collective-permute-start(f32[16,512]{1,0:T(8,128)S(1)} %get-tuple-element.127), channel_id=1, source_target_pairs={{0,192},{64,128},{128,64},{192,0},{1,193},{65,129},{129,65},{193,1... | collective-permute-start | bytes 98312 | tf_op jit(solution)/shard_map/ppermute | solution.py:388
  144.5 3.3 %collective-permute-start.35 = (f32[16,512]{1,0:T(8,128)S(1)}, f32[16,512]{1,0:T(8,128)S(1)}, u32[]{:S(2)}, u32[]{:S(2)}) collective-permute-start(f32[16,512]{1,0:T(8,128)S(1)} %get-tuple-element.127), channel_id=1, source_target_pairs={{0,128},{64,192},{128,0},{192,64},{1,129},{65,193},{129,1},{193,65... | collective-permute-start | bytes 98312 | tf_op jit(solution)/shard_map/ppermute | solution.py:388
  145.3 2.4 %collective-permute-start.34 = (f32[16,512]{1,0:T(8,128)S(1)}, f32[16,512]{1,0:T(8,128)S(1)}, u32[]{:S(2)}, u32[]{:S(2)}) collective-permute-start(f32[16,512]{1,0:T(8,128)S(1)} %get-tuple-element.127), channel_id=1, source_target_pairs={{0,64},{64,0},{128,192},{192,128},{1,65},{65,1},{129,193},{193,129... | collective-permute-start | bytes 98312 | tf_op jit(solution)/shard_map/ppermute | solution.py:388

commit v6 on v5

--- a/solution.py
+++ b/solution.py
@@ -194,16 +194,20 @@
 
 
 def particular_kernel(direction_ref, source_ref, rate_ref, high_ref, low_ref, out_ref):
-    now = [jnp.zeros((LATERAL, BLK), jnp.float32) for _ in range(SHELL)]
-    for t in range(LAYERS):
+    def layer(t, now):
+        following = []
         for b in range(SHELL):
             lanes = pl.ds(b * BLK, BLK)
             at = jnp.where(direction_ref[b] == 1, t, LAYERS - 1 - t)
             rows = pl.ds(pl.multiple_of(at * LATERAL, LATERAL), LATERAL)
-            now[b] = product(
+            face = product(
                 source_ref[rows, lanes] + rate_ref[:, lanes] * now[b], high_ref[b, 0], low_ref[b, 0]
             )
-            out_ref[rows, lanes] = now[b]
+            out_ref[rows, lanes] = face
+            following.append(face)
+        return tuple(following)
+
+    lax.fori_loop(0, LAYERS, layer, (jnp.zeros((LATERAL, BLK), jnp.float32),) * SHELL)
 
 
 def finish_kernel(
@@ -338,7 +342,12 @@
         prior=after,
     )
     far_got, near = lax.optimization_barrier((far_got, near))
-    beside = ((near[1], 2, 1), (near[3], 2, -1), (near[5], 1, 1), (near[7], 1, -1))
+    beside = (
+        (near[2][:2], 2, 1),
+        (near[2][2:], 2, -1),
+        (near[6][:2], 1, 1),
+        (near[6][2:], 1, -1),
+    )
     late = ring(ring_sums(1, 3, prior, far_got), 1)
     early, high, low, wall = lax.optimization_barrier((early, high, low, wall))
     kept = ring_sums(0, 0, prior, early)
@@ -351,12 +360,17 @@
     for block, axis, step in ((a1, 1, 1), (a2, 1, 2), (a3, 1, -1), (b1, 2, 1), (b2, 2, 2), (b3, 2, -1)):
         crossed.append(send(block, axis, step))
     a_got, b_got = crossed[:3], crossed[3:]
-    ready_a = near[0] + near_got[0] + near_got[1]
-    ready_b = near[4] + near_got[2] + near_got[3]
-    ready_a, ready_b = lax.optimization_barrier((ready_a, ready_b))
-    across, _ = lax.optimization_barrier(((near[2], near[6]), (a_got, b_got)))
-    far_x = send(across[0], 2, 2)
-    far_y = send(across[1], 1, 2)
+    near_got, _ = lax.optimization_barrier((near_got, (a1, a2, a3, b1, b2, b3)))
+    onward = (
+        jnp.concatenate([near[1][:2] + near_got[0], near[1][2:]], axis=0),
+        jnp.concatenate([near[3][:2], near[3][2:] + near_got[1]], axis=0),
+        jnp.concatenate([near[5][:2] + near_got[2], near[5][2:]], axis=0),
+        jnp.concatenate([near[7][:2], near[7][2:] + near_got[3]], axis=0),
+    )
+    onward, _ = lax.optimization_barrier((onward, (a_got, b_got)))
+    arrived = []
+    for index, (axis, step) in enumerate(((2, 1), (2, -1), (1, 1), (1, -1))):
+        arrived.append(send(onward[index], axis, step))
     a_own, a_got = lax.optimization_barrier(((kept[0], late[0]), a_got))
     b_own, b_got = lax.optimization_barrier(((kept[2], late[2]), b_got))
     a_sum = a_own[0][0] + a_own[1][0] + a_got[0] + a_got[1] + a_got[2]
@@ -368,14 +382,14 @@
     from_below = send(above, 0, 1)
     from_above = send(below, 0, -1)
 
-    def ends(ready, got, axis):
-        parts = [ready[i] + got[i] for i in range(SIDE)]
+    def ends(own, below_got, above_got, axis):
+        parts = [own[i] + below_got[i] + above_got[i] for i in range(SIDE)]
         moved = []
         for index, step in enumerate((1, 2, -1)):
             moved.append(send(parts[index + 1], axis, step))
         return [parts[0]] + moved
 
-    halves = ends(ready_a, far_x, 1) + ends(ready_b, far_y, 2)
+    halves = ends(near[0], arrived[0], arrived[1], 1) + ends(near[4], arrived[2], arrived[3], 2)
 
     whole = ((CELL, WIDTH), jnp.float32)
     source, last = small_call(

time: 150 us -> 147 us (0.980)
  starting transfers between devices: 70.5 us -> 67.9 us
    ppermute x34 -> x36, starting transfers between devices: 60.1 us -> 53.7 us  [send(): return lax.ppermute(block, 'modes', route(axis, step))]
    ppermute x3, starting transfers between devices: 10.4 us -> 14.2 us  [per_device(): lax.ppermute(last, 'slab', [(i, i ^ k) for i in range(4)])]
    ppermute x34 -> x36, waiting for transfers between devices: 49.6 us -> 49.4 us  [send(): return lax.ppermute(block, 'modes', route(axis, step))]
  transfers between devices with their start and end apart: 37 -> 39, of which waited for: 16 -> 12; matrix products, arithmetic and copies ran while one was open for 1% -> 1% of each run, Pallas kernels for 10% -> 11%
where the time goes in v6:
time: 147 us
  starting transfers between devices  67.9 us (46%)
  waiting for transfers between devices  49.4 us (34%)
  Pallas kernels  24.3 us (17%)
  local copies, waits for them, and re-layouts  3.6 us (2%)
  other arithmetic  1.74 us (1%)
    ppermute x36, starting transfers between devices, send(): return lax.ppermute(block, 'modes', route(axis, step))  53.7 us
    ppermute x36, waiting for transfers between devices, send(): return lax.ppermute(block, 'modes', route(axis, step))  49.4 us
    pallas_call x5, Pallas kernels, partial_sums(): pl.pallas_call(functools.partial(partial_kernel, jobs, len(addends)), gri...  16.6 us
    ppermute x3, starting transfers between devices, per_device(): lax.ppermute(last, 'slab', [(i, i ^ k) for i in range(4)])  14.2 us
    unnamed x22, local copies, waits for them, and re-layouts  3.42 us
  transfers between devices with their start and end apart: 39, of which 12 were waited for; matrix products, arithmetic and copies ran while one was open for 1% of the time, Pallas kernels for 11%

profile of v6, /device:TPU:1, one launch (start us, length us, event | category | flops | bytes accessed | tf_op | source)
XLA Modules:
  0.0 147.4 jit_solution(955276394666609933)
XLA Ops:
  0.0 5.2 %partial_sums.6 = (f32[2,192,512]{2,1,0:T(8,128)}, f32[2,192,512]{2,1,0:T(8,128)}, f32[2,192,512]{2,1,0:T(8,128)}, f32[2,192,512]{2,1,0:T(8,128)}) custom-call(s32[1]{0:T(128)} %bitcast.1.place_ref, s32[4,64]{1,0:T(4,128)} %pattern_ref.9, f32[128,512]{1,0:T(8,128)} %x_ref.8, f32[1,512]{1,0:T(1,128)} %bitcast.87, f32[64,1,512]{2,1,0:T(1,128)} %bitcast.47, ...), custom_call_target="tpu_custom_call" | custom-call | flops 201326592 | bytes 4718592 | tf_op jit(solution)/shard_map/partial_sums/pallas_call | solution.py:107
  5.3 2.1 %collective-permute-start.4 = (f32[2,192,512]{2,1,0:T(8,128)}, f32[2,192,512]{2,1,0:T(8,128)S(1)}, u32[]{:S(2)}, u32[]{:S(2)}) collective-permute-start(f32[2,192,512]{2,1,0:T(8,128)} %get-tuple-element.78), channel_id=1, source_target_pairs={{0,1},{1,2},{2,3},{3,0},{4,5},{5,6},{6,7},{7,4},{8,9},{9,10},{10,1... | collective-permute-start | bytes 2359304 | tf_op jit(solution)/shard_map/ppermute | solution.py:35
  7.4 1.4 collective-permute-start.5
  8.7 1.4 collective-permute-start.6
  10.1 1.4 collective-permute-start.7
  11.6 3.4 %copy-done = bf16[4,64,128,128]{3,2,1,0:T(8,128)(2,1)S(1)} copy-done((bf16[4,64,128,128]{3,2,1,0:T(8,128)(2,1)S(1)}, bf16[4,64,128,128]{3,2,1,0:T(8,128)(2,1)}, u32[]{:S(2)}) %copy-start) | copy-done | bytes 8388632
  15.0 2.4 %partial_sums.5 = (f32[2,192,512]{2,1,0:T(8,128)S(1)}, f32[2,192,512]{2,1,0:T(8,128)S(1)}, f32[2,192,512]{2,1,0:T(8,128)S(1)}, f32[2,192,512]{2,1,0:T(8,128)S(1)}) custom-call(s32[1]{0:T(128)} %bitcast.1.place_ref, s32[4,64]{1,0:T(4,128)S(1)} %copy-done.3, f32[128,512]{1,0:T(8,128)S(1)} %copy-done.2, f32[1,512]{1,0:T(1,128)S(1)} %bitcast.88, ...), custom_call_target="tpu_custom_call" | custom-call | flops 201326592 | bytes 4718592 | tf_op jit(solution)/shard_map/partial_sums/pallas_call | solution.py:107
  17.4 1.4 collective-permute-start
  18.8 3.5 %partial_sums.7 = (f32[4,64,512]{2,1,0:T(8,128)S(1)}, f32[4,64,512]{2,1,0:T(8,128)S(1)}, f32[4,64,512]{2,1,0:T(8,128)S(1)}, f32[4,64,512]{2,1,0:T(8,128)S(1)}, f...) custom-call(s32[1]{0:T(128)} %bitcast.1.place_ref, ...), custom_call_target="tpu_custom_call" | custom-call | flops 268435456 | bytes 6291456 | tf_op jit(solution)/shard_map/partial_sums/pallas_call | solution.py:107
  22.3 1.7 %collective-permute-done.4.refs_16_ = f32[2,192,512]{2,1,0:T(8,128)S(1)} collective-permute-done((f32[2,192,512]{2,1,0:T(8,128)}, f32[2,192,512]{2,1,0:T(8,128)S(1)}, u32[]{:S(2)}, u32[]{:S(2)}) %collective-permute-start.4) | collective-permute-done | bytes 786464 | tf_op jit(solution)/shard_map/ppermute | solution.py:35
  23.9 1.9 %collective-permute-start.1 = (f32[2,192,512]{2,1,0:T(8,128)S(1)}, f32[2,192,512]{2,1,0:T(8,128)S(1)}, u32[]{:S(2)}, u32[]{:S(2)}) collective-permute-start(f32[2,192,512]{2,1,0:T(8,128)S(1)} %get-tuple-element.72), channel_id=1, source_target_pairs={{0,1},{1,2},{2,3},{3,0},{4,5},{5,6},{6,7},{7,4},{8,9},{9,10},{10,1... | collective-permute-start | bytes 2359304 | tf_op jit(solution)/shard_map/ppermute | solution.py:35
  25.9 3.0 %collective-permute-start.2 = (f32[2,192,512]{2,1,0:T(8,128)S(1)}, f32[2,192,512]{2,1,0:T(8,128)S(1)}, u32[]{:S(2)}, u32[]{:S(2)}) collective-permute-start(f32[2,192,512]{2,1,0:T(8,128)S(1)} %get-tuple-element.73), channel_id=1, source_target_pairs={{0,12},{1,13},{2,14},{3,15},{4,0},{5,1},{6,2},{7,3},{8,4},{9,5},{1... | collective-permute-start | bytes 2359304 | tf_op jit(solution)/shard_map/ppermute | solution.py:35
  28.9 2.7 %partial_sums.9 = (f32[2,192,512]{2,1,0:T(8,128)S(1)}, f32[2,192,512]{2,1,0:T(8,128)S(1)}, f32[2,192,512]{2,1,0:T(8,128)S(1)}, f32[2,192,512]{2,1,0:T(8,128)S(1)}) custom-call(s32[1]{0:T(128)} %bitcast.1.place_ref, s32[4,64]{1,0:T(4,128)S(1)} %copy-done.3, f32[128,512]{1,0:T(8,128)S(1)} %copy-done.2, f32[1,512]{1,0:T(1,128)S(1)} %bitcast.90, ...), custom_call_target="tpu_custom_call" | custom-call | flops 201326592 | bytes 4718592 | tf_op jit(solution)/shard_map/partial_sums/pallas_call | solution.py:107
  31.7 1.3 collective-permute-start.12
  33.0 9.3 %collective-permute-done.refs_16_ = f32[2,192,512]{2,1,0:T(8,128)S(1)} collective-permute-done((f32[2,192,512]{2,1,0:T(8,128)S(1)}, f32[2,192,512]{2,1,0:T(8,128)S(1)}, u32[]{:S(2)}, u32[]{:S(2)}) %collective-permute-start) | collective-permute-done | bytes 786464 | tf_op jit(solution)/shard_map/ppermute | solution.py:35
  42.3 1.6 %collective-permute-start.14 = (f32[2,192,512]{2,1,0:T(8,128)S(1)}, f32[2,192,512]{2,1,0:T(8,128)S(1)}, u32[]{:S(2)}, u32[]{:S(2)}) collective-permute-start(f32[2,192,512]{2,1,0:T(8,128)S(1)} %get-tuple-element.108), channel_id=1, source_target_pairs={{0,4},{1,5},{2,6},{3,7},{4,8},{5,9},{6,10},{7,11},{8,12},{9,13},{1... | collective-permute-start | bytes 2359304 | tf_op jit(solution)/shard_map/ppermute | solution.py:35
  44.0 2.2 %shard_map.109 = (bf16[4,8,128,128]{3,2,1,0:T(8,128)(2,1)S(1)}, bf16[4,8,128,128]{3,2,1,0:T(8,128)(2,1)S(1)}) custom-call(f32[1,512]{1,0:T(1,128)S(1)} %bitcast.92, f32[4,128,128]{2,1,0:T(8,128)S(1)} %copy-done.7), custom_call_target="tpu_custom_call" | custom-call | flops 200000000 | bytes 3145728 | tf_op jit(solution)/shard_map/pallas_call | solution.py:324
  46.2 2.9 %collective-permute-start.13 = (f32[2,192,512]{2,1,0:T(8,128)S(1)}, f32[2,192,512]{2,1,0:T(8,128)S(1)}, u32[]{:S(2)}, u32[]{:S(2)}) collective-permute-start(f32[2,192,512]{2,1,0:T(8,128)S(1)} %get-tuple-element.106), channel_id=1, source_target_pairs={{0,3},{1,0},{2,1},{3,2},{4,7},{5,4},{6,5},{7,6},{8,11},{9,8},{10,9... | collective-permute-start | bytes 2359304 | tf_op jit(solution)/shard_map/ppermute | solution.py:35
  49.3 1.5 collective-permute-start.15
  50.8 2.7 %partial_sums.8 = (f32[2,192,512]{2,1,0:T(8,128)S(1)}, f32[2,192,512]{2,1,0:T(8,128)S(1)}, f32[2,192,512]{2,1,0:T(8,128)S(1)}, f32[2,192,512]{2,1,0:T(8,128)S(1)}) custom-call(s32[1]{0:T(128)} %bitcast.1.place_ref, s32[4,64]{1,0:T(4,128)S(1)} %copy-done.3, f32[128,512]{1,0:T(8,128)S(1)} %copy-done.2, f32[1,512]{1,0:T(1,128)S(1)} %bitcast.91, ...), custom_call_target="tpu_custom_call" | custom-call | flops 201326592 | bytes 4718592 | tf_op jit(solution)/shard_map/partial_sums/pallas_call | solution.py:107
  53.6 5.5 %collective-permute-done.12 = f32[2,192,512]{2,1,0:T(8,128)S(1)} collective-permute-done((f32[2,192,512]{2,1,0:T(8,128)S(1)}, f32[2,192,512]{2,1,0:T(8,128)S(1)}, u32[]{:S(2)}, u32[]{:S(2)}) %collective-permute-start.12) | collective-permute-done | bytes 786464 | tf_op jit(solution)/shard_map/ppermute | solution.py:35
  59.0 1.0 collective-permute-start.8
  60.1 3.3 %collective-permute-done.14 = f32[2,192,512]{2,1,0:T(8,128)S(1)} collective-permute-done((f32[2,192,512]{2,1,0:T(8,128)S(1)}, f32[2,192,512]{2,1,0:T(8,128)S(1)}, u32[]{:S(2)}, u32[]{:S(2)}) %collective-permute-start.14) | collective-permute-done | bytes 786464 | tf_op jit(solution)/shard_map/ppermute | solution.py:35
  63.4 1.5 collective-permute-start.11
  65.4 1.4 collective-permute-start.16
  67.0 2.6 %collective-permute-done.9 = f32[2,64,512]{2,1,0:T(8,128)S(1)} collective-permute-done((f32[2,64,512]{2,1,0:T(8,128)S(1)}, f32[2,64,512]{2,1,0:T(8,128)S(1)}, u32[]{:S(2)}, u32[]{:S(2)}) %collective-permute-start.9) | collective-permute-done | bytes 262176 | tf_op jit(solution)/shard_map/ppermute | solution.py:35
  69.5 1.6 %collective-permute-start.18 = (f32[192,512]{1,0:T(8,128)S(1)}, f32[192,512]{1,0:T(8,128)S(1)}, u32[]{:S(2)}, u32[]{:S(2)}) collective-permute-start(f32[192,512]{1,0:T(8,128)S(1)} %get-tuple-element.147), channel_id=1, source_target_pairs={{0,12},{1,13},{2,14},{3,15},{4,0},{5,1},{6,2},{7,3},{8,4},{9,5},{1... | collective-permute-start | bytes 1179656 | tf_op jit(solution)/shard_map/ppermute | solution.py:35
  71.1 1.5 collective-permute-start.17
  73.4 2.7 %collective-permute-start.21 = (f32[192,512]{1,0:T(8,128)S(1)}, f32[192,512]{1,0:T(8,128)S(1)}, u32[]{:S(2)}, u32[]{:S(2)}) collective-permute-start(f32[192,512]{1,0:T(8,128)S(1)} %get-tuple-element.145), channel_id=1, source_target_pairs={{0,3},{1,0},{2,1},{3,2},{4,7},{5,4},{6,5},{7,6},{8,11},{9,8},{10,9... | collective-permute-start | bytes 1179656 | tf_op jit(solution)/shard_map/ppermute | solution.py:35
  76.5 3.3 %collective-permute-done.16 = f32[192,512]{1,0:T(8,128)S(1)} collective-permute-done((f32[192,512]{1,0:T(8,128)S(1)}, f32[192,512]{1,0:T(8,128)S(1)}, u32[]{:S(2)}, u32[]{:S(2)}) %collective-permute-start.16) | collective-permute-done | bytes 393248 | tf_op jit(solution)/shard_map/ppermute | solution.py:35
  79.8 1.6 %collective-permute-start.20 = (f32[192,512]{1,0:T(8,128)S(1)}, f32[192,512]{1,0:T(8,128)S(1)}, u32[]{:S(2)}, u32[]{:S(2)}) collective-permute-start(f32[192,512]{1,0:T(8,128)S(1)} %get-tuple-element.146), channel_id=1, source_target_pairs={{0,2},{1,3},{2,0},{3,1},{4,6},{5,7},{6,4},{7,5},{8,10},{9,11},{10,... | collective-permute-start | bytes 1179656 | tf_op jit(solution)/shard_map/ppermute | solution.py:35
  81.5 3.0 %collective-permute-done.17 = f32[192,512]{1,0:T(8,128)S(1)} collective-permute-done((f32[192,512]{1,0:T(8,128)S(1)}, f32[192,512]{1,0:T(8,128)S(1)}, u32[]{:S(2)}, u32[]{:S(2)}) %collective-permute-start.17) | collective-permute-done | bytes 393248 | tf_op jit(solution)/shard_map/ppermute | solution.py:35
  84.7 2.9 %collective-permute-start.32 = (f32[64,512]{1,0:T(8,128)S(1)}, f32[64,512]{1,0:T(8,128)S(1)}, u32[]{:S(2)}, u32[]{:S(2)}) collective-permute-start(f32[64,512]{1,0:T(8,128)S(1)} %slice.255), channel_id=1, source_target_pairs={{0,16},{1,17},{2,18},{3,19},{4,20},{5,21},{6,22},{7,23},{8,24},{9,... | collective-permute-start | bytes 393224 | tf_op jit(solution)/shard_map/ppermute | solution.py:35
  87.6 3.2 %collective-permute-done.20 = f32[192,512]{1,0:T(8,128)S(1)} collective-permute-done((f32[192,512]{1,0:T(8,128)S(1)}, f32[192,512]{1,0:T(8,128)S(1)}, u32[]{:S(2)}, u32[]{:S(2)}) %collective-permute-start.20) | collective-permute-done | bytes 393248 | tf_op jit(solution)/shard_map/ppermute | solution.py:35
  91.0 6.1 %collective-permute-start.34 = (f32[64,512]{1,0:T(8,128)S(1)}, f32[64,512]{1,0:T(8,128)S(1)}, u32[]{:S(2)}, u32[]{:S(2)}) collective-permute-start(f32[64,512]{1,0:T(8,128)S(1)} %get-tuple-element.162), channel_id=1, source_target_pairs={{0,48},{1,49},{2,50},{3,51},{4,52},{5,53},{6,54},{7,55},{8,56},{9,... | collective-permute-start | bytes 393224 | tf_op jit(solution)/shard_map/ppermute | solution.py:35
  97.1 2.7 %collective-permute-start.23 = (f32[4,64,512]{2,1,0:T(8,128)S(1)}, f32[4,64,512]{2,1,0:T(8,128)S(1)}, u32[]{:S(2)}, u32[]{:S(2)}) collective-permute-start(f32[4,64,512]{2,1,0:T(8,128)S(1)} %pad_maximum_fusion.1), channel_id=1, source_target_pairs={{0,3},{1,0},{2,1},{3,2},{4,7},{5,4},{6,5},{7,6},{8,11},{9,8},{10,9... | collective-permute-start | bytes 1572872 | tf_op jit(solution)/shard_map/ppermute | solution.py:35
  100.7 1.8 %collective-permute-start.28 = (f32[4,64,512]{2,1,0:T(8,128)S(1)}, f32[4,64,512]{2,1,0:T(8,128)S(1)}, u32[]{:S(2)}, u32[]{:S(2)}) collective-permute-start(f32[4,64,512]{2,1,0:T(8,128)S(1)} %pad_maximum_fusion.3), channel_id=1, source_target_pairs={{0,12},{1,13},{2,14},{3,15},{4,0},{5,1},{6,2},{7,3},{8,4},{9,5},{1... | collective-permute-start | bytes 1572872 | tf_op jit(solution)/shard_map/ppermute | solution.py:35
  102.7 3.9 %collective-permute-done.22 = f32[4,64,512]{2,1,0:T(8,128)S(1)} collective-permute-done((f32[4,64,512]{2,1,0:T(8,128)S(1)}, f32[4,64,512]{2,1,0:T(8,128)S(1)}, u32[]{:S(2)}, u32[]{:S(2)}) %collective-permute-start.22) | collective-permute-done | bytes 524320 | tf_op jit(solution)/shard_map/ppermute | solution.py:35
  106.6 5.2 %collective-permute-start.35 = (f32[128,512]{1,0:T(8,128)S(1)}, f32[128,512]{1,0:T(8,128)S(1)}, u32[]{:S(2)}, u32[]{:S(2)}) collective-permute-start(f32[128,512]{1,0:T(8,128)S(1)} %pad_maximum_fusion.5), channel_id=1, source_target_pairs={{0,48},{1,49},{2,50},{3,51},{4,52},{5,53},{6,54},{7,55},{8,56},{9,... | collective-permute-start | bytes 786440 | tf_op jit(solution)/shard_map/ppermute | solution.py:35
  112.6 1.0 collective-permute-start.24
  113.8 6.9 %collective-permute-done.35.refs_9_ = f32[128,512]{1,0:T(8,128)S(1)} collective-permute-done((f32[128,512]{1,0:T(8,128)S(1)}, f32[128,512]{1,0:T(8,128)S(1)}, u32[]{:S(2)}, u32[]{:S(2)}) %collective-permute-start.35) | collective-permute-done | bytes 262176 | tf_op jit(solution)/shard_map/ppermute | solution.py:35
  120.9 5.5 %collective-permute-done.30.refs_6_ = f32[64,512]{1,0:T(8,128)S(1)} collective-permute-done((f32[64,512]{1,0:T(8,128)S(1)}, f32[64,512]{1,0:T(8,128)S(1)}, u32[]{:S(2)}, u32[]{:S(2)}) %collective-permute-start.30) | collective-permute-done | bytes 131104 | tf_op jit(solution)/shard_map/ppermute | solution.py:35
  126.4 1.2 collective-permute-done.29.refs_5_
  127.6 1.2 shard_map.110
  128.8 12.4 %collective-permute-start.38 = (f32[16,512]{1,0:T(8,128)S(1)}, f32[16,512]{1,0:T(8,128)S(1)}, u32[]{:S(2)}, u32[]{:S(2)}) collective-permute-start(f32[16,512]{1,0:T(8,128)S(1)} %get-tuple-element.135), channel_id=1, source_target_pairs={{0,192},{64,128},{128,64},{192,0},{1,193},{65,129},{129,65},{193,1... | collective-permute-start | bytes 98312 | tf_op jit(solution)/shard_map/ppermute | solution.py:402
  141.2 1.8 %collective-permute-start.37 = (f32[16,512]{1,0:T(8,128)S(1)}, f32[16,512]{1,0:T(8,128)S(1)}, u32[]{:S(2)}, u32[]{:S(2)}) collective-permute-start(f32[16,512]{1,0:T(8,128)S(1)} %get-tuple-element.135), channel_id=1, source_target_pairs={{0,128},{64,192},{128,0},{192,64},{1,129},{65,193},{129,1},{193,65... | collective-permute-start | bytes 98312 | tf_op jit(solution)/shard_map/ppermute | solution.py:402
  143.0 2.0 %shard_map.111.particular_ref = f32[128,512]{1,0:T(8,128)S(1)} custom-call(s32[4]{0:T(128)S(1)} %copy-done.6, f32[128,512]{1,0:T(8,128)S(1)} %get-tuple-element.136.source_ref, f32[1,512]{1,0:T(1,128)S(1)} %bitcast.93, bf16[4,8,128,128]{3,2,1,0:T(8,128)(2,1)S(1)} %get-tuple-element.133.refs_10_.high_ref, ...), custom_call_target="tpu_custom_call" | custom-call | flops 40000000 | bytes 3145728 | tf_op jit(solution)/shard_map/pallas_call | solution.py:404
  145.1 2.3 %shard_map.112 = f32[128,512]{1,0:T(8,128)} custom-call(s32[4]{0:T(128)S(1)} %copy-done.6, s32[1]{0:T(128)} %bitcast.slab_ref, f32[16,512]{1,0:T(8,128)S(1)} %select_reduce_fusion.wall_ref, f32[16,512]{1,0:T(8,128)S(1)} %collective-permute-done.36.one_ref, f32[16,512]{1,0:T(8,128)S(1)} %collective-permute-done.37.two_ref, ...), custom_call_target="tpu_custom_call" | custom-call | flops 60000000 | bytes 3145728 | tf_op jit(solution)/shard_map/pallas_call | solution.py:407
  (88 shorter events, 5.0 us)
Async XLA Ops:
  0.0 11.6 %copy-start.1 = (f32[32768]{0:T(1024)S(1)}, f32[32768]{0:T(1024)}, u32[]{:S(2)}) copy-start(f32[32768]{0:T(1024)} %param.15) | copy-start | bytes 393220
  0.0 11.6 %copy-start.2 = (f32[128,512]{1,0:T(8,128)S(1)}, f32[128,512]{1,0:T(8,128)}, u32[]{:S(2)}) copy-start(f32[128,512]{1,0:T(8,128)} %x_ref.8) | copy-start | bytes 786436
  0.0 11.6 %copy-start.3 = (s32[4,64]{1,0:T(4,128)S(1)}, s32[4,64]{1,0:T(4,128)}, u32[]{:S(2)}) copy-start(s32[4,64]{1,0:T(4,128)} %pattern_ref.9) | copy-start | bytes 3076
  0.0 11.6 %copy-start.4 = (f32[512]{0:T(512)S(1)}, f32[512]{0:T(512)}, u32[]{:S(2)}) copy-start(f32[512]{0:T(512)} %param.14) | copy-start | bytes 6148
  5.3 18.7 %collective-permute-start.4 = (f32[2,192,512]{2,1,0:T(8,128)}, f32[2,192,512]{2,1,0:T(8,128)S(1)}, u32[]{:S(2)}, u32[]{:S(2)}) collective-permute-start(f32[2,192,512]{2,1,0:T(8,128)} %get-tuple-element.78), channel_id=1, source_target_pairs={{0,1},{1,2},{2,3},{3,0},{4,5},{5,6},{6,7},{7,4},{8,9},{9,10},{10,1... | collective-permute-start | bytes 2359304 | tf_op jit(solution)/shard_map/ppermute | solution.py:35
  7.4 18.5 %collective-permute-start.5 = (f32[2,192,512]{2,1,0:T(8,128)}, f32[2,192,512]{2,1,0:T(8,128)S(1)}, u32[]{:S(2)}, u32[]{:S(2)}) collective-permute-start(f32[2,192,512]{2,1,0:T(8,128)} %get-tuple-element.79), channel_id=1, source_target_pairs={{0,3},{1,0},{2,1},{3,2},{4,7},{5,4},{6,5},{7,6},{8,11},{9,8},{10,9... | collective-permute-start | bytes 2359304 | tf_op jit(solution)/shard_map/ppermute | solution.py:35
  8.7 20.1 %collective-permute-start.6 = (f32[2,192,512]{2,1,0:T(8,128)}, f32[2,192,512]{2,1,0:T(8,128)S(1)}, u32[]{:S(2)}, u32[]{:S(2)}) collective-permute-start(f32[2,192,512]{2,1,0:T(8,128)} %get-tuple-element.80), channel_id=1, source_target_pairs={{0,4},{1,5},{2,6},{3,7},{4,8},{5,9},{6,10},{7,11},{8,12},{9,13},{1... | collective-permute-start | bytes 2359304 | tf_op jit(solution)/shard_map/ppermute | solution.py:35
  10.1 18.7 %collective-permute-start.7 = (f32[2,192,512]{2,1,0:T(8,128)}, f32[2,192,512]{2,1,0:T(8,128)S(1)}, u32[]{:S(2)}, u32[]{:S(2)}) collective-permute-start(f32[2,192,512]{2,1,0:T(8,128)} %get-tuple-element.81), channel_id=1, source_target_pairs={{0,12},{1,13},{2,14},{3,15},{4,0},{5,1},{6,2},{7,3},{8,4},{9,5},{1... | collective-permute-start | bytes 2359304 | tf_op jit(solution)/shard_map/ppermute | solution.py:35
  17.4 24.9 %collective-permute-start = (f32[2,192,512]{2,1,0:T(8,128)S(1)}, f32[2,192,512]{2,1,0:T(8,128)S(1)}, u32[]{:S(2)}, u32[]{:S(2)}) collective-permute-start(f32[2,192,512]{2,1,0:T(8,128)S(1)} %get-tuple-element.71), channel_id=1, source_target_pairs={{0,3},{1,0},{2,1},{3,2},{4,7},{5,4},{6,5},{7,6},{8,11},{9,8},{10,9... | collective-permute-start | bytes 2359304 | tf_op jit(solution)/shard_map/ppermute | solution.py:35
  18.8 10.1 %copy-start.8 = (f32[4,512]{1,0:T(4,128)S(1)}, f32[4,512]{1,0:T(4,128)}, u32[]{:S(2)}) copy-start(f32[4,512]{1,0:T(4,128)} %param.19) | copy-start | bytes 24580
  18.8 10.1 %copy-start.9 = (f32[4,512]{1,0:T(4,128)S(1)}, f32[4,512]{1,0:T(4,128)}, u32[]{:S(2)}) copy-start(f32[4,512]{1,0:T(4,128)} %param.20) | copy-start | bytes 24580
  23.9 22.2 %collective-permute-start.1 = (f32[2,192,512]{2,1,0:T(8,128)S(1)}, f32[2,192,512]{2,1,0:T(8,128)S(1)}, u32[]{:S(2)}, u32[]{:S(2)}) collective-permute-start(f32[2,192,512]{2,1,0:T(8,128)S(1)} %get-tuple-element.72), channel_id=1, source_target_pairs={{0,1},{1,2},{2,3},{3,0},{4,5},{5,6},{6,7},{7,4},{8,9},{9,10},{10,1... | collective-permute-start | bytes 2359304 | tf_op jit(solution)/shard_map/ppermute | solution.py:35
  25.9 23.3 %collective-permute-start.2 = (f32[2,192,512]{2,1,0:T(8,128)S(1)}, f32[2,192,512]{2,1,0:T(8,128)S(1)}, u32[]{:S(2)}, u32[]{:S(2)}) collective-permute-start(f32[2,192,512]{2,1,0:T(8,128)S(1)} %get-tuple-element.73), channel_id=1, source_target_pairs={{0,12},{1,13},{2,14},{3,15},{4,0},{5,1},{6,2},{7,3},{8,4},{9,5},{1... | collective-permute-start | bytes 2359304 | tf_op jit(solution)/shard_map/ppermute | solution.py:35
  28.8 20.3 %collective-permute-start.3 = (f32[2,192,512]{2,1,0:T(8,128)S(1)}, f32[2,192,512]{2,1,0:T(8,128)S(1)}, u32[]{:S(2)}, u32[]{:S(2)}) collective-permute-start(f32[2,192,512]{2,1,0:T(8,128)S(1)} %get-tuple-element.74), channel_id=1, source_target_pairs={{0,4},{1,5},{2,6},{3,7},{4,8},{5,9},{6,10},{7,11},{8,12},{9,13},{1... | collective-permute-start | bytes 2359304 | tf_op jit(solution)/shard_map/ppermute | solution.py:35
  28.9 4.1 %copy-start.10 = (s32[16]{0:T(128)S(1)}, s32[16]{0:T(128)}, u32[]{:S(2)}) copy-start(s32[16]{0:T(128)} %param.21) | copy-start | bytes 196
  28.9 15.1 %copy-start.5 = (f32[512]{0:T(512)S(1)}, f32[512]{0:T(512)}, u32[]{:S(2)}) copy-start(f32[512]{0:T(512)} %param.17) | copy-start | bytes 6148
  28.9 15.0 %copy-start.7 = (f32[4,128,128]{2,1,0:T(8,128)S(1)}, f32[4,128,128]{2,1,0:T(8,128)}, u32[]{:S(2)}) copy-start(f32[4,128,128]{2,1,0:T(8,128)} %inscatter_ref.1) | copy-start | bytes 786436
  31.7 27.4 %collective-permute-start.12 = (f32[2,192,512]{2,1,0:T(8,128)S(1)}, f32[2,192,512]{2,1,0:T(8,128)S(1)}, u32[]{:S(2)}, u32[]{:S(2)}) collective-permute-start(f32[2,192,512]{2,1,0:T(8,128)S(1)} %get-tuple-element.104), channel_id=1, source_target_pairs={{0,1},{1,2},{2,3},{3,0},{4,5},{5,6},{6,7},{7,4},{8,9},{9,10},{10,1... | collective-permute-start | bytes 2359304 | tf_op jit(solution)/shard_map/ppermute | solution.py:35
  42.3 21.1 %collective-permute-start.14 = (f32[2,192,512]{2,1,0:T(8,128)S(1)}, f32[2,192,512]{2,1,0:T(8,128)S(1)}, u32[]{:S(2)}, u32[]{:S(2)}) collective-permute-start(f32[2,192,512]{2,1,0:T(8,128)S(1)} %get-tuple-element.108), channel_id=1, source_target_pairs={{0,4},{1,5},{2,6},{3,7},{4,8},{5,9},{6,10},{7,11},{8,12},{9,13},{1... | collective-permute-start | bytes 2359304 | tf_op jit(solution)/shard_map/ppermute | solution.py:35
  46.2 18.8 %collective-permute-start.13 = (f32[2,192,512]{2,1,0:T(8,128)S(1)}, f32[2,192,512]{2,1,0:T(8,128)S(1)}, u32[]{:S(2)}, u32[]{:S(2)}) collective-permute-start(f32[2,192,512]{2,1,0:T(8,128)S(1)} %get-tuple-element.106), channel_id=1, source_target_pairs={{0,3},{1,0},{2,1},{3,2},{4,7},{5,4},{6,5},{7,6},{8,11},{9,8},{10,9... | collective-permute-start | bytes 2359304 | tf_op jit(solution)/shard_map/ppermute | solution.py:35
  49.2 20.4 %collective-permute-start.9 = (f32[2,64,512]{2,1,0:T(8,128)S(1)}, f32[2,64,512]{2,1,0:T(8,128)S(1)}, u32[]{:S(2)}, u32[]{:S(2)}) collective-permute-start(f32[2,64,512]{2,1,0:T(8,128)S(1)} %get-tuple-element.159), channel_id=1, source_target_pairs={{0,3},{1,0},{2,1},{3,2},{4,7},{5,4},{6,5},{7,6},{8,11},{9,8},{10,9... | collective-permute-start | bytes 786440 | tf_op jit(solution)/shard_map/ppermute | solution.py:35
  49.3 16.0 %collective-permute-start.15 = (f32[2,192,512]{2,1,0:T(8,128)S(1)}, f32[2,192,512]{2,1,0:T(8,128)S(1)}, u32[]{:S(2)}, u32[]{:S(2)}) collective-permute-start(f32[2,192,512]{2,1,0:T(8,128)S(1)} %get-tuple-element.110), channel_id=1, source_target_pairs={{0,12},{1,13},{2,14},{3,15},{4,0},{5,1},{6,2},{7,3},{8,4},{9,5},{1... | collective-permute-start | bytes 2359304 | tf_op jit(solution)/shard_map/ppermute | solution.py:35
  59.0 12.1 %collective-permute-start.8 = (f32[2,64,512]{2,1,0:T(8,128)S(1)}, f32[2,64,512]{2,1,0:T(8,128)S(1)}, u32[]{:S(2)}, u32[]{:S(2)}) collective-permute-start(f32[2,64,512]{2,1,0:T(8,128)S(1)} %get-tuple-element.160), channel_id=1, source_target_pairs={{0,1},{1,2},{2,3},{3,0},{4,5},{5,6},{6,7},{7,4},{8,9},{9,10},{10,1... | collective-permute-start | bytes 786440 | tf_op jit(solution)/shard_map/ppermute | solution.py:35
  63.4 9.2 %collective-permute-start.11 = (f32[2,64,512]{2,1,0:T(8,128)S(1)}, f32[2,64,512]{2,1,0:T(8,128)S(1)}, u32[]{:S(2)}, u32[]{:S(2)}) collective-permute-start(f32[2,64,512]{2,1,0:T(8,128)S(1)} %get-tuple-element.157), channel_id=1, source_target_pairs={{0,12},{1,13},{2,14},{3,15},{4,0},{5,1},{6,2},{7,3},{8,4},{9,5},{1... | collective-permute-start | bytes 786440 | tf_op jit(solution)/shard_map/ppermute | solution.py:35
  64.9 8.4 %collective-permute-start.10 = (f32[2,64,512]{2,1,0:T(8,128)S(1)}, f32[2,64,512]{2,1,0:T(8,128)S(1)}, u32[]{:S(2)}, u32[]{:S(2)}) collective-permute-start(f32[2,64,512]{2,1,0:T(8,128)S(1)} %get-tuple-element.158), channel_id=1, source_target_pairs={{0,4},{1,5},{2,6},{3,7},{4,8},{5,9},{6,10},{7,11},{8,12},{9,13},{1... | collective-permute-start | bytes 786440 | tf_op jit(solution)/shard_map/ppermute | solution.py:35
  65.4 14.5 %collective-permute-start.16 = (f32[192,512]{1,0:T(8,128)S(1)}, f32[192,512]{1,0:T(8,128)S(1)}, u32[]{:S(2)}, u32[]{:S(2)}) collective-permute-start(f32[192,512]{1,0:T(8,128)S(1)} %fusion.5), channel_id=1, source_target_pairs={{0,4},{1,5},{2,6},{3,7},{4,8},{5,9},{6,10},{7,11},{8,12},{9,13},{1... | collective-permute-start | bytes 1179656 | tf_op jit(solution)/shard_map/ppermute | solution.py:35
  69.5 11.9 %collective-permute-start.18 = (f32[192,512]{1,0:T(8,128)S(1)}, f32[192,512]{1,0:T(8,128)S(1)}, u32[]{:S(2)}, u32[]{:S(2)}) collective-permute-start(f32[192,512]{1,0:T(8,128)S(1)} %get-tuple-element.147), channel_id=1, source_target_pairs={{0,12},{1,13},{2,14},{3,15},{4,0},{5,1},{6,2},{7,3},{8,4},{9,5},{1... | collective-permute-start | bytes 1179656 | tf_op jit(solution)/shard_map/ppermute | solution.py:35
  71.1 13.3 %collective-permute-start.17 = (f32[192,512]{1,0:T(8,128)S(1)}, f32[192,512]{1,0:T(8,128)S(1)}, u32[]{:S(2)}, u32[]{:S(2)}) collective-permute-start(f32[192,512]{1,0:T(8,128)S(1)} %get-tuple-element.148), channel_id=1, source_target_pairs={{0,8},{1,9},{2,10},{3,11},{4,12},{5,13},{6,14},{7,15},{8,0},{9,1},... | collective-permute-start | bytes 1179656 | tf_op jit(solution)/shard_map/ppermute | solution.py:35
  72.6 15.0 %collective-permute-start.19 = (f32[192,512]{1,0:T(8,128)S(1)}, f32[192,512]{1,0:T(8,128)S(1)}, u32[]{:S(2)}, u32[]{:S(2)}) collective-permute-start(f32[192,512]{1,0:T(8,128)S(1)} %fusion.2), channel_id=1, source_target_pairs={{0,1},{1,2},{2,3},{3,0},{4,5},{5,6},{6,7},{7,4},{8,9},{9,10},{10,1... | collective-permute-start | bytes 1179656 | tf_op jit(solution)/shard_map/ppermute | solution.py:35
  73.4 14.2 %collective-permute-start.21 = (f32[192,512]{1,0:T(8,128)S(1)}, f32[192,512]{1,0:T(8,128)S(1)}, u32[]{:S(2)}, u32[]{:S(2)}) collective-permute-start(f32[192,512]{1,0:T(8,128)S(1)} %get-tuple-element.145), channel_id=1, source_target_pairs={{0,3},{1,0},{2,1},{3,2},{4,7},{5,4},{6,5},{7,6},{8,11},{9,8},{10,9... | collective-permute-start | bytes 1179656 | tf_op jit(solution)/shard_map/ppermute | solution.py:35
  79.8 11.0 %collective-permute-start.20 = (f32[192,512]{1,0:T(8,128)S(1)}, f32[192,512]{1,0:T(8,128)S(1)}, u32[]{:S(2)}, u32[]{:S(2)}) collective-permute-start(f32[192,512]{1,0:T(8,128)S(1)} %get-tuple-element.146), channel_id=1, source_target_pairs={{0,2},{1,3},{2,0},{3,1},{4,6},{5,7},{6,4},{7,5},{8,10},{9,11},{10,... | collective-permute-start | bytes 1179656 | tf_op jit(solution)/shard_map/ppermute | solution.py:35
  84.7 16.0 %collective-permute-start.32 = (f32[64,512]{1,0:T(8,128)S(1)}, f32[64,512]{1,0:T(8,128)S(1)}, u32[]{:S(2)}, u32[]{:S(2)}) collective-permute-start(f32[64,512]{1,0:T(8,128)S(1)} %slice.255), channel_id=1, source_target_pairs={{0,16},{1,17},{2,18},{3,19},{4,20},{5,21},{6,22},{7,23},{8,24},{9,... | collective-permute-start | bytes 393224 | tf_op jit(solution)/shard_map/ppermute | solution.py:35
  91.0 11.5 %collective-permute-start.34 = (f32[64,512]{1,0:T(8,128)S(1)}, f32[64,512]{1,0:T(8,128)S(1)}, u32[]{:S(2)}, u32[]{:S(2)}) collective-permute-start(f32[64,512]{1,0:T(8,128)S(1)} %get-tuple-element.162), channel_id=1, source_target_pairs={{0,48},{1,49},{2,50},{3,51},{4,52},{5,53},{6,54},{7,55},{8,56},{9,... | collective-permute-start | bytes 393224 | tf_op jit(solution)/shard_map/ppermute | solution.py:35
  97.1 9.4 %collective-permute-start.22 = (f32[4,64,512]{2,1,0:T(8,128)S(1)}, f32[4,64,512]{2,1,0:T(8,128)S(1)}, u32[]{:S(2)}, u32[]{:S(2)}) collective-permute-start(f32[4,64,512]{2,1,0:T(8,128)S(1)} %pad_maximum_fusion), channel_id=1, source_target_pairs={{0,1},{1,2},{2,3},{3,0},{4,5},{5,6},{6,7},{7,4},{8,9},{9,10},{10,1... | collective-permute-start | bytes 1572872 | tf_op jit(solution)/shard_map/ppermute | solution.py:35
  97.1 14.6 %collective-permute-start.23 = (f32[4,64,512]{2,1,0:T(8,128)S(1)}, f32[4,64,512]{2,1,0:T(8,128)S(1)}, u32[]{:S(2)}, u32[]{:S(2)}) collective-permute-start(f32[4,64,512]{2,1,0:T(8,128)S(1)} %pad_maximum_fusion.1), channel_id=1, source_target_pairs={{0,3},{1,0},{2,1},{3,2},{4,7},{5,4},{6,5},{7,6},{8,11},{9,8},{10,9... | collective-permute-start | bytes 1572872 | tf_op jit(solution)/shard_map/ppermute | solution.py:35
  99.8 12.5 %collective-permute-start.27 = (f32[4,64,512]{2,1,0:T(8,128)S(1)}, f32[4,64,512]{2,1,0:T(8,128)S(1)}, u32[]{:S(2)}, u32[]{:S(2)}) collective-permute-start(f32[4,64,512]{2,1,0:T(8,128)S(1)} %pad_maximum_fusion.2), channel_id=1, source_target_pairs={{0,4},{1,5},{2,6},{3,7},{4,8},{5,9},{6,10},{7,11},{8,12},{9,13},{1... | collective-permute-start | bytes 1572872 | tf_op jit(solution)/shard_map/ppermute | solution.py:35
  100.7 11.8 %collective-permute-start.28 = (f32[4,64,512]{2,1,0:T(8,128)S(1)}, f32[4,64,512]{2,1,0:T(8,128)S(1)}, u32[]{:S(2)}, u32[]{:S(2)}) collective-permute-start(f32[4,64,512]{2,1,0:T(8,128)S(1)} %pad_maximum_fusion.3), channel_id=1, source_target_pairs={{0,12},{1,13},{2,14},{3,15},{4,0},{5,1},{6,2},{7,3},{8,4},{9,5},{1... | collective-permute-start | bytes 1572872 | tf_op jit(solution)/shard_map/ppermute | solution.py:35
  102.6 11.2 %collective-permute-start.33 = (f32[128,512]{1,0:T(8,128)S(1)}, f32[128,512]{1,0:T(8,128)S(1)}, u32[]{:S(2)}, u32[]{:S(2)}) collective-permute-start(f32[128,512]{1,0:T(8,128)S(1)} %pad_maximum_fusion.4), channel_id=1, source_target_pairs={{0,16},{1,17},{2,18},{3,19},{4,20},{5,21},{6,22},{7,23},{8,24},{9,... | collective-permute-start | bytes 786440 | tf_op jit(solution)/shard_map/ppermute | solution.py:35
  106.6 14.1 %collective-permute-start.35 = (f32[128,512]{1,0:T(8,128)S(1)}, f32[128,512]{1,0:T(8,128)S(1)}, u32[]{:S(2)}, u32[]{:S(2)}) collective-permute-start(f32[128,512]{1,0:T(8,128)S(1)} %pad_maximum_fusion.5), channel_id=1, source_target_pairs={{0,48},{1,49},{2,50},{3,51},{4,52},{5,53},{6,54},{7,55},{8,56},{9,... | collective-permute-start | bytes 786440 | tf_op jit(solution)/shard_map/ppermute | solution.py:35
  111.9 8.9 %collective-permute-start.26 = (f32[64,512]{1,0:T(8,128)S(1)}, f32[64,512]{1,0:T(8,128)S(1)}, u32[]{:S(2)}, u32[]{:S(2)}) collective-permute-start(f32[64,512]{1,0:T(8,128)S(1)} %get-tuple-element.141), channel_id=1, source_target_pairs={{0,12},{1,13},{2,14},{3,15},{4,0},{5,1},{6,2},{7,3},{8,4},{9,5},{1... | collective-permute-start | bytes 393224 | tf_op jit(solution)/shard_map/ppermute | solution.py:35
  112.3 8.6 %collective-permute-start.25 = (f32[64,512]{1,0:T(8,128)S(1)}, f32[64,512]{1,0:T(8,128)S(1)}, u32[]{:S(2)}, u32[]{:S(2)}) collective-permute-start(f32[64,512]{1,0:T(8,128)S(1)} %get-tuple-element.142), channel_id=1, source_target_pairs={{0,8},{1,9},{2,10},{3,11},{4,12},{5,13},{6,14},{7,15},{8,0},{9,1},... | collective-permute-start | bytes 393224 | tf_op jit(solution)/shard_map/ppermute | solution.py:35
  112.6 8.3 %collective-permute-start.24 = (f32[64,512]{1,0:T(8,128)S(1)}, f32[64,512]{1,0:T(8,128)S(1)}, u32[]{:S(2)}, u32[]{:S(2)}) collective-permute-start(f32[64,512]{1,0:T(8,128)S(1)} %get-tuple-element.143), channel_id=1, source_target_pairs={{0,4},{1,5},{2,6},{3,7},{4,8},{5,9},{6,10},{7,11},{8,12},{9,13},{1... | collective-permute-start | bytes 393224 | tf_op jit(solution)/shard_map/ppermute | solution.py:35
  113.8 7.1 %collective-permute-start.31 = (f32[64,512]{1,0:T(8,128)S(1)}, f32[64,512]{1,0:T(8,128)S(1)}, u32[]{:S(2)}, u32[]{:S(2)}) collective-permute-start(f32[64,512]{1,0:T(8,128)S(1)} %get-tuple-element.137), channel_id=1, source_target_pairs={{0,3},{1,0},{2,1},{3,2},{4,7},{5,4},{6,5},{7,6},{8,11},{9,8},{10,9... | collective-permute-start | bytes 393224 | tf_op jit(solution)/shard_map/ppermute | solution.py:35
  120.7 5.7 %collective-permute-start.30 = (f32[64,512]{1,0:T(8,128)S(1)}, f32[64,512]{1,0:T(8,128)S(1)}, u32[]{:S(2)}, u32[]{:S(2)}) collective-permute-start(f32[64,512]{1,0:T(8,128)S(1)} %get-tuple-element.138), channel_id=1, source_target_pairs={{0,2},{1,3},{2,0},{3,1},{4,6},{5,7},{6,4},{7,5},{8,10},{9,11},{10,... | collective-permute-start | bytes 393224 | tf_op jit(solution)/shard_map/ppermute | solution.py:35
  120.8 6.7 %collective-permute-start.29 = (f32[64,512]{1,0:T(8,128)S(1)}, f32[64,512]{1,0:T(8,128)S(1)}, u32[]{:S(2)}, u32[]{:S(2)}) collective-permute-start(f32[64,512]{1,0:T(8,128)S(1)} %get-tuple-element.139), channel_id=1, source_target_pairs={{0,1},{1,2},{2,3},{3,0},{4,5},{5,6},{6,7},{7,4},{8,9},{9,10},{10,1... | collective-permute-start | bytes 393224 | tf_op jit(solution)/shard_map/ppermute | solution.py:35
  128.8 16.2 %collective-permute-start.38 = (f32[16,512]{1,0:T(8,128)S(1)}, f32[16,512]{1,0:T(8,128)S(1)}, u32[]{:S(2)}, u32[]{:S(2)}) collective-permute-start(f32[16,512]{1,0:T(8,128)S(1)} %get-tuple-element.135), channel_id=1, source_target_pairs={{0,192},{64,128},{128,64},{192,0},{1,193},{65,129},{129,65},{193,1... | collective-permute-start | bytes 98312 | tf_op jit(solution)/shard_map/ppermute | solution.py:402
  141.2 3.8 %collective-permute-start.37 = (f32[16,512]{1,0:T(8,128)S(1)}, f32[16,512]{1,0:T(8,128)S(1)}, u32[]{:S(2)}, u32[]{:S(2)}) collective-permute-start(f32[16,512]{1,0:T(8,128)S(1)} %get-tuple-element.135), channel_id=1, source_target_pairs={{0,128},{64,192},{128,0},{192,64},{1,129},{65,193},{129,1},{193,65... | collective-permute-start | bytes 98312 | tf_op jit(solution)/shard_map/ppermute | solution.py:402
  143.0 2.1 %collective-permute-start.36 = (f32[16,512]{1,0:T(8,128)S(1)}, f32[16,512]{1,0:T(8,128)S(1)}, u32[]{:S(2)}, u32[]{:S(2)}) collective-permute-start(f32[16,512]{1,0:T(8,128)S(1)} %get-tuple-element.135), channel_id=1, source_target_pairs={{0,64},{64,0},{128,192},{192,128},{1,65},{65,1},{129,193},{193,129... | collective-permute-start | bytes 98312 | tf_op jit(solution)/shard_map/ppermute | solution.py:402
  (2 other events, 7.2 us)
